TPU v7x, 32 devices: a whole 2x2x4 slice. The times are simulated.
32 devices in a mesh: expert: 8 (over z, x), tensor: 4 (over y, core).
Axes of the slice: x: 2, y: 2, z: 4, core: 2. Of those that a mesh axis runs over, the one named last changes fastest.
Arguments:
- tokens: bfloat16 [8192, 2048], P(('expert', 'tensor')), may hold values from -6 to 6
- cotangent: bfloat16 [8192, 2048], P(('expert', 'tensor')), may hold values from -6 to 6
- routes: int32 [8192, 8], P(('expert', 'tensor')), may hold values from 0 to 15, all different within a row; in each aligned block of 256 rows (0 to 255, 256 to 511, ...) at most 170 rows name the same one
- norm_in: float32 [2048], replicated, may hold values from 0.5 to 1.5
- query_w: bfloat16 [2048, 2048], P(None, 'tensor'), may hold values from -0.125 to 0.125
- key_w: bfloat16 [2048, 2048], P(None, 'tensor'), may hold values from -0.125 to 0.125
- value_w: bfloat16 [2048, 2048], P(None, 'tensor'), may hold values from -0.125 to 0.125
- out_w: bfloat16 [2048, 2048], P('tensor'), may hold values from -1 to 1
- query_gain: float32 [128], replicated, may hold values from 0.1 to 1.9
- key_gain: float32 [128], replicated, may hold values from 0.1 to 1.9
- norm_mid: float32 [2048], replicated, may hold values from 0.5 to 1.5
- router_w: float32 [2048, 16], replicated, may hold values from -0.0625 to 0.0625
- gate_w: bfloat16 [16, 2048, 1024], P('expert'), may hold values from -0.125 to 0.125
- up_w: bfloat16 [16, 2048, 1024], P('expert'), may hold values from -0.125 to 0.125
- down_w: bfloat16 [16, 1024, 2048], P('expert'), may hold values from -0.875 to 0.875
Outputs:
- output: bfloat16 [8192, 2048], P(('expert', 'tensor'))
- input_grad: float32 [8192, 2048], P(('expert', 'tensor'))
- norm_in_grad: float32 [2048], replicated
- query_w_grad: float32 [2048, 2048], P('expert', 'tensor')
- key_w_grad: float32 [2048, 2048], P('expert', 'tensor')
- value_w_grad: float32 [2048, 2048], P('expert', 'tensor')
- out_w_grad: float32 [2048, 2048], P('tensor', 'expert')
- query_gain_grad: float32 [128], replicated
- key_gain_grad: float32 [128], replicated
- norm_mid_grad: float32 [2048], replicated
- router_w_grad: float32 [2048, 16], replicated
- gate_w_grad: float32 [16, 2048, 1024], P('expert', None, 'tensor')
- up_w_grad: float32 [16, 2048, 1024], P('expert', None, 'tensor')
- down_w_grad: float32 [16, 1024, 2048], P('expert', 'tensor')
Inputs may be any that keep to these rules, and one draw needn't show every extreme that they name: `routes`: each row names 8 different experts. Among the 256 rows of one device (aligned blocks), no expert is named by more than 170 rows, and in some block one expert is named by exactly 170.
All inputs are finite; a program needn't handle non-finite values.
Results may differ from a plain program's by a relative error of at most 0.02.
Values may be sent and summed in bfloat16 or wider, within the bound.
A program may use at most 320 MiB of HBM per device.

v0:
```python
import math

import jax
import jax.numpy as jnp
from jax import lax
from jax.sharding import PartitionSpec as P

epsilon = 1e-06
highest = lax.Precision.HIGHEST
contract_last = (((1,), (1,)), ((), ()))
contract_first = (((0,), (0,)), ((), ()))


def inverse_rms(values):
    return lax.rsqrt(jnp.mean(values * values, axis=-1, keepdims=True) + epsilon)


def norm_backward(grad_norm, values, inverse, norm_gain):
    weighted = grad_norm * norm_gain
    inner_mean = jnp.mean(weighted * values, axis=-1, keepdims=True)
    return inverse * weighted - values * inverse * inverse * inverse * inner_mean


def rotary_tables(length, head_width):
    half_dim = head_width // 2
    frequency = jnp.exp(
        -math.log(10000.0) * 2.0 * jnp.arange(half_dim, dtype=jnp.float32) / head_width
    )
    angles = jnp.arange(length, dtype=jnp.float32)[:, None] * frequency[None, :]
    return (jnp.cos(angles)[:, None, :], jnp.sin(angles)[:, None, :])


def rotate(values, cosine, sine_table):
    half_dim = values.shape[-1] // 2
    first_half = values[..., :half_dim]
    second_half = values[..., half_dim:]
    return jnp.concatenate(
        [
            first_half * cosine - second_half * sine_table,
            second_half * cosine + first_half * sine_table,
        ],
        axis=-1,
    )


def rotate_back(gradient, cosine, sine_table):
    half_dim = gradient.shape[-1] // 2
    first_half = gradient[..., :half_dim]
    second_half = gradient[..., half_dim:]
    return jnp.concatenate(
        [
            first_half * cosine + second_half * sine_table,
            second_half * cosine - first_half * sine_table,
        ],
        axis=-1,
    )


def swiglu_back(hidden_grad, gate_pre, up_pre):
    sigmoid_part = jax.nn.sigmoid(gate_pre)
    gate_back = (
        hidden_grad * up_pre * sigmoid_part * (1.0 + gate_pre * (1.0 - sigmoid_part))
    ).astype(jnp.bfloat16)
    up_back = (hidden_grad * gate_pre * sigmoid_part).astype(jnp.bfloat16)
    return (gate_back, up_back)


def per_device(
    tokens,
    cotangent,
    routes,
    norm_in,
    query_w,
    key_w,
    value_w,
    out_w,
    query_gain,
    key_gain,
    norm_mid,
    router_w,
    gate_w,
    up_w,
    down_w,
):
    rows_own = tokens.shape[0]
    model_width = tokens.shape[1]
    tensor_count = lax.axis_size("tensor")
    expert_count = lax.axis_size("expert")
    head_width = query_gain.shape[0]
    local_heads = query_w.shape[1] // head_width
    experts_local = gate_w.shape[0]
    experts_all = router_w.shape[1]
    top_count = routes.shape[1]
    hidden_width = gate_w.shape[2]
    capacity = max(2, rows_own * top_count * 4 // (experts_all * 3))
    factor = 1.0 / math.sqrt(head_width)
    source = tokens.astype(jnp.float32)
    scale_in = inverse_rms(source)
    normed_low = (source * scale_in * norm_in).astype(jnp.bfloat16)
    gathered = lax.all_gather(normed_low, "tensor", axis=0, tiled=True)
    seq_len = gathered.shape[0]
    query_pre = jnp.dot(gathered, query_w, preferred_element_type=jnp.float32)
    key_pre = jnp.dot(gathered, key_w, preferred_element_type=jnp.float32)
    value_low = jnp.dot(gathered, value_w, preferred_element_type=jnp.float32).astype(jnp.bfloat16)
    cosine, sine_table = rotary_tables(seq_len, head_width)
    query_heads = query_pre.reshape(seq_len, local_heads, head_width)
    key_heads = key_pre.reshape(seq_len, local_heads, head_width)
    query_scale = inverse_rms(query_heads)
    key_scale = inverse_rms(key_heads)
    query_low = rotate(query_heads * query_scale * query_gain, cosine, sine_table).astype(
        jnp.bfloat16
    )
    key_low = rotate(key_heads * key_scale * key_gain, cosine, sine_table).astype(jnp.bfloat16)
    value_heads = value_low.reshape(seq_len, local_heads, head_width)
    block_rows = min(512, seq_len)
    block_count = seq_len // block_rows
    query_blocks = query_low.reshape(block_count, block_rows, local_heads, head_width)

    def attend(query_block):
        scores = (
            jnp.einsum("qhd,khd->hqk", query_block, key_low, preferred_element_type=jnp.float32)
            * factor
        )
        row_max = jnp.max(scores, axis=-1, keepdims=True)
        shifted = jnp.exp(scores - row_max)
        row_sum = jnp.sum(shifted, axis=-1, keepdims=True)
        probs_low = (shifted / row_sum).astype(jnp.bfloat16)
        mixture = jnp.einsum(
            "hqk,khd->qhd", probs_low, value_heads, preferred_element_type=jnp.float32
        )
        return (mixture.astype(jnp.bfloat16), (row_max + jnp.log(row_sum))[..., 0])

    attended_blocks, log_sums = lax.map(attend, query_blocks)
    attended = attended_blocks.reshape(seq_len, local_heads * head_width)
    attn_out = lax.psum_scatter(
        jnp.dot(attended, out_w, preferred_element_type=jnp.float32),
        "tensor",
        scatter_dimension=0,
        tiled=True,
    )
    middle = source + attn_out
    scale_mid = inverse_rms(middle)
    normed_mid = middle * scale_mid * norm_mid
    mid_low = normed_mid.astype(jnp.bfloat16)
    logits = jnp.dot(normed_mid, router_w, precision=highest, preferred_element_type=jnp.float32)
    route_mask = routes[:, :, None] == jnp.arange(experts_all, dtype=jnp.int32)[None, None, :]
    mask_float = route_mask.astype(jnp.float32)
    chosen = jnp.sum(mask_float * logits[:, None, :], axis=-1)
    gating = jax.nn.softmax(chosen, axis=-1)
    mask_flat = route_mask.reshape(rows_own * top_count, experts_all).astype(jnp.int32)
    running = jnp.cumsum(mask_flat, axis=0)
    slot_index = jnp.sum((running - 1) * mask_flat, axis=1)
    positions = routes.reshape(-1) * capacity + slot_index
    row_owner = jnp.arange(rows_own * top_count, dtype=jnp.int32) // top_count
    outgoing = (
        jnp.zeros((experts_all * capacity, model_width), jnp.bfloat16)
        .at[positions]
        .set(mid_low[row_owner])
    )

    def route_rows(buffer):
        sent = buffer.reshape(expert_count, experts_local * capacity, model_width)
        arrived = lax.all_to_all(sent, "expert", split_axis=0, concat_axis=0, tiled=True)
        return arrived.reshape(expert_count, experts_local, capacity, model_width)

    def return_rows(buffer):
        sent = buffer.reshape(expert_count, experts_local * capacity, model_width)
        arrived = lax.all_to_all(sent, "expert", split_axis=0, concat_axis=0, tiled=True)
        return arrived.reshape(experts_all * capacity, model_width)

    received = route_rows(outgoing)
    gate_pre = jnp.einsum("secd,edf->secf", received, gate_w, preferred_element_type=jnp.float32)
    up_pre = jnp.einsum("secd,edf->secf", received, up_w, preferred_element_type=jnp.float32)
    hidden_low = (gate_pre * jax.nn.sigmoid(gate_pre) * up_pre).astype(jnp.bfloat16)
    expert_out = jnp.einsum(
        "secf,efd->secd", hidden_low, down_w, preferred_element_type=jnp.float32
    ).astype(jnp.bfloat16)
    returned = return_rows(expert_out)
    per_route = returned[positions].reshape(rows_own, top_count, model_width).astype(jnp.float32)
    output = (middle + jnp.sum(gating[:, :, None] * per_route, axis=1)).astype(jnp.bfloat16)
    upstream = cotangent.astype(jnp.float32)
    gate_grad = jnp.sum(per_route * upstream[:, None, :], axis=-1)
    route_out_grad = (
        (gating[:, :, None] * upstream[:, None, :])
        .astype(jnp.bfloat16)
        .reshape(rows_own * top_count, model_width)
    )
    grad_outgoing = (
        jnp.zeros((experts_all * capacity, model_width), jnp.bfloat16)
        .at[positions]
        .set(route_out_grad)
    )
    grad_received = route_rows(grad_outgoing)
    hidden_grad = jnp.einsum(
        "secd,efd->secf", grad_received, down_w, preferred_element_type=jnp.float32
    )
    gate_back, up_back = swiglu_back(hidden_grad, gate_pre, up_pre)
    input_rows = jnp.einsum("secf,edf->secd", gate_back, gate_w, preferred_element_type=jnp.float32)
    input_rows = (
        input_rows + jnp.einsum("secf,edf->secd", up_back, up_w, preferred_element_type=jnp.float32)
    ).astype(jnp.bfloat16)
    returned_grads = return_rows(input_rows)
    expert_input_grad = jnp.sum(
        returned_grads[positions].reshape(rows_own, top_count, model_width).astype(jnp.float32),
        axis=1,
    )
    all_inputs, all_grads = (
        lax.all_gather(received, "tensor", axis=0, tiled=True),
        lax.all_gather(grad_received, "tensor", axis=0, tiled=True),
    )
    part_width = hidden_width // tensor_count
    first_column = lax.axis_index("tensor") * part_width
    gate_part = lax.dynamic_slice_in_dim(gate_w, first_column, part_width, 2)
    up_part = lax.dynamic_slice_in_dim(up_w, first_column, part_width, 2)
    down_part = lax.dynamic_slice_in_dim(down_w, first_column, part_width, 1)
    gate_again = jnp.einsum(
        "secd,edf->secf", all_inputs, gate_part, preferred_element_type=jnp.float32
    )
    up_again = jnp.einsum("secd,edf->secf", all_inputs, up_part, preferred_element_type=jnp.float32)
    hidden_again = (gate_again * jax.nn.sigmoid(gate_again) * up_again).astype(jnp.bfloat16)
    hidden_back = jnp.einsum(
        "secd,efd->secf", all_grads, down_part, preferred_element_type=jnp.float32
    )
    gate_part_back, up_part_back = swiglu_back(hidden_back, gate_again, up_again)
    gate_w_grad = jnp.einsum(
        "secd,secf->edf", all_inputs, gate_part_back, preferred_element_type=jnp.float32
    )
    up_w_grad = jnp.einsum(
        "secd,secf->edf", all_inputs, up_part_back, preferred_element_type=jnp.float32
    )
    down_w_grad = jnp.einsum(
        "secf,secd->efd", hidden_again, all_grads, preferred_element_type=jnp.float32
    )
    inner_gate = jnp.sum(gating * gate_grad, axis=-1, keepdims=True)
    chosen_grad = gating * (gate_grad - inner_gate)
    logit_grad = jnp.sum(chosen_grad[:, :, None] * mask_float, axis=1)
    router_part = lax.dot_general(
        normed_mid,
        logit_grad,
        contract_first,
        precision=highest,
        preferred_element_type=jnp.float32,
    )
    normed_mid_grad = expert_input_grad + lax.dot_general(
        logit_grad, router_w, contract_last, precision=highest, preferred_element_type=jnp.float32
    )
    norm_mid_part = jnp.sum(normed_mid_grad * middle * scale_mid, axis=0)
    middle_grad = upstream + norm_backward(normed_mid_grad, middle, scale_mid, norm_mid)
    branch_low = middle_grad.astype(jnp.bfloat16)
    branch_all = lax.all_gather(branch_low, "tensor", axis=0, tiled=True)
    attended_grad = lax.dot_general(
        branch_all, out_w, contract_last, preferred_element_type=jnp.float32
    ).astype(jnp.bfloat16)
    out_w_part = lax.dot_general(
        attended, branch_all, contract_first, preferred_element_type=jnp.float32
    )
    grad_blocks = attended_grad.reshape(block_count, block_rows, local_heads, head_width)

    def attend_back(carry, inputs):
        key_total, value_total = carry
        query_block, grad_block, log_block = inputs
        scores = (
            jnp.einsum("qhd,khd->hqk", query_block, key_low, preferred_element_type=jnp.float32)
            * factor
        )
        probs = jnp.exp(scores - log_block[:, :, None])
        probs_low = probs.astype(jnp.bfloat16)
        value_total = value_total + jnp.einsum(
            "hqk,qhd->khd", probs_low, grad_block, preferred_element_type=jnp.float32
        )
        prob_grad = jnp.einsum(
            "qhd,khd->hqk", grad_block, value_heads, preferred_element_type=jnp.float32
        )
        delta = jnp.sum(probs * prob_grad, axis=-1, keepdims=True)
        score_low = (probs * (prob_grad - delta)).astype(jnp.bfloat16)
        query_part = (
            jnp.einsum("hqk,khd->qhd", score_low, key_low, preferred_element_type=jnp.float32)
            * factor
        )
        key_total = (
            key_total
            + jnp.einsum("hqk,qhd->khd", score_low, query_block, preferred_element_type=jnp.float32)
            * factor
        )
        return ((key_total, value_total), query_part)

    zero_heads = jnp.zeros((seq_len, local_heads, head_width), jnp.float32)
    (key_grad, value_total), query_parts = lax.scan(
        attend_back, (zero_heads, zero_heads), (query_blocks, grad_blocks, log_sums)
    )
    query_grad = query_parts.reshape(seq_len, local_heads, head_width)
    value_grad_low = value_total.reshape(seq_len, local_heads * head_width).astype(jnp.bfloat16)
    query_rot_grad = rotate_back(query_grad, cosine, sine_table)
    key_rot_grad = rotate_back(key_grad, cosine, sine_table)
    query_gain_part = jnp.sum(query_rot_grad * query_heads * query_scale, axis=(0, 1))
    key_gain_part = jnp.sum(key_rot_grad * key_heads * key_scale, axis=(0, 1))
    query_pre_grad = (
        norm_backward(query_rot_grad, query_heads, query_scale, query_gain)
        .reshape(seq_len, local_heads * head_width)
        .astype(jnp.bfloat16)
    )
    key_pre_grad = (
        norm_backward(key_rot_grad, key_heads, key_scale, key_gain)
        .reshape(seq_len, local_heads * head_width)
        .astype(jnp.bfloat16)
    )
    query_w_part = lax.dot_general(
        gathered, query_pre_grad, contract_first, preferred_element_type=jnp.float32
    )
    key_w_part = lax.dot_general(
        gathered, key_pre_grad, contract_first, preferred_element_type=jnp.float32
    )
    value_w_part = lax.dot_general(
        gathered, value_grad_low, contract_first, preferred_element_type=jnp.float32
    )
    summed = lax.dot_general(
        query_pre_grad, query_w, contract_last, preferred_element_type=jnp.float32
    )
    summed = summed + lax.dot_general(
        key_pre_grad, key_w, contract_last, preferred_element_type=jnp.float32
    )
    rows_grad = lax.psum_scatter(
        (
            summed
            + lax.dot_general(
                value_grad_low, value_w, contract_last, preferred_element_type=jnp.float32
            )
        ).astype(jnp.bfloat16),
        "tensor",
        scatter_dimension=0,
        tiled=True,
    ).astype(jnp.float32)
    norm_in_part = jnp.sum(rows_grad * source * scale_in, axis=0)
    input_grad = middle_grad + norm_backward(rows_grad, source, scale_in, norm_in)
    query_w_grad, key_w_grad, value_w_grad, out_w_grad = (
        lax.psum_scatter(
            query_w_part.astype(jnp.bfloat16), "expert", scatter_dimension=0, tiled=True
        ).astype(jnp.float32),
        lax.psum_scatter(
            key_w_part.astype(jnp.bfloat16), "expert", scatter_dimension=0, tiled=True
        ).astype(jnp.float32),
        lax.psum_scatter(
            value_w_part.astype(jnp.bfloat16), "expert", scatter_dimension=0, tiled=True
        ).astype(jnp.float32),
        lax.psum_scatter(
            out_w_part.astype(jnp.bfloat16), "expert", scatter_dimension=1, tiled=True
        ).astype(jnp.float32),
    )
    norm_in_grad, query_gain_grad, key_gain_grad, norm_mid_grad, router_w_grad = lax.psum(
        (norm_in_part, query_gain_part, key_gain_part, norm_mid_part, router_part),
        ("expert", "tensor"),
    )
    return (
        output,
        input_grad,
        norm_in_grad,
        query_w_grad,
        key_w_grad,
        value_w_grad,
        out_w_grad,
        query_gain_grad,
        key_gain_grad,
        norm_mid_grad,
        router_w_grad,
        gate_w_grad,
        up_w_grad,
        down_w_grad,
    )


def solution(mesh):
    placed = (
        P(("expert", "tensor"), None),
        P(("expert", "tensor"), None),
        P(("expert", "tensor"), None),
        P(),
        P(None, "tensor"),
        P(None, "tensor"),
        P(None, "tensor"),
        P("tensor", None),
        P(),
        P(),
        P(),
        P(),
        P("expert", None, None),
        P("expert", None, None),
        P("expert", None, None),
    )
    return jax.shard_map(
        per_device,
        mesh=mesh,
        in_specs=placed,
        out_specs=(
            P(("expert", "tensor"), None),
            P(("expert", "tensor"), None),
            P(),
            P("expert", "tensor"),
            P("expert", "tensor"),
            P("expert", "tensor"),
            P("tensor", "expert"),
            P(),
            P(),
            P(),
            P(),
            P("expert", None, "tensor"),
            P("expert", None, "tensor"),
            P("expert", "tensor", None),
        ),
        check_vma=False,
    )
```

profile of v0, /device:TPU:0, one launch (start us, length us, event | category | flops | bytes accessed | tf_op | source)
XLA Modules:
  0.0 2555.7 jit_solution(6938795689948673481)
XLA Ops:
  14.0 35.3 %all-gather.5.cloned.1.call-done = bf16[1024,2048]{1,0:T(8,128)(2,1)} async-done(((bf16[256,2048]{1,0:T(8,128)(2,1)}), bf16[1024,2048]{1,0:T(8,128)(2,1)}) %all-gather.5.cloned.1.call-update) | async-done | bytes 4194320 | tf_op jit(solution)/shard_map/all_gather | solution.py:100
  49.3 5.9 multiply_reduce_fusion.8
  58.3 6.7 multiply_reduce_fusion.7
  81.8 16.2 while.27
  98.0 7.9 fusion.132
  112.6 65.2 %reduce-scatter.7.cloned.1.call-done = f32[256,2048]{1,0:T(8,128)} async-done(((f32[1024,2048]{1,0:T(8,128)}), f32[256,2048]{1,0:T(8,128)}) %reduce-scatter.7.cloned.1.call-update) | async-done | bytes 2097168 | tf_op jit(solution)/shard_map/reduce_scatter | solution.py:135
  181.3 46.0 %scatter_custom_fusion = bf16[2720,2048]{1,0:T(8,128)(2,1)} fusion(s32[2048]{0:T(1024)S(1)} %bitcast.406, bf16[256,2048]{1,0:T(8,128)(2,1)S(1)} %fusion.129, s32[2048]{0:T(1024)S(1)} %broadcast_clamp_fusion.1, bf16[]{:T(256)} %constant.92.clone.1), kind=kCustom, calls=%fused_computation.98 | custom fusion | bytes 11141122 | tf_op jit(solution)/shard_map/scatter | solution.py:158
  227.3 9.2 reshape.426
  236.4 5.6 all-to-all-start
  248.6 19.8 scatter_custom_fusion.1
  268.4 9.2 reshape.430
  277.6 209.4 %all-to-all-done = bf16[8,340,2048]{2,1,0:T(8,128)(2,1)} async-done(((bf16[8,340,2048]{2,1,0:T(8,128)(2,1)}), bf16[8,340,2048]{2,1,0:T(8,128)(2,1)}, u32[]{:S(2)}, u32[]{:S(2)}) %all-to-all-start) | async-done | bytes 11141152 | tf_op jit(solution)/shard_map/all_to_all | solution.py:163
  487.0 5.2 all-to-all-start.2
  492.3 23.3 copy.157
  515.6 28.3 %fusion.60 = f32[2,8,170,1024]{3,2,1,0:T(8,128)} fusion(bf16[2,2048,1024]{2,1,0:T(8,128)(2,1)} %param.31, bf16[8,2,170,2048]{3,0,2,1:T(8,128)(2,1)S(1)} %bitcast.391), kind=kOutput, calls=%fused_computation.92 | convolution fusion | flops 11408506880 | bytes 30670848 | tf_op jit(solution)/shard_map/secd,edf->secf/dot_general | solution.py:172
  543.9 25.2 fusion.56
  569.1 167.2 %all-to-all-done.2 = bf16[8,340,2048]{2,1,0:T(8,128)(2,1)} async-done(((bf16[8,340,2048]{2,1,0:T(8,128)(2,1)}), bf16[8,340,2048]{2,1,0:T(8,128)(2,1)}, u32[]{:S(2)}, u32[]{:S(2)}) %all-to-all-start.2) | async-done | bytes 11141152 | tf_op jit(solution)/shard_map/all_to_all | solution.py:163
  736.3 24.6 copy.163
  760.9 29.2 %fusion.62 = f32[2,8,170,1024]{3,2,1,0:T(8,128)} fusion(bf16[2,1024,2048]{2,1,0:T(8,128)(2,1)} %param.33, bf16[8,2,170,2048]{3,0,2,1:T(8,128)(2,1)} %bitcast.389), kind=kOutput, calls=%fused_computation.94 | convolution fusion | flops 11408506880 | bytes 30670848 | tf_op jit(solution)/shard_map/secd,efd->secf/dot_general | solution.py:194
  790.1 23.5 fusion.54
  813.6 29.0 %fusion.30 = bf16[8,2,170,2048]{3,2,0,1:T(8,128)(2,1)} fusion(f32[2,8,170,2048]{3,2,1,0:T(8,128)} %fusion.54, bf16[2,2048,1024]{2,1,0:T(8,128)(2,1)} %param.31, f32[2,8,170,1024]{3,2,1,0:T(8,128)} %fusion.62, f32[2,8,170,1024]{3,2,1,0:T(8,128)} %fusion.56, f32[2,8,170,1024]{3,2,1,0:T(8,128)} %fusion.60), kind=kOutput, calls=%fused_computation.51 | convolution fusion | flops 11447500800 | bytes 75235328 | tf_op jit(solution)/shard_map/secf,edf->secd/dot_general | solution.py:198
  842.5 23.0 copy.165
  865.6 17.0 copy.166
  882.5 5.5 all-to-all-start.3
  888.0 21.7 convert_bitcast_fusion
  909.7 23.0 copy.160
  932.7 16.9 copy.161
  949.7 181.7 %all-to-all-done.3 = bf16[8,340,2048]{2,1,0:T(8,128)(2,1)} async-done(((bf16[8,340,2048]{2,1,0:T(8,128)(2,1)}), bf16[8,340,2048]{2,1,0:T(8,128)(2,1)}, u32[]{:S(2)}, u32[]{:S(2)}) %all-to-all-start.3) | async-done | bytes 11141152 | tf_op jit(solution)/shard_map/all_to_all | solution.py:168
  1131.4 5.2 all-to-all-start.1
  1136.7 9.3 reshape.433
  1146.1 21.9 gather_fusion.1
  1168.0 11.3 convert_reduce_fusion
  1179.3 201.4 %all-to-all-done.1 = bf16[8,340,2048]{2,1,0:T(8,128)(2,1)} async-done(((bf16[8,340,2048]{2,1,0:T(8,128)(2,1)}), bf16[8,340,2048]{2,1,0:T(8,128)(2,1)}, u32[]{:S(2)}, u32[]{:S(2)}) %all-to-all-start.1) | async-done | bytes 11141152 | tf_op jit(solution)/shard_map/all_to_all | solution.py:168
  1380.7 9.6 reshape.429
  1390.3 22.0 gather_fusion
  1412.3 9.6 fusion.28
  1422.2 5.3 multiply_reduce_fusion.2
  1430.8 33.2 %all-gather.7.cloned.1.call-done = bf16[1024,2048]{1,0:T(8,128)(2,1)} async-done(((bf16[256,2048]{1,0:T(8,128)(2,1)}), bf16[1024,2048]{1,0:T(8,128)(2,1)}) %all-gather.7.cloned.1.call-update) | async-done | bytes 4194320 | tf_op jit(solution)/shard_map/all_gather | solution.py:250
  1464.0 6.2 convolution_convert_fusion.4
  1472.5 42.5 %while.28 = (s32[]{:T(128)}, f32[1024,4,128]{0,2,1:T(8,128)}, f32[1024,4,128]{0,2,1:T(8,128)}, f32[2,512,4,128]{3,1,0,2:T(8,128)}, bf16[2,512,4,128]{3,1,2,0:T(8...) while((s32[]{:T(128)}, f32[1024,4,128]{0,2,1:T(8,128)}, ...), condition=%wide.region_25.26_spmd.clone, body=%wide.region_23.25_spmd.clone.sunk | while | flops 2712401920 | bytes 208724464 | solution.py:288
  1481.7 4.8 bitcast_add_fusion.4
  1502.6 5.5 bitcast_add_fusion.4
  1517.9 6.8 multiply_add_fusion
  1537.6 5.2 multiply_reduce_fusion.3
  1556.6 6.0 convolution_convert_fusion.1
  1563.2 6.2 convolution_convert_fusion
  1574.3 6.4 add_convert_fusion.1
  1580.8 14.0 copy.158
  1595.1 14.1 copy.164
  1615.4 61.1 %reduce-scatter.13.cloned.1.call-done = bf16[256,512]{1,0:T(8,128)(2,1)} async-done(((bf16[2048,512]{1,0:T(8,128)(2,1)}), bf16[256,512]{1,0:T(8,128)(2,1)}) %reduce-scatter.13.cloned.1.call-update) | async-done | bytes 262160 | tf_op jit(solution)/shard_map/reduce_scatter | solution.py:339
  1678.3 69.3 %reduce-scatter.15.cloned.1.call-done = bf16[256,512]{1,0:T(8,128)(2,1)} async-done(((bf16[2048,512]{1,0:T(8,128)(2,1)}), bf16[256,512]{1,0:T(8,128)(2,1)}) %reduce-scatter.15.cloned.1.call-update) | async-done | bytes 262160 | tf_op jit(solution)/shard_map/reduce_scatter | solution.py:342
  1749.4 69.3 %reduce-scatter.17.cloned.1.call-done = bf16[512,256]{1,0:T(8,128)(2,1)} async-done(((bf16[512,2048]{1,0:T(8,128)(2,1)}), bf16[512,256]{1,0:T(8,128)(2,1)}) %reduce-scatter.17.cloned.1.call-update) | async-done | bytes 262160 | tf_op jit(solution)/shard_map/reduce_scatter | solution.py:345
  1820.6 45.1 %reduce-scatter.9.cloned.1.call-done = bf16[256,2048]{1,0:T(8,128)(2,1)} async-done(((bf16[1024,2048]{1,0:T(8,128)(2,1)}), bf16[256,2048]{1,0:T(8,128)(2,1)}) %reduce-scatter.9.cloned.1.call-update) | async-done | bytes 1048592 | tf_op jit(solution)/shard_map/reduce_scatter | solution.py:322
  1867.5 40.0 %all-reduce = (f32[2048]{0:T(1024)}, f32[128]{0:T(128)}, f32[128]{0:T(128)}, f32[2048]{0:T(1024)}) all-reduce(f32[2048]{0:T(1024)S(1)} %get-tuple-element.210, f32[128]{0:T(128)S(1)} %bitcast_reduce_fusion.1, f32[128]{0:T(128)S(1)} %bitcast_reduce_fusion, ...), channel_id=1, replica_groups=mesh['expert'=8,'tensor'=4] {'expert','tensor'}, use_global_device_ids=true, to_apply=%region_31.32 | all-reduce | flops 4352 | bytes 34816 | tf_op jit(solution)/shard_map/psum | solution.py:349
  1907.5 6.5 fusion.106
  1914.1 228.6 %all-gather.9.cloned.1.call-done = bf16[32,2,170,2048]{3,2,0,1:T(8,128)(2,1)} async-done(((bf16[8,2,170,2048]{3,2,0,1:T(8,128)(2,1)}), bf16[32,2,170,2048]{3,2,0,1:T(8,128)(2,1)}) %all-gather.9.cloned.1.call-update) | async-done | bytes 44564496 | tf_op jit(solution)/shard_map/all_gather | solution.py:208
  2142.6 29.6 %fusion.119 = f32[2,256,32,170]{1,3,2,0:T(8,128)} fusion(bf16[32,2,170,2048]{3,2,0,1:T(8,128)(2,1)} %all-gather.9.cloned.1.call-done, bf16[2,2048,1024]{2,1,0:T(8,128)(2,1)} %param.31, s32[]{:T(128)S(6)} %select_n.43), kind=kOutput, calls=%fused_computation.159 | convolution fusion | flops 11408506880 | bytes 59375620 | tf_op jit(solution)/shard_map/secd,edf->secf/dot_general | solution.py:216
  2172.2 24.4 fusion.121
  2196.6 222.2 %all-gather.11.cloned.1.call-done = bf16[32,2,170,2048]{3,2,0,1:T(8,128)(2,1)} async-done(((bf16[8,2,170,2048]{3,2,0,1:T(8,128)(2,1)}), bf16[32,2,170,2048]{3,2,0,1:T(8,128)(2,1)}) %all-gather.11.cloned.1.call-update) | async-done | bytes 44564496 | tf_op jit(solution)/shard_map/all_gather | solution.py:209
  2418.7 23.5 fusion.123
  2442.2 28.0 %fusion.96 = f32[2,256,2048]{2,1,0:T(8,128)} fusion(bf16[32,2,170,2048]{3,2,0,1:T(8,128)(2,1)} %all-gather.11.cloned.1.call-done, f32[2,256,32,170]{1,3,2,0:T(8,128)} %fusion.119, f32[2,256,32,170]{1,3,2,0:T(8,128)} %fusion.121), kind=kOutput, calls=%fused_computation.130 | convolution fusion | flops 11425218560 | bytes 71041024 | tf_op jit(solution)/shard_map/secf,secd->efd/dot_general | solution.py:231
  2470.3 35.0 %fusion.93 = f32[2,2048,256]{2,1,0:T(8,128)} fusion(bf16[32,2,170,2048]{3,2,0,1:T(8,128)(2,1)} %all-gather.9.cloned.1.call-done, f32[2,256,32,170]{1,3,2,0:T(8,128)} %fusion.119, f32[2,256,32,170]{1,3,2,0:T(8,128)} %fusion.121, f32[2,256,32,170]{1,3,2,0:T(8,128)} %fusion.123), kind=kOutput, calls=%fused_computation.129 | convolution fusion | flops 11436359680 | bytes 82182144 | tf_op jit(solution)/shard_map/secd,secf->edf/dot_general | solution.py:225
  2505.3 32.6 %fusion.90 = f32[2,2048,256]{2,1,0:T(8,128)} fusion(bf16[32,2,170,2048]{3,2,0,1:T(8,128)(2,1)} %all-gather.9.cloned.1.call-done, f32[2,256,32,170]{1,3,2,0:T(8,128)} %fusion.119, f32[2,256,32,170]{1,3,2,0:T(8,128)} %fusion.123), kind=kOutput, calls=%fused_computation.128 | convolution fusion | flops 11425218560 | bytes 71041024 | tf_op jit(solution)/shard_map/secd,secf->edf/dot_general | solution.py:228
  2537.9 9.4 all-reduce.3.cloned.1.call-done
  (307 shorter events, 146.8 us)
Async XLA Ops:
  7.2 42.2 %copy-start = (bf16[2048,512]{1,0:T(8,128)(2,1)S(1)}, bf16[2048,512]{1,0:T(8,128)(2,1)}, u32[]{:S(2)}) copy-start(bf16[2048,512]{1,0:T(8,128)(2,1)} %param.23) | copy-start | bytes 6291460
  7.2 42.1 %all-gather.5.cloned.1.call-start = ((), (), s32[]{:S(2)}) async-start(), calls=%async_computation.10 | async-start | bytes 5242880 | tf_op jit(solution)/shard_map/all_gather | solution.py:100
  12.0 165.8 %reduce-scatter.7.cloned.1.call-start = ((), (), s32[]{:S(2)}) async-start(), calls=%async_computation.11 | async-start | bytes 10485760 | tf_op jit(solution)/shard_map/reduce_scatter | solution.py:135
  14.0 57.5 %copy-start.24 = (f32[1024,64]{1,0:T(8,128)}, f32[1024,64]{1,0:T(8,128)S(1)}, u32[]{:S(2)}) copy-start(f32[1024,64]{1,0:T(8,128)S(1)} %get-tuple-element.274) | copy-start | bytes 786436
  14.0 57.5 %copy-start.26 = (f32[1024,64]{1,0:T(8,128)}, f32[1024,64]{1,0:T(8,128)S(1)}, u32[]{:S(2)}) copy-start(f32[1024,64]{1,0:T(8,128)S(1)} %get-tuple-element.275) | copy-start | bytes 786436
  67.9 3.6 copy-start.41
  67.9 3.6 copy-start.43
  71.5 4.4 copy-start.70
  98.0 7.9 copy-start.4
  98.0 7.9 copy-start.49
  105.9 71.9 %copy-start.15 = (bf16[256,2048]{1,0:T(8,128)(2,1)S(1)}, bf16[256,2048]{1,0:T(8,128)(2,1)}, u32[]{:S(2)}) copy-start(bf16[256,2048]{1,0:T(8,128)(2,1)} %param.19) | copy-start | bytes 3145732
  106.6 74.5 %copy-start.38 = (f32[2048]{0:T(1024)S(1)}, f32[2048]{0:T(1024)}, u32[]{:S(2)}) copy-start(f32[2048]{0:T(1024)} %param.29) | copy-start | bytes 24580
  112.6 136.0 %copy-start.56 = (s32[2048,1]{0,1:T(1,128)}, s32[2048,1]{0,1:T(1,128)S(1)}, u32[]{:S(2)}) copy-start(s32[2048,1]{0,1:T(1,128)S(1)} %compare_select_fusion.1) | copy-start | bytes 24580
  179.8 63.9 %copy-start.52 = (f32[256]{0:T(256)}, f32[256]{0:T(256)S(1)}, u32[]{:S(2)}) copy-start(f32[256]{0:T(256)S(1)} %add_rsqrt_fusion.2) | copy-start | bytes 3076
  236.4 5.6 copy-start.20
  236.4 7.2 copy-start.34
  236.4 250.6 %all-to-all-start = ((bf16[8,340,2048]{2,1,0:T(8,128)(2,1)}), bf16[8,340,2048]{2,1,0:T(8,128)(2,1)}, u32[]{:S(2)}, u32[]{:S(2)}) async-start(bf16[8,340,2048]{2,1,0:T(8,128)(2,1)} %reshape.426), calls=%async_computation.1 | async-start | bytes 22544384 | tf_op jit(solution)/shard_map/all_to_all | solution.py:163
  248.4 20.0 copy-start.30
  487.0 249.2 %all-to-all-start.2 = ((bf16[8,340,2048]{2,1,0:T(8,128)(2,1)}), bf16[8,340,2048]{2,1,0:T(8,128)(2,1)}, u32[]{:S(2)}, u32[]{:S(2)}) async-start(bf16[8,340,2048]{2,1,0:T(8,128)(2,1)} %reshape.430), calls=%async_computation.3 | async-start | bytes 22544384 | tf_op jit(solution)/shard_map/all_to_all | solution.py:163
  515.6 28.3 %copy-start.12 = (bf16[8,340,2048]{2,0,1:T(8,128)(2,1)}, bf16[8,340,2048]{2,0,1:T(8,128)(2,1)S(1)}, u32[]{:S(2)}) copy-start(bf16[8,340,2048]{2,0,1:T(8,128)(2,1)S(1)} %copy.157) | copy-start | bytes 33423364
  882.5 248.9 %all-to-all-start.3 = ((bf16[8,340,2048]{2,1,0:T(8,128)(2,1)}), bf16[8,340,2048]{2,1,0:T(8,128)(2,1)}, u32[]{:S(2)}, u32[]{:S(2)}) async-start(bf16[8,340,2048]{2,1,0:T(8,128)(2,1)} %copy.166), calls=%async_computation.4 | async-start | bytes 22544384 | tf_op jit(solution)/shard_map/all_to_all | solution.py:168
  949.7 187.0 %copy-start.57 = (s32[2048,1]{0,1:T(1,128)S(1)}, s32[2048,1]{0,1:T(1,128)}, u32[]{:S(2)}) copy-start(s32[2048,1]{0,1:T(1,128)} %copy-done.56) | copy-start | bytes 24580
  1131.4 249.3 %all-to-all-start.1 = ((bf16[8,340,2048]{2,1,0:T(8,128)(2,1)}), bf16[8,340,2048]{2,1,0:T(8,128)(2,1)}, u32[]{:S(2)}, u32[]{:S(2)}) async-start(bf16[8,340,2048]{2,1,0:T(8,128)(2,1)} %copy.161), calls=%async_computation.2 | async-start | bytes 22544384 | tf_op jit(solution)/shard_map/all_to_all | solution.py:168
  1136.6 327.3 %all-gather.7.cloned.1.call-start = ((), (), s32[]{:S(2)}) async-start(), calls=%async_computation.12 | async-start | bytes 5242880 | tf_op jit(solution)/shard_map/all_gather | solution.py:250
  1390.2 22.0 copy-start.31
  1412.3 9.8 copy-start.37
  1412.3 9.8 copy-start.59
  1412.3 9.8 copy-start.63
  1412.3 9.8 copy-start.48
  1412.3 9.9 copy-start.35
  1412.3 9.9 copy-start.39
  1412.3 9.8 copy-start.53
  1422.0 6.9 copy-start.21
  1422.0 6.8 copy-start.9
  1422.2 8.5 copy-start.45
  1427.5 3.2 copy-start.67
  1427.5 42.6 %copy-start.64 = (f32[256]{0:T(256)}, f32[256]{0:T(256)S(1)}, u32[]{:S(2)}) copy-start(f32[256]{0:T(256)S(1)} %broadcast_multiply_fusion.4) | copy-start | bytes 3076
  1430.7 182.9 %reduce-scatter.11.cloned.1.call-start = ((), (), s32[]{:S(2)}) async-start(), calls=%async_computation.14 | async-start | bytes 2359296 | tf_op jit(solution)/shard_map/reduce_scatter | solution.py:336
  1430.8 41.7 %copy-start.5 = (bf16[1024,4,128]{2,0,1:T(8,128)(2,1)S(1)}, bf16[1024,4,128]{2,0,1:T(8,128)(2,1)}, u32[]{:S(2)}) copy-start(bf16[1024,4,128]{2,0,1:T(8,128)(2,1)} %copy-done.4) | copy-start | bytes 3145732
  1430.8 41.7 %copy-start.50 = (f32[2,4,512]{2,1,0:T(4,128)S(1)}, f32[2,4,512]{2,1,0:T(4,128)}, u32[]{:S(2)}) copy-start(f32[2,4,512]{2,1,0:T(4,128)} %copy-done.49) | copy-start | bytes 49156
  1474.9 3.4 copy-start.1
  1481.7 5.5 copy-start.2
  1481.7 5.6 copy-start.7
  1481.7 6.3 copy-start.10
  1495.9 3.4 copy-start.1
  1502.6 5.9 copy-start.2
  1502.6 6.2 copy-start.7
  1502.6 6.9 copy-start.10
  1517.9 6.8 copy-start.17
  1530.2 3.5 copy-start.71
  1533.7 3.9 copy-start.69
  1537.5 139.0 %reduce-scatter.13.cloned.1.call-start = ((), (), s32[]{:S(2)}) async-start(), calls=%async_computation.15 | async-start | bytes 2359296 | tf_op jit(solution)/shard_map/reduce_scatter | solution.py:339
  1545.7 4.2 copy-start.72
  1553.7 193.9 %reduce-scatter.15.cloned.1.call-start = ((), (), s32[]{:S(2)}) async-start(), calls=%async_computation.16 | async-start | bytes 2359296 | tf_op jit(solution)/shard_map/reduce_scatter | solution.py:342
  1562.7 256.1 %reduce-scatter.17.cloned.1.call-start = ((), (), s32[]{:S(2)}) async-start(), calls=%async_computation.17 | async-start | bytes 2359296 | tf_op jit(solution)/shard_map/reduce_scatter | solution.py:345
  1569.4 296.2 %reduce-scatter.9.cloned.1.call-start = ((), (), s32[]{:S(2)}) async-start(), calls=%async_computation.13 | async-start | bytes 5242880 | tf_op jit(solution)/shard_map/reduce_scatter | solution.py:322
  1580.8 561.8 %all-gather.9.cloned.1.call-start = ((), (), s32[]{:S(2)}) async-start(), calls=%async_computation.19 | async-start | bytes 57671680 | tf_op jit(solution)/shard_map/all_gather | solution.py:208
  1594.9 823.9 %all-gather.11.cloned.1.call-start = ((), (), s32[]{:S(2)}) async-start(), calls=%async_computation.20 | async-start | bytes 57671680 | tf_op jit(solution)/shard_map/all_gather | solution.py:209
  1609.2 256.5 %copy-start.16 = (bf16[256,2048]{1,0:T(8,128)(2,1)S(1)}, bf16[256,2048]{1,0:T(8,128)(2,1)}, u32[]{:S(2)}) copy-start(bf16[256,2048]{1,0:T(8,128)(2,1)} %param.19) | copy-start | bytes 3145732
  1609.2 256.5 %copy-start.51 = (f32[2048]{0:T(1024)S(1)}, f32[2048]{0:T(1024)}, u32[]{:S(2)}) copy-start(f32[2048]{0:T(1024)} %param.22) | copy-start | bytes 24580
  1609.2 256.4 %copy-start.61 = (f32[256]{0:T(256)S(1)}, f32[256]{0:T(256)}, u32[]{:S(2)}) copy-start(f32[256]{0:T(256)} %copy-done.60) | copy-start | bytes 3076
  1609.2 258.3 %copy-start.55 = (f32[2048]{0:T(1024)S(1)}, f32[2048]{0:T(1024)}, u32[]{:S(2)}) copy-start(f32[2048]{0:T(1024)} %get-tuple-element.208) | copy-start | bytes 24580
  1609.2 298.3 %copy-start.65 = (f32[256]{0:T(256)S(1)}, f32[256]{0:T(256)}, u32[]{:S(2)}) copy-start(f32[256]{0:T(256)} %copy-done.64) | copy-start | bytes 3076
  1609.2 938.1 %all-reduce.3.cloned.1.call-start = ((), (), s32[]{:S(2)}) async-start(), calls=%async_computation.18 | async-start | bytes 262144 | tf_op jit(solution)/shard_map/psum | solution.py:349
  (41 other events, 77.0 us)
Sparse Core Ops, SparseCore 0:
  12.1 37.1 all-gather.4
  106.0 71.7 reduce-scatter.6
  1430.8 33.1 all-gather.6
  1537.6 67.8 reduce-scatter.10
  1609.9 66.5 reduce-scatter.12
  1680.9 66.7 reduce-scatter.14
  1751.6 67.1 reduce-scatter.16
  1822.0 43.5 reduce-scatter.8
  1867.2 275.3 all-gather.8
  2144.0 274.6 all-gather.10
  2424.9 122.3 all-reduce.2
where the time goes:
time: 2560 us
  waiting for transfers between devices  1600 us (62%)
  matrix products  440 us (17%)
  local copies, waits for them, and re-layouts  324 us (13%)
  other arithmetic  115 us (4%)
  blocking collectives  40 us (2%)
    all_to_all x2, waiting for transfers between devices, return_rows(): lax.all_to_all(sent, 'expert', split_axis=0, concat_axis=0, tiled=True)  383 us
    all_to_all x2, waiting for transfers between devices, route_rows(): lax.all_to_all(sent, 'expert', split_axis=0, concat_axis=0, tiled=True)  377 us
    all_gather x1, waiting for transfers between devices, per_device(): lax.all_gather(received, 'tensor', axis=0, tiled=True)  229 us
    all_gather x1, waiting for transfers between devices, per_device(): lax.all_gather(grad_received, 'tensor', axis=0, tiled=True)  222 us
    reduce_scatter x1, waiting for transfers between devices, per_device(): lax.psum_scatter(out_w_part.astype(jnp.bfloat16), 'expert', scatter_dimen...  69.3 us
    reduce_scatter x1, waiting for transfers between devices, per_device(): lax.psum_scatter(value_w_part.astype(jnp.bfloat16), 'expert', scatter_dim...  69.3 us
    reduce_scatter x1, waiting for transfers between devices, per_device(): lax.psum_scatter(jnp.dot(attended, out_w, preferred_element_type=jnp.floa...  65.2 us
    reduce_scatter x1, waiting for transfers between devices, per_device(): lax.psum_scatter(key_w_part.astype(jnp.bfloat16), 'expert', scatter_dimen...  61.1 us
  transfers between devices with their start and end apart: 15, of which 14 were waited for; matrix products, arithmetic and copies ran while one was open for 19% of the time, Pallas kernels for 0%

commit v1 on v0

--- a/solution.py
+++ b/solution.py
@@ -92,8 +92,8 @@
     experts_all = router_w.shape[1]
     top_count = routes.shape[1]
     hidden_width = gate_w.shape[2]
-    capacity = max(2, rows_own * top_count * 4 // (experts_all * 3))
     factor = 1.0 / math.sqrt(head_width)
+    cot_all = lax.all_gather(cotangent, "expert", axis=0, tiled=True)
     source = tokens.astype(jnp.float32)
     scale_in = inverse_rms(source)
     normed_low = (source * scale_in * norm_in).astype(jnp.bfloat16)
@@ -133,11 +133,11 @@
     attended_blocks, log_sums = lax.map(attend, query_blocks)
     attended = attended_blocks.reshape(seq_len, local_heads * head_width)
     attn_out = lax.psum_scatter(
-        jnp.dot(attended, out_w, preferred_element_type=jnp.float32),
+        jnp.dot(attended, out_w, preferred_element_type=jnp.float32).astype(jnp.bfloat16),
         "tensor",
         scatter_dimension=0,
         tiled=True,
-    )
+    ).astype(jnp.float32)
     middle = source + attn_out
     scale_mid = inverse_rms(middle)
     normed_mid = middle * scale_mid * norm_mid
@@ -147,90 +147,82 @@
     mask_float = route_mask.astype(jnp.float32)
     chosen = jnp.sum(mask_float * logits[:, None, :], axis=-1)
     gating = jax.nn.softmax(chosen, axis=-1)
-    mask_flat = route_mask.reshape(rows_own * top_count, experts_all).astype(jnp.int32)
-    running = jnp.cumsum(mask_flat, axis=0)
-    slot_index = jnp.sum((running - 1) * mask_flat, axis=1)
-    positions = routes.reshape(-1) * capacity + slot_index
-    row_owner = jnp.arange(rows_own * top_count, dtype=jnp.int32) // top_count
-    outgoing = (
-        jnp.zeros((experts_all * capacity, model_width), jnp.bfloat16)
-        .at[positions]
-        .set(mid_low[row_owner])
-    )
-
-    def route_rows(buffer):
-        sent = buffer.reshape(expert_count, experts_local * capacity, model_width)
-        arrived = lax.all_to_all(sent, "expert", split_axis=0, concat_axis=0, tiled=True)
-        return arrived.reshape(expert_count, experts_local, capacity, model_width)
-
-    def return_rows(buffer):
-        sent = buffer.reshape(expert_count, experts_local * capacity, model_width)
-        arrived = lax.all_to_all(sent, "expert", split_axis=0, concat_axis=0, tiled=True)
-        return arrived.reshape(experts_all * capacity, model_width)
-
-    received = route_rows(outgoing)
-    gate_pre = jnp.einsum("secd,edf->secf", received, gate_w, preferred_element_type=jnp.float32)
-    up_pre = jnp.einsum("secd,edf->secf", received, up_w, preferred_element_type=jnp.float32)
-    hidden_low = (gate_pre * jax.nn.sigmoid(gate_pre) * up_pre).astype(jnp.bfloat16)
-    expert_out = jnp.einsum(
-        "secf,efd->secd", hidden_low, down_w, preferred_element_type=jnp.float32
-    ).astype(jnp.bfloat16)
-    returned = return_rows(expert_out)
-    per_route = returned[positions].reshape(rows_own, top_count, model_width).astype(jnp.float32)
-    output = (middle + jnp.sum(gating[:, :, None] * per_route, axis=1)).astype(jnp.bfloat16)
     upstream = cotangent.astype(jnp.float32)
-    gate_grad = jnp.sum(per_route * upstream[:, None, :], axis=-1)
-    route_out_grad = (
-        (gating[:, :, None] * upstream[:, None, :])
-        .astype(jnp.bfloat16)
-        .reshape(rows_own * top_count, model_width)
-    )
-    grad_outgoing = (
-        jnp.zeros((experts_all * capacity, model_width), jnp.bfloat16)
-        .at[positions]
-        .set(route_out_grad)
-    )
-    grad_received = route_rows(grad_outgoing)
-    hidden_grad = jnp.einsum(
-        "secd,efd->secf", grad_received, down_w, preferred_element_type=jnp.float32
-    )
-    gate_back, up_back = swiglu_back(hidden_grad, gate_pre, up_pre)
-    input_rows = jnp.einsum("secf,edf->secd", gate_back, gate_w, preferred_element_type=jnp.float32)
-    input_rows = (
-        input_rows + jnp.einsum("secf,edf->secd", up_back, up_w, preferred_element_type=jnp.float32)
-    ).astype(jnp.bfloat16)
-    returned_grads = return_rows(input_rows)
-    expert_input_grad = jnp.sum(
-        returned_grads[positions].reshape(rows_own, top_count, model_width).astype(jnp.float32),
-        axis=1,
-    )
-    all_inputs, all_grads = (
-        lax.all_gather(received, "tensor", axis=0, tiled=True),
-        lax.all_gather(grad_received, "tensor", axis=0, tiled=True),
-    )
+    gates = jnp.sum(mask_float * gating[:, :, None], axis=1)
+    x_all = lax.all_gather(mid_low, "expert", axis=0, tiled=True)
+    gates_all = lax.all_gather(gates, "expert", axis=0, tiled=True)
+    first_expert = lax.axis_index("expert") * experts_local
+    own_gates = lax.dynamic_slice_in_dim(gates_all, first_expert, experts_local, 1)
     part_width = hidden_width // tensor_count
-    first_column = lax.axis_index("tensor") * part_width
-    gate_part = lax.dynamic_slice_in_dim(gate_w, first_column, part_width, 2)
-    up_part = lax.dynamic_slice_in_dim(up_w, first_column, part_width, 2)
-    down_part = lax.dynamic_slice_in_dim(down_w, first_column, part_width, 1)
-    gate_again = jnp.einsum(
-        "secd,edf->secf", all_inputs, gate_part, preferred_element_type=jnp.float32
-    )
-    up_again = jnp.einsum("secd,edf->secf", all_inputs, up_part, preferred_element_type=jnp.float32)
-    hidden_again = (gate_again * jax.nn.sigmoid(gate_again) * up_again).astype(jnp.bfloat16)
-    hidden_back = jnp.einsum(
-        "secd,efd->secf", all_grads, down_part, preferred_element_type=jnp.float32
-    )
-    gate_part_back, up_part_back = swiglu_back(hidden_back, gate_again, up_again)
-    gate_w_grad = jnp.einsum(
-        "secd,secf->edf", all_inputs, gate_part_back, preferred_element_type=jnp.float32
-    )
-    up_w_grad = jnp.einsum(
-        "secd,secf->edf", all_inputs, up_part_back, preferred_element_type=jnp.float32
-    )
-    down_w_grad = jnp.einsum(
-        "secf,secd->efd", hidden_again, all_grads, preferred_element_type=jnp.float32
-    )
+    rows_all = x_all.shape[0]
+    y_part = jnp.zeros((rows_all, model_width), jnp.float32)
+    x_grad_part = jnp.zeros((rows_all, model_width), jnp.float32)
+    gate_grads, gate_parts, up_parts, down_parts = [], [], [], []
+    for e in range(experts_local):
+        hidden_raw = lax.dot_general(
+            cot_all, down_w[e], contract_last, preferred_element_type=jnp.float32
+        )
+        gate_pre = jnp.dot(x_all, gate_w[e], preferred_element_type=jnp.float32)
+        up_pre = jnp.dot(x_all, up_w[e], preferred_element_type=jnp.float32)
+        weight = own_gates[:, e : e + 1]
+        hidden = gate_pre * jax.nn.sigmoid(gate_pre) * up_pre
+        gate_grads.append(jnp.sum(hidden * hidden_raw, axis=1))
+        hidden_low = (hidden * weight).astype(jnp.bfloat16)
+        gate_back, up_back = swiglu_back(hidden_raw * weight, gate_pre, up_pre)
+        y_part = y_part + jnp.dot(hidden_low, down_w[e], preferred_element_type=jnp.float32)
+        x_grad_part = x_grad_part + lax.dot_general(
+            gate_back, gate_w[e], contract_last, preferred_element_type=jnp.float32
+        )
+        x_grad_part = x_grad_part + lax.dot_general(
+            up_back, up_w[e], contract_last, preferred_element_type=jnp.float32
+        )
+        gate_parts.append(
+            jnp.einsum(
+                "nd,ntf->tdf",
+                x_all,
+                gate_back.reshape(rows_all, tensor_count, part_width),
+                preferred_element_type=jnp.float32,
+            ).astype(jnp.bfloat16)
+        )
+        up_parts.append(
+            jnp.einsum(
+                "nd,ntf->tdf",
+                x_all,
+                up_back.reshape(rows_all, tensor_count, part_width),
+                preferred_element_type=jnp.float32,
+            ).astype(jnp.bfloat16)
+        )
+        down_parts.append(
+            lax.dot_general(
+                hidden_low, cot_all, contract_first, preferred_element_type=jnp.float32
+            ).astype(jnp.bfloat16)
+        )
+    x_grad = lax.psum_scatter(
+        x_grad_part.astype(jnp.bfloat16), "expert", scatter_dimension=0, tiled=True
+    )
+    expert_input_grad = x_grad.astype(jnp.float32)
+    gate_grad_sent = jnp.stack(gate_grads, axis=-1)
+    gate_grad_all = lax.all_to_all(gate_grad_sent, "expert", split_axis=0, concat_axis=0, tiled=True)
+    gate_grad_dense = (
+        gate_grad_all.reshape(expert_count, rows_own, experts_local)
+        .transpose(1, 0, 2)
+        .reshape(rows_own, experts_all)
+    )
+    gate_grad = jnp.sum(mask_float * gate_grad_dense[:, None, :], axis=-1)
+    y_sum = lax.psum_scatter(
+        y_part.astype(jnp.bfloat16), "expert", scatter_dimension=0, tiled=True
+    )
+    output = (middle + y_sum.astype(jnp.float32)).astype(jnp.bfloat16)
+
+    def own_part(parts):
+        return [
+            lax.psum_scatter(p, "tensor", scatter_dimension=0, tiled=True).astype(jnp.float32)
+            for p in parts
+        ]
+
+    gate_w_grad = jnp.concatenate(own_part(gate_parts), axis=0)
+    up_w_grad = jnp.concatenate(own_part(up_parts), axis=0)
+    down_w_grad = jnp.stack(own_part(down_parts), axis=0)
     inner_gate = jnp.sum(gating * gate_grad, axis=-1, keepdims=True)
     chosen_grad = gating * (gate_grad - inner_gate)
     logit_grad = jnp.sum(chosen_grad[:, :, None] * mask_float, axis=1)

time: 2560 us -> 1700 us (0.66)
  waiting for transfers between devices: 1600 us -> 1060 us
  local copies, waits for them, and re-layouts: 324 us -> 46.7 us
  matrix products: 440 us -> 404 us
  blocking collectives: 40 us -> 70.1 us
    all_to_all x4 -> x1, waiting for transfers between devices: 760 us -> 3.24 us  [per_device(): lax.all_to_all(gate_grad_sent, 'expert', split_axis=0, concat_axis=0, til...]
    reduce_scatter x0 -> x8, waiting for transfers between devices: none -> 353 us  [the longest x1 151 us: per_device(): lax.psum_scatter(y_part.astype(jnp.bfloat16), 'expert', scatter_dimension...]
    all_gather x2, waiting for transfers between devices: 451 us -> 222 us  [the longest x1 124 us: per_device(): x_all = lax.all_gather(mid_low, 'expert', axis=0, tiled=True)]
    reshape x8 -> x0, local copies, waits for them, and re-layouts: 99.3 us -> none  [the longest x2 33.9 us: return_rows(): sent = buffer.reshape(expert_count, experts_local * capacity, model_width)]
    psum x1, waiting for transfers between devices: 9.43 us -> 81.7 us  [per_device(): lax.psum((norm_in_part, query_gain_part, key_gain_part, norm_mid_part, ro...]
    reduce_scatter x1, waiting for transfers between devices: 0.02 us -> 68.6 us  [per_device(): lax.psum_scatter(query_w_part.astype(jnp.bfloat16), 'expert', scatter_dim...]
    all_to_all x2 -> x0, local copies, waits for them, and re-layouts: 47.9 us -> none  [route_rows(): lax.all_to_all(sent, 'expert', split_axis=0, concat_axis=0, tiled=True)]
    convert_element_type x2 -> x0, local copies, waits for them, and re-layouts: 46 us -> none  [the longest x1 23 us: per_device(): input_rows = (input_rows + jnp.einsum('secf,edf->secd', up_back, up_w, pr...]
  transfers between devices with their start and end apart: 15 -> 20, of which waited for: 14 -> 15; matrix products, arithmetic and copies ran while one was open for 19% -> 18% of each run, Pallas kernels for 0% -> 0%
where the time goes in v1:
time: 1700 us
  waiting for transfers between devices  1060 us (62%)
  matrix products  404 us (24%)
  other arithmetic  99.1 us (6%)
  blocking collectives  70.1 us (4%)
  local copies, waits for them, and re-layouts  46.7 us (3%)
    reduce_scatter x1, waiting for transfers between devices, per_device(): lax.psum_scatter(y_part.astype(jnp.bfloat16), 'expert', scatter_dimension...  151 us
    reduce_scatter x1, waiting for transfers between devices, per_device(): lax.psum_scatter(x_grad_part.astype(jnp.bfloat16), 'expert', scatter_dime...  147 us
    all_gather x1, waiting for transfers between devices, per_device(): x_all = lax.all_gather(mid_low, 'expert', axis=0, tiled=True)  124 us
    all_gather x1, waiting for transfers between devices, per_device(): cot_all = lax.all_gather(cotangent, 'expert', axis=0, tiled=True)  97.2 us
    psum x1, waiting for transfers between devices, per_device(): lax.psum((norm_in_part, query_gain_part, key_gain_part, norm_mid_part, ro...  81.7 us
    reduce_scatter x1, waiting for transfers between devices, per_device(): lax.psum_scatter(key_w_part.astype(jnp.bfloat16), 'expert', scatter_dimen...  69 us
    reduce_scatter x1, waiting for transfers between devices, per_device(): lax.psum_scatter(query_w_part.astype(jnp.bfloat16), 'expert', scatter_dim...  68.6 us
    reduce_scatter x1, waiting for transfers between devices, per_device(): lax.psum_scatter(value_w_part.astype(jnp.bfloat16), 'expert', scatter_dim...  68.1 us
  transfers between devices with their start and end apart: 20, of which 15 were waited for; matrix products, arithmetic and copies ran while one was open for 18% of the time, Pallas kernels for 0%

profile of v1, /device:TPU:0, one launch (start us, length us, event | category | flops | bytes accessed | tf_op | source)
XLA Modules:
  0.0 1699.4 jit_solution(10612123125915313644)
XLA Ops:
  14.0 35.3 %all-gather.5.cloned.1.call-done = bf16[1024,2048]{1,0:T(8,128)(2,1)} async-done(((bf16[256,2048]{1,0:T(8,128)(2,1)}), bf16[1024,2048]{1,0:T(8,128)(2,1)}) %all-gather.5.cloned.1.call-update) | async-done | bytes 4194320 | tf_op jit(solution)/shard_map/all_gather | solution.py:100
  49.3 6.2 convolution_convert_fusion.8
  58.3 5.9 multiply_reduce_fusion.10
  67.1 6.5 multiply_reduce_fusion.9
  76.6 3.5 multiply_multiply_fusion.2
  83.8 16.2 while.27
  100.0 6.6 convolution_convert_fusion.2
  106.8 44.6 %reduce-scatter.15.cloned.1.call-done = bf16[256,2048]{1,0:T(8,128)(2,1)} async-done(((bf16[1024,2048]{1,0:T(8,128)(2,1)}), bf16[256,2048]{1,0:T(8,128)(2,1)}) %reduce-scatter.15.cloned.1.call-update) | async-done | bytes 1048592 | tf_op jit(solution)/shard_map/reduce_scatter | solution.py:135
  156.2 124.5 %all-gather.7.cloned.1.call-done = bf16[2048,2048]{1,0:T(8,128)(2,1)} async-done(((bf16[256,2048]{1,0:T(8,128)(2,1)}), bf16[2048,2048]{1,0:T(8,128)(2,1)}) %all-gather.7.cloned.1.call-update) | async-done | bytes 8388624 | tf_op jit(solution)/shard_map/all_gather | solution.py:152
  280.7 14.9 fusion.51
  295.7 13.2 fusion.55
  308.9 97.2 %all-gather.9.cloned.1.call-done = bf16[2048,2048]{1,0:T(8,128)(2,1)} async-done(((bf16[256,2048]{1,0:T(8,128)(2,1)}), bf16[2048,2048]{1,0:T(8,128)(2,1)}) %all-gather.9.cloned.1.call-update) | async-done | bytes 8388624 | tf_op jit(solution)/shard_map/all_gather | solution.py:96
  406.1 19.7 %multiply_reduce_fusion.3 = (f32[2048]{0:T(1024)S(1)}, f32[2048,1024]{0,1:T(8,128)}) fusion(f32[2048,1024]{0,1:T(8,128)} %fusion.51, f32[2048,1024]{0,1:T(8,128)} %fusion.55, bf16[2048,2048]{1,0:T(8,128)(2,1)} %all-gather.9.cloned.1.call-done, bf16[2,1024,2048]{2,1,0:T(8,128)(2,1)} %param.33), kind=kOutput, calls=%fused_computation.50 | convolution fusion | flops 8604612608 | bytes 37756928 | tf_op jit(solution)/shard_map/dot_general | solution.py:162
  425.8 12.6 fusion.39
  438.5 17.5 %fusion.43 = f32[2048,1024]{0,1:T(8,128)} fusion(bf16[2048,2048]{1,0:T(8,128)(2,1)} %all-gather.7.cloned.1.call-done, bf16[2,2048,1024]{2,1,0:T(8,128)(2,1)} %param.31), kind=kOutput, calls=%fused_computation.79 | convolution fusion | flops 8589934592 | bytes 20971520 | tf_op jit(solution)/shard_map/dot_general | solution.py:165
  456.0 17.1 %multiply_reduce_fusion.2 = (f32[2048]{0:T(1024)S(1)}, f32[2048,1024]{0,1:T(8,128)}) fusion(f32[2048,1024]{0,1:T(8,128)S(1)} %fusion.39, f32[2048,1024]{0,1:T(8,128)} %fusion.43, bf16[2048,2048]{1,0:T(8,128)(2,1)} %all-gather.9.cloned.1.call-done, bf16[2,1024,2048]{2,1,0:T(8,128)(2,1)} %param.33), kind=kOutput, calls=%fused_computation.49 | convolution fusion | flops 8604612608 | bytes 37756928 | tf_op jit(solution)/shard_map/dot_general | solution.py:162
  473.7 3.3 all-to-all-start
  477.1 3.2 fusion.98
  480.4 3.2 all-to-all-done
  483.8 30.6 %all_gather.17 = f32[2048,16]{0,1:T(8,128)S(1)} all-gather(f32[256,16]{0,1:T(8,128)S(1)} %get-tuple-element.252), channel_id=1, replica_groups=mesh['expert'=8,'tensor'=4] {'expert'}, dimensions={0}, use_global_device_ids=true | all-gather | bytes 147456 | tf_op jit(solution)/shard_map/all_gather | solution.py:153
  514.5 12.5 multiply_convert_fusion.1
  527.0 15.7 fusion.41
  542.7 9.2 multiply_convert_fusion.3
  551.8 16.7 fusion.53
  568.6 14.1 fusion.49
  582.7 25.7 %add_convert_fusion = bf16[2048,2048]{1,0:T(8,128)(2,1)} fusion(f32[2048,2048]{1,0:T(8,128)} %fusion.41, f32[2048,2048]{1,0:T(8,128)} %fusion.53, f32[2048,2048]{1,0:T(8,128)} %fusion.49, bf16[2048,1024]{0,1:T(8,128)(2,1)} %get-tuple-element.299, bf16[2,2048,1024]{2,1,0:T(8,128)(2,1)} %param.32), kind=kOutput, calls=%fused_computation.38 | convolution fusion | flops 8606711808 | bytes 67108864 | tf_op jit(solution)/shard_map/dot_general | solution.py:176
  608.5 147.1 %reduce-scatter.19.cloned.1.call-done = bf16[256,2048]{1,0:T(8,128)(2,1)} async-done(((bf16[2048,2048]{1,0:T(8,128)(2,1)}), bf16[256,2048]{1,0:T(8,128)(2,1)}) %reduce-scatter.19.cloned.1.call-update) | async-done | bytes 1048592 | tf_op jit(solution)/shard_map/reduce_scatter | solution.py:200
  755.6 4.9 multiply_reduce_fusion.4
  764.1 13.9 convert_bitcast_fusion.2
  778.0 14.0 convert_bitcast_fusion.3
  792.1 13.9 convert_bitcast_fusion
  806.0 15.0 convert_bitcast_fusion.1
  821.1 16.7 convolution_convert_fusion
  837.9 16.5 convolution_convert_fusion.1
  854.5 6.4 convolution_convert_fusion.7
  862.0 6.3 convolution_convert_fusion.3
  868.4 30.8 %while.28 = (s32[]{:T(128)}, f32[1024,4,128]{0,2,1:T(8,128)}, f32[1024,4,128]{0,2,1:T(8,128)}, f32[2,512,4,128]{3,1,0,2:T(8,128)}, bf16[2,512,4,128]{3,1,2,0:T(8...) while((s32[]{:T(128)}, f32[1024,4,128]{0,2,1:T(8,128)}, ...), condition=%wide.region_23.24_spmd.clone, body=%wide.region_21.23_spmd.clone.sunk | while | flops 2712401920 | bytes 137421200 | solution.py:280
  901.9 6.6 convolution_convert_fusion.4
  911.8 7.5 multiply_add_fusion
  924.7 3.2 fusion.92
  928.1 3.9 convolution_convert_fusion.6
  932.1 5.2 multiply_reduce_fusion.5
  940.2 3.2 fusion.96
  944.4 3.8 convolution_convert_fusion.5
  953.3 6.5 add_convert_fusion.2
  960.5 20.6 %fusion.47 = f32[2048,2048]{1,0:T(8,128)} fusion(bf16[2,1024,2048]{2,1,0:T(8,128)(2,1)} %param.33, f32[2048]{0:T(1024)S(1)} %bitcast.295, f32[2048,1024]{0,1:T(8,128)} %fusion.51, f32[2048,1024]{0,1:T(8,128)} %fusion.55), kind=kOutput, calls=%fused_computation.83 | convolution fusion | flops 8604614656 | bytes 37756928 | tf_op jit(solution)/shard_map/dot_general | solution.py:172
  981.1 21.9 %add_convert_fusion.1 = bf16[2048,2048]{1,0:T(8,128)(2,1)} fusion(f32[2048,2048]{1,0:T(8,128)} %fusion.47, bf16[2,1024,2048]{2,1,0:T(8,128)(2,1)} %param.33, f32[2048]{0:T(1024)S(1)} %bitcast.292, f32[2048,1024]{0,1:T(8,128)} %copy-done.15, f32[2048,1024]{0,1:T(8,128)} %fusion.43), kind=kOutput, calls=%fused_computation.39 | convolution fusion | flops 8613003264 | bytes 46145536 | tf_op jit(solution)/shard_map/dot_general | solution.py:172
  1004.2 3.4 fusion.97
  1007.7 4.4 maximum_convert_fusion
  1012.1 5.3 copy.112
  1017.4 3.8 maximum_convert_fusion.1
  1021.3 5.3 copy.113
  1026.6 7.8 reduce-scatter.41.cloned.1.call-done
  1034.4 47.1 %reduce-scatter.39.cloned.1.call-done = bf16[256,2048]{1,0:T(8,128)(2,1)} async-done(((bf16[1024,2048]{1,0:T(8,128)(2,1)}), bf16[256,2048]{1,0:T(8,128)(2,1)}) %reduce-scatter.39.cloned.1.call-update) | async-done | bytes 1048592 | tf_op jit(solution)/shard_map/reduce_scatter | solution.py:219
  1081.5 3.8 maximum_convert_fusion.2
  1085.4 67.9 %reduce-scatter.29.cloned.1.call-done = bf16[512,256]{1,0:T(8,128)(2,1)} async-done(((bf16[512,2048]{1,0:T(8,128)(2,1)}), bf16[512,256]{1,0:T(8,128)(2,1)}) %reduce-scatter.29.cloned.1.call-update) | async-done | bytes 262160 | tf_op jit(solution)/shard_map/reduce_scatter | solution.py:337
  1155.1 68.1 %reduce-scatter.27.cloned.1.call-done = bf16[256,512]{1,0:T(8,128)(2,1)} async-done(((bf16[2048,512]{1,0:T(8,128)(2,1)}), bf16[256,512]{1,0:T(8,128)(2,1)}) %reduce-scatter.27.cloned.1.call-update) | async-done | bytes 262160 | tf_op jit(solution)/shard_map/reduce_scatter | solution.py:334
  1225.0 68.6 %reduce-scatter.23.cloned.1.call-done = bf16[256,512]{1,0:T(8,128)(2,1)} async-done(((bf16[2048,512]{1,0:T(8,128)(2,1)}), bf16[256,512]{1,0:T(8,128)(2,1)}) %reduce-scatter.23.cloned.1.call-update) | async-done | bytes 262160 | tf_op jit(solution)/shard_map/reduce_scatter | solution.py:328
  1295.4 69.0 %reduce-scatter.25.cloned.1.call-done = bf16[256,512]{1,0:T(8,128)(2,1)} async-done(((bf16[2048,512]{1,0:T(8,128)(2,1)}), bf16[256,512]{1,0:T(8,128)(2,1)}) %reduce-scatter.25.cloned.1.call-update) | async-done | bytes 262160 | tf_op jit(solution)/shard_map/reduce_scatter | solution.py:331
  1366.1 44.1 %reduce-scatter.21.cloned.1.call-done = bf16[256,2048]{1,0:T(8,128)(2,1)} async-done(((bf16[1024,2048]{1,0:T(8,128)(2,1)}), bf16[256,2048]{1,0:T(8,128)(2,1)}) %reduce-scatter.21.cloned.1.call-update) | async-done | bytes 1048592 | tf_op jit(solution)/shard_map/reduce_scatter | solution.py:314
  1412.1 151.1 %reduce-scatter.17.cloned.1.call-done = bf16[256,2048]{1,0:T(8,128)(2,1)} async-done(((bf16[2048,2048]{1,0:T(8,128)(2,1)}), bf16[256,2048]{1,0:T(8,128)(2,1)}) %reduce-scatter.17.cloned.1.call-update) | async-done | bytes 1048592 | tf_op jit(solution)/shard_map/reduce_scatter | solution.py:212
  1563.2 6.3 fusion.84
  1569.6 39.5 %all-reduce = (f32[2048]{0:T(1024)}, f32[128]{0:T(128)}, f32[128]{0:T(128)}, f32[2048]{0:T(1024)}) all-reduce(f32[2048]{0:T(1024)S(1)} %get-tuple-element.249, f32[128]{0:T(128)S(1)} %bitcast_reduce_fusion.1, f32[128]{0:T(128)S(1)} %bitcast_reduce_fusion, ...), channel_id=1, replica_groups=mesh['expert'=8,'tensor'=4] {'expert','tensor'}, use_global_device_ids=true, to_apply=%region_29.30 | all-reduce | flops 4352 | bytes 34816 | tf_op jit(solution)/shard_map/psum | solution.py:341
  1609.1 81.7 %all-reduce.3.cloned.1.call-done = f32[2048,16]{0,1:T(8,128)} async-done(((f32[2048,16]{0,1:T(8,128)}), f32[2048,16]{0,1:T(8,128)}) %all-reduce.3.cloned.1.call-update) | async-done | bytes 131088 | tf_op jit(solution)/shard_map/psum | solution.py:341
  (277 shorter events, 109.1 us)
Async XLA Ops:
  7.2 51.1 %copy-start = (bf16[2048,512]{1,0:T(8,128)(2,1)S(1)}, bf16[2048,512]{1,0:T(8,128)(2,1)}, u32[]{:S(2)}) copy-start(bf16[2048,512]{1,0:T(8,128)(2,1)} %param.23) | copy-start | bytes 6291460
  7.2 42.1 %all-gather.5.cloned.1.call-start = ((), (), s32[]{:S(2)}) async-start(), calls=%async_computation.15 | async-start | bytes 5242880 | tf_op jit(solution)/shard_map/all_gather | solution.py:100
  12.0 139.4 %reduce-scatter.15.cloned.1.call-start = ((), (), s32[]{:S(2)}) async-start(), calls=%async_computation.16 | async-start | bytes 5242880 | tf_op jit(solution)/shard_map/reduce_scatter | solution.py:135
  14.0 66.1 %copy-start.19 = (f32[1024,64]{1,0:T(8,128)}, f32[1024,64]{1,0:T(8,128)S(1)}, u32[]{:S(2)}) copy-start(f32[1024,64]{1,0:T(8,128)S(1)} %get-tuple-element.323) | copy-start | bytes 786436
  14.0 66.1 %copy-start.21 = (f32[1024,64]{1,0:T(8,128)}, f32[1024,64]{1,0:T(8,128)S(1)}, u32[]{:S(2)}) copy-start(f32[1024,64]{1,0:T(8,128)S(1)} %get-tuple-element.324) | copy-start | bytes 786436
  64.2 12.4 copy-start.30
  73.6 2.9 copy-start.51
  73.6 2.9 copy-start.53
  73.6 6.5 copy-start.28
  100.0 6.7 copy-start.3
  100.0 6.7 copy-start.32
  106.7 46.4 %copy-start.35 = (f32[2048]{0:T(1024)S(1)}, f32[2048]{0:T(1024)}, u32[]{:S(2)}) copy-start(f32[2048]{0:T(1024)} %param.29) | copy-start | bytes 24580
  106.7 44.7 %copy-start.8 = (bf16[256,2048]{1,0:T(8,128)(2,1)S(1)}, bf16[256,2048]{1,0:T(8,128)(2,1)}, u32[]{:S(2)}) copy-start(bf16[256,2048]{1,0:T(8,128)(2,1)} %param.19) | copy-start | bytes 3145732
  106.7 174.0 %all-gather.7.cloned.1.call-start = ((), (), s32[]{:S(2)}) async-start(), calls=%async_computation.17 | async-start | bytes 9437184 | tf_op jit(solution)/shard_map/all_gather | solution.py:152
  153.0 607.5 %copy-start.44 = (f32[256]{0:T(256)}, f32[256]{0:T(256)S(1)}, u32[]{:S(2)}) copy-start(f32[256]{0:T(256)S(1)} %add_rsqrt_fusion.2) | copy-start | bytes 3076
  155.7 250.4 %all-gather.9.cloned.1.call-start = ((), (), s32[]{:S(2)}) async-start(), calls=%async_computation.19 | async-start | bytes 9437184 | tf_op jit(solution)/shard_map/all_gather | solution.py:96
  280.7 14.9 copy-start.55
  438.5 17.5 %copy-start.15 = (f32[2048,1024]{0,1:T(8,128)}, f32[2048,1024]{0,1:T(8,128)S(1)}, u32[]{:S(2)}) copy-start(f32[2048,1024]{0,1:T(8,128)S(1)} %fusion.39) | copy-start | bytes 25165828
  456.0 21.1 %copy-start.61 = (f32[2048,16]{0,1:T(8,128)S(1)}, f32[2048,16]{0,1:T(8,128)}, u32[]{:S(2)}) copy-start(f32[2048,16]{0,1:T(8,128)} %param.30) | copy-start | bytes 393220
  456.0 27.6 %copy-start.41 = (s32[256,8]{0,1:T(8,128)S(1)}, s32[256,8]{0,1:T(8,128)}, u32[]{:S(2)}) copy-start(s32[256,8]{0,1:T(8,128)} %param.21) | copy-start | bytes 24580
  473.7 9.9 all-to-all-start
  477.1 278.5 %reduce-scatter.19.cloned.1.call-start = ((), (), s32[]{:S(2)}) async-start(), calls=%async_computation.20 | async-start | bytes 9437184 | tf_op jit(solution)/shard_map/reduce_scatter | solution.py:200
  483.8 271.8 %copy-start.46 = (f32[256,16]{0,1:T(8,128)}, f32[256,16]{0,1:T(8,128)S(1)}, u32[]{:S(2)}) copy-start(f32[256,16]{0,1:T(8,128)S(1)} %get-tuple-element.251) | copy-start | bytes 49156
  514.5 306.7 %copy-start.37 = (f32[2048,1]{0,1:T(1,128)}, f32[2048,1]{0,1:T(1,128)S(1)}, u32[]{:S(2)}) copy-start(f32[2048,1]{0,1:T(1,128)S(1)} %get-tuple-element.321) | copy-start | bytes 24580
  514.5 323.4 %copy-start.39 = (f32[2048,1]{0,1:T(1,128)}, f32[2048,1]{0,1:T(1,128)S(1)}, u32[]{:S(2)}) copy-start(f32[2048,1]{0,1:T(1,128)S(1)} %get-tuple-element.322) | copy-start | bytes 24580
  527.0 15.7 copy-start.24
  527.0 15.7 slice-start
  527.0 15.7 slice-start.1
  551.8 16.7 copy-start.23
  608.4 246.1 %all-gather.11.cloned.1.call-start = ((), (), s32[]{:S(2)}) async-start(), calls=%async_computation.21 | async-start | bytes 5242880 | tf_op jit(solution)/shard_map/all_gather | solution.py:242
  755.6 6.3 copy-start.13
  755.6 6.3 copy-start.14
  760.5 17.4 %copy-start.48 = (f32[256]{0:T(256)}, f32[256]{0:T(256)S(1)}, u32[]{:S(2)}) copy-start(f32[256]{0:T(256)S(1)} %broadcast_multiply_fusion.3) | copy-start | bytes 3076
  764.0 243.7 %reduce-scatter.33.cloned.1.call-start = ((), (), s32[]{:S(2)}) async-start(), calls=%async_computation.29 | async-start | bytes 5242880 | tf_op jit(solution)/shard_map/reduce_scatter | solution.py:219
  778.0 229.8 %reduce-scatter.31.cloned.1.call-start = ((), (), s32[]{:S(2)}) async-start(), calls=%async_computation.28 | async-start | bytes 5242880 | tf_op jit(solution)/shard_map/reduce_scatter | solution.py:219
  792.0 225.4 %reduce-scatter.37.cloned.1.call-start = ((), (), s32[]{:S(2)}) async-start(), calls=%async_computation.31 | async-start | bytes 5242880 | tf_op jit(solution)/shard_map/reduce_scatter | solution.py:219
  806.0 211.5 %reduce-scatter.35.cloned.1.call-start = ((), (), s32[]{:S(2)}) async-start(), calls=%async_computation.30 | async-start | bytes 5242880 | tf_op jit(solution)/shard_map/reduce_scatter | solution.py:219
  821.1 213.3 %reduce-scatter.41.cloned.1.call-start = ((), (), s32[]{:S(2)}) async-start(), calls=%async_computation.33 | async-start | bytes 5242880 | tf_op jit(solution)/shard_map/reduce_scatter | solution.py:219
  837.8 243.7 %reduce-scatter.39.cloned.1.call-start = ((), (), s32[]{:S(2)}) async-start(), calls=%async_computation.32 | async-start | bytes 5242880 | tf_op jit(solution)/shard_map/reduce_scatter | solution.py:219
  854.4 298.9 %reduce-scatter.29.cloned.1.call-start = ((), (), s32[]{:S(2)}) async-start(), calls=%async_computation.26 | async-start | bytes 2359296 | tf_op jit(solution)/shard_map/reduce_scatter | solution.py:337
  862.0 6.4 copy-start.4
  862.0 6.4 copy-start.33
  868.3 354.8 %reduce-scatter.27.cloned.1.call-start = ((), (), s32[]{:S(2)}) async-start(), calls=%async_computation.25 | async-start | bytes 2359296 | tf_op jit(solution)/shard_map/reduce_scatter | solution.py:334
  875.0 2.7 copy-start.7
  890.2 2.7 copy-start.7
  901.9 6.7 copy-start.52
  908.5 3.2 copy-start.20
  908.5 3.2 copy-start.22
  908.6 385.0 %reduce-scatter.23.cloned.1.call-start = ((), (), s32[]{:S(2)}) async-start(), calls=%async_computation.23 | async-start | bytes 2359296 | tf_op jit(solution)/shard_map/reduce_scatter | solution.py:328
  911.8 7.5 copy-start.12
  921.7 3.0 copy-start.31
  924.6 3.4 copy-start.56
  928.1 3.9 copy-start.54
  932.0 432.3 %reduce-scatter.25.cloned.1.call-start = ((), (), s32[]{:S(2)}) async-start(), calls=%async_computation.24 | async-start | bytes 2359296 | tf_op jit(solution)/shard_map/reduce_scatter | solution.py:331
  937.3 2.9 copy-start.29
  940.2 4.2 copy-start.57
  948.2 462.0 %reduce-scatter.21.cloned.1.call-start = ((), (), s32[]{:S(2)}) async-start(), calls=%async_computation.22 | async-start | bytes 5242880 | tf_op jit(solution)/shard_map/reduce_scatter | solution.py:314
  959.9 21.2 %copy-start.38 = (f32[2048,1]{0,1:T(1,128)S(1)}, f32[2048,1]{0,1:T(1,128)}, u32[]{:S(2)}) copy-start(f32[2048,1]{0,1:T(1,128)} %copy-done.37) | copy-start | bytes 24580
  959.9 603.4 %reduce-scatter.17.cloned.1.call-start = ((), (), s32[]{:S(2)}) async-start(), calls=%async_computation.18 | async-start | bytes 9437184 | tf_op jit(solution)/shard_map/reduce_scatter | solution.py:212
  1003.0 687.8 %all-reduce.3.cloned.1.call-start = ((), (), s32[]{:S(2)}) async-start(), calls=%async_computation.27 | async-start | bytes 262144 | tf_op jit(solution)/shard_map/psum | solution.py:341
  1081.5 328.7 %copy-start.34 = (f32[2048]{0:T(1024)S(1)}, f32[2048]{0:T(1024)}, u32[]{:S(2)}) copy-start(f32[2048]{0:T(1024)} %param.22) | copy-start | bytes 24580
  1081.5 328.7 %copy-start.43 = (f32[256]{0:T(256)S(1)}, f32[256]{0:T(256)}, u32[]{:S(2)}) copy-start(f32[256]{0:T(256)} %copy-done.42) | copy-start | bytes 3076
  1085.4 477.9 %copy-start.49 = (f32[256]{0:T(256)S(1)}, f32[256]{0:T(256)}, u32[]{:S(2)}) copy-start(f32[256]{0:T(256)} %copy-done.48) | copy-start | bytes 3076
  1412.1 157.4 %copy-start.50 = (f32[2048]{0:T(1024)S(1)}, f32[2048]{0:T(1024)}, u32[]{:S(2)}) copy-start(f32[2048]{0:T(1024)} %get-tuple-element.247) | copy-start | bytes 24580
  (31 other events, 51.4 us)
Sparse Core Ops, SparseCore 0:
  12.1 37.1 all-gather.4
  106.8 44.4 reduce-scatter.14
  155.8 124.9 all-gather.6
  282.9 123.1 all-gather.8
  608.6 146.9 reduce-scatter.18
  764.1 33.4 all-gather.10
  800.2 44.5 reduce-scatter.32
  848.0 44.5 reduce-scatter.30
  895.7 44.5 reduce-scatter.36
  942.8 44.5 reduce-scatter.34
  989.8 44.5 reduce-scatter.40
  1037.0 44.5 reduce-scatter.38
  1085.0 68.2 reduce-scatter.28
  1156.7 66.4 reduce-scatter.26
  1226.6 66.9 reduce-scatter.22
  1297.5 66.7 reduce-scatter.24
  1366.7 43.4 reduce-scatter.20
  1414.2 149.0 reduce-scatter.16
  1569.3 121.4 all-reduce.2

commit v2 on v1

--- a/solution.py
+++ b/solution.py
@@ -1,8 +1,11 @@
+import functools
 import math
 
 import jax
 import jax.numpy as jnp
 from jax import lax
+from jax.experimental import pallas as pl
+from jax.experimental.pallas import tpu as pltpu
 from jax.sharding import PartitionSpec as P
 
 epsilon = 1e-06
@@ -65,7 +68,997 @@
     return (gate_back, up_back)
 
 
+chunks = 4
+
+
+def pick(index, values):
+    result = values[-1]
+    for j in reversed(range(len(values) - 1)):
+        result = jnp.where(index == j, values[j], result)
+    return result
+
+
+def expert_kernel(
+    experts_all,
+    own_rows,
+    raw_all,
+    gate_hbm,
+    up_hbm,
+    rows_all,
+    hidden_all,
+    gate_all,
+    up_all,
+    total,
+    gate_v,
+    up_v,
+    rows_v,
+    raw_v,
+    hidden_v,
+    gate_b,
+    up_b,
+    parts,
+    side_in,
+    line_in,
+    weight_sem,
+    own_sem,
+    raw_sem,
+    out_sem,
+    rows_sem,
+    gather_recv,
+    gather_send,
+    side_recv,
+    side_send,
+    line_recv,
+    line_send,
+):
+    position = lax.axis_index("expert")
+    peer = lax.axis_index("tensor")
+    z = position // 2
+    x = position % 2
+    experts_local, width, hidden = gate_v.shape
+    rows = rows_v.shape[1]
+    chunk = rows // chunks
+    middle = (z == 1) | (z == 2)
+    ends = (z == 0) | (z == 3)
+    line_slots = [
+        z,
+        pick(z, [1, 0, 3, 2]),
+        pick(z, [2, 2, 1, 1]),
+        pick(z, [3, 3, 0, 0]),
+    ]
+
+    def device(zz, xx):
+        return (zz * 2 + xx, peer)
+
+    def slot_z(k):
+        return pick(k, line_slots)
+
+    weight_copies = [
+        pltpu.make_async_copy(gate_hbm, gate_v, weight_sem.at[0]),
+        pltpu.make_async_copy(up_hbm, up_v, weight_sem.at[1]),
+    ]
+    own_copy = pltpu.make_async_copy(own_rows, rows_v.at[position], own_sem)
+    own_copy.start()
+    for copy in weight_copies:
+        copy.start()
+
+    barrier = pltpu.get_barrier_semaphore()
+    pl.semaphore_signal(barrier, inc=1, device_id=device(z, 1 - x), device_id_type=pl.DeviceIdType.MESH)
+
+    @pl.when(z < 3)
+    def _():
+        pl.semaphore_signal(barrier, inc=1, device_id=device(z + 1, x), device_id_type=pl.DeviceIdType.MESH)
+
+    @pl.when(z > 0)
+    def _():
+        pl.semaphore_signal(barrier, inc=1, device_id=device(z - 1, x), device_id_type=pl.DeviceIdType.MESH)
+
+    pl.semaphore_wait(barrier, 2 + middle.astype(jnp.int32))
+
+    def gather_copy(source, block, index, zz, xx):
+        return pltpu.make_async_remote_copy(
+            src_ref=source,
+            dst_ref=rows_v.at[block],
+            send_sem=gather_send.at[index],
+            recv_sem=gather_recv.at[block],
+            device_id=device(zz, xx),
+            device_id_type=pl.DeviceIdType.MESH,
+        )
+
+    def own_send(index, zz, xx):
+        return gather_copy(own_rows, position, index, zz, xx)
+
+    own_send(0, z, 1 - x).start()
+
+    @pl.when(z < 3)
+    def _():
+        own_send(1, z + 1, x).start()
+
+    @pl.when(z > 0)
+    def _():
+        own_send(2, z - 1, x).start()
+
+    def forward_side(k):
+        block = slot_z(k) * 2 + x
+        return gather_copy(rows_v.at[block], block, 2 + k, z, 1 - x)
+
+    def forward_line(k):
+        block = slot_z(k) * 2 + x
+        target = jnp.where(slot_z(k) < z, z + 1, z - 1)
+        return gather_copy(rows_v.at[block], block, 5 + k, jnp.clip(target, 0, 3), x)
+
+    def arrived(block):
+        gather_copy(own_rows, block, 0, z, 1 - x).wait_recv()
+        pltpu.make_async_copy(rows_v.at[block], rows_all.at[block], rows_sem.at[block]).start()
+
+    def arrive(k):
+        arrived(slot_z(k) * 2 + x)
+        forward_side(k).start()
+
+        @pl.when(middle)
+        def _():
+            forward_line(k).start()
+
+    def side_copy(k, c):
+        area = pl.ds(c * chunk, chunk)
+        return pltpu.make_async_remote_copy(
+            src_ref=parts.at[4 + k, area],
+            dst_ref=side_in.at[k, area],
+            send_sem=side_send.at[k, c],
+            recv_sem=side_recv.at[k, c],
+            device_id=device(z, 1 - x),
+            device_id_type=pl.DeviceIdType.MESH,
+        )
+
+    def line_slot(k):
+        target = slot_z(k)
+        return jnp.where(target < z, target, target + 1)
+
+    def line_copy(k, c):
+        area = pl.ds(c * chunk, chunk)
+        target = jnp.where(slot_z(k) < z, z - 1, z + 1)
+        return pltpu.make_async_remote_copy(
+            src_ref=parts.at[k, area],
+            dst_ref=line_in.at[line_slot(k), area],
+            send_sem=line_send.at[k - 1, c],
+            recv_sem=line_recv.at[line_slot(k), c],
+            device_id=device(jnp.clip(target, 0, 3), x),
+            device_id_type=pl.DeviceIdType.MESH,
+        )
+
+    def line_wait(slot, c):
+        area = pl.ds(c * chunk, chunk)
+        pltpu.make_async_remote_copy(
+            src_ref=parts.at[0, area],
+            dst_ref=line_in.at[slot, area],
+            send_sem=line_send.at[0, c],
+            recv_sem=line_recv.at[slot, c],
+            device_id=device(z, 1 - x),
+            device_id_type=pl.DeviceIdType.MESH,
+        ).wait_recv()
+
+    def relay(k, c, has_line):
+        area = pl.ds(c * chunk, chunk)
+        side_copy(k, c).wait_recv()
+        summed = parts[k, area].astype(jnp.float32) + side_in[k, area].astype(jnp.float32)
+        if has_line is False:
+            parts[k, area] = summed.astype(jnp.bfloat16)
+        else:
+
+            @pl.when(middle)
+            def _():
+                line_wait(line_slot(k), c)
+                parts[k, area] = (
+                    summed + line_in[line_slot(k), area].astype(jnp.float32)
+                ).astype(jnp.bfloat16)
+
+            if has_line is None:
+
+                @pl.when(ends)
+                def _():
+                    parts[k, area] = summed.astype(jnp.bfloat16)
+
+        line_copy(k, c).start()
+
+    def block_of(step):
+        k = pick(step, [0, 1, 0, 2, 1, 3, 2, 3])
+        side = pick(step, [0, 0, 1, 0, 1, 0, 1, 1])
+        return k, side, slot_z(k) * 2 + jnp.where(side == 1, 1 - x, x)
+
+    def raw_copy(step, slot):
+        return pltpu.make_async_copy(raw_all.at[block_of(step)[2]], raw_v.at[slot], raw_sem.at[slot])
+
+    def out_copies(block):
+        return [
+            pltpu.make_async_copy(hidden_v, hidden_all.at[block], out_sem.at[0]),
+            pltpu.make_async_copy(gate_b, gate_all.at[block], out_sem.at[1]),
+            pltpu.make_async_copy(up_b, up_all.at[block], out_sem.at[2]),
+        ]
+
+    raw_copy(0, 0).start()
+    own_copy.wait()
+    pltpu.make_async_copy(rows_v.at[position], rows_all.at[position], rows_sem.at[position]).start()
+    for copy in weight_copies:
+        copy.wait()
+
+    def one_step(step, carry):
+        k, side, block = block_of(step)
+        slot = step % 2
+
+        @pl.when(step == 1)
+        def _():
+            arrive(1)
+
+            @pl.when(middle)
+            def _():
+                arrive(2)
+
+        @pl.when(step == 3)
+        def _():
+            @pl.when(ends)
+            def _():
+                arrive(2)
+
+            @pl.when(middle)
+            def _():
+                arrive(3)
+
+        @pl.when((step == 5) & ends)
+        def _():
+            arrive(3)
+
+        @pl.when(side == 1)
+        def _():
+            arrived(block)
+
+        @pl.when((step == 7) & ends)
+        def _():
+            def one(c, carry):
+                relay(1, c, False)
+                return carry
+
+            lax.fori_loop(0, chunks, one, 0)
+
+        @pl.when(step < 7)
+        def _():
+            raw_copy(step + 1, 1 - slot).start()
+
+        @pl.when(step > 0)
+        def _():
+            for copy in out_copies(block):
+                copy.wait()
+
+        raw_copy(step, slot).wait()
+        rows_low = rows_v[block, :, :width]
+        extra = rows_v[block, :, width:].astype(jnp.float32)
+        lane = lax.broadcasted_iota(jnp.int32, extra.shape, 1)
+        ext = jnp.zeros(extra.shape, jnp.float32)
+        for e in range(experts_local):
+            expert = position * experts_local + e
+            high = lane == expert
+            low = lane == expert + experts_all
+            weight = jnp.sum(jnp.where(high | low, extra, 0.0), axis=1, keepdims=True)
+            gate_grad = jnp.zeros((rows, 1), jnp.float32)
+            for f in range(hidden // 512):
+                columns = pl.ds(f * 512, 512)
+                gate_pre = jnp.dot(rows_low, gate_v[e, :, columns], preferred_element_type=jnp.float32)
+                up_pre = jnp.dot(rows_low, up_v[e, :, columns], preferred_element_type=jnp.float32)
+                target = pl.ds(e * hidden + f * 512, 512)
+                raw = raw_v[slot, :, target].astype(jnp.float32)
+                sig = jax.nn.sigmoid(gate_pre)
+                act = gate_pre * sig
+                hid = act * up_pre
+                gate_grad = gate_grad + jnp.sum(hid * raw, axis=1, keepdims=True)
+                hidden_v[:, target] = (hid * weight).astype(jnp.bfloat16)
+                grad = raw * weight
+                gate_b[:, target] = (grad * up_pre * sig * (1.0 + gate_pre * (1.0 - sig))).astype(jnp.bfloat16)
+                up_b[:, target] = (grad * act).astype(jnp.bfloat16)
+            grad_high = gate_grad.astype(jnp.bfloat16).astype(jnp.float32)
+            ext = jnp.where(high, grad_high, ext)
+            ext = jnp.where(low, gate_grad - grad_high, ext)
+        place = side * 4 + k
+        parts[place, :, width:] = ext.astype(jnp.bfloat16)
+        for copy in out_copies(block):
+            copy.start()
+        for d in range(width // 1024):
+            span = pl.ds(d * 1024, 1024)
+            summed = jnp.zeros((rows, 1024), jnp.float32)
+            for e in range(experts_local):
+                target = pl.ds(e * hidden, hidden)
+                summed = summed + lax.dot_general(
+                    gate_b[:, target], gate_v[e, span, :], contract_last, preferred_element_type=jnp.float32
+                )
+                summed = summed + lax.dot_general(
+                    up_b[:, target], up_v[e, span, :], contract_last, preferred_element_type=jnp.float32
+                )
+            parts[place, :, span] = summed.astype(jnp.bfloat16)
+
+        @pl.when(side == 1)
+        def _():
+            for c in range(chunks):
+                side_copy(k, c).start()
+
+        return carry
+
+    lax.fori_loop(0, 8, one_step, 0)
+
+    def relay_two(c, carry):
+        relay(2, c, None)
+        return carry
+
+    lax.fori_loop(0, chunks, relay_two, 0)
+
+    def relay_rest(c, carry):
+        relay(3, c, None)
+
+        @pl.when(middle)
+        def _():
+            relay(1, c, True)
+
+        return carry
+
+    lax.fori_loop(0, chunks, relay_rest, 0)
+
+    def finish(c, carry):
+        area = pl.ds(c * chunk, chunk)
+        side_copy(0, c).wait_recv()
+        total[area] = parts[0, area].astype(jnp.float32) + side_in[0, area].astype(jnp.float32)
+
+        @pl.when(z < 3)
+        def _():
+            line_wait(z, c)
+            total[area] += line_in[z, area].astype(jnp.float32)
+
+        @pl.when(z > 0)
+        def _():
+            line_wait(z + 1, c)
+            total[area] += line_in[z + 1, area].astype(jnp.float32)
+
+        for k in range(4):
+            side_copy(k, c).wait_send()
+        for k in range(1, 4):
+            line_copy(k, c).wait_send()
+        return carry
+
+    lax.fori_loop(0, chunks, finish, 0)
+
+    own_send(0, z, 1 - x).wait_send()
+
+    @pl.when(z < 3)
+    def _():
+        own_send(1, z + 1, x).wait_send()
+
+    @pl.when(z > 0)
+    def _():
+        own_send(2, z - 1, x).wait_send()
+
+    for k in range(1, 4):
+        forward_side(k).wait_send()
+
+        @pl.when(middle)
+        def _(k=k):
+            forward_line(k).wait_send()
+
+    for copy in out_copies(position):
+        copy.wait()
+    for block in range(8):
+        pltpu.make_async_copy(rows_v.at[block], rows_all.at[block], rows_sem.at[block]).wait()
+
+
+def expert_pass(own_rows, raw_all, gate_w, up_w, experts_all, collective):
+    rows, wide = own_rows.shape
+    experts_local, width, hidden = gate_w.shape
+    inner = experts_local * hidden
+    any_space = pl.BlockSpec(memory_space=pl.ANY)
+    low = jnp.bfloat16
+    dma = pltpu.SemaphoreType.DMA
+    return pl.pallas_call(
+        functools.partial(expert_kernel, experts_all),
+        name="expert_pass",
+        out_shape=(
+            jax.ShapeDtypeStruct((8, rows, wide), low),
+            jax.ShapeDtypeStruct((8, rows, inner), low),
+            jax.ShapeDtypeStruct((8, rows, inner), low),
+            jax.ShapeDtypeStruct((8, rows, inner), low),
+            jax.ShapeDtypeStruct((rows, wide), jnp.float32),
+        ),
+        in_specs=[any_space] * 4,
+        out_specs=(any_space,) * 4 + (pl.BlockSpec(memory_space=pltpu.VMEM),),
+        scratch_shapes=[
+            pltpu.VMEM((experts_local, width, hidden), low),
+            pltpu.VMEM((experts_local, width, hidden), low),
+            pltpu.VMEM((8, rows, wide), low),
+            pltpu.VMEM((2, rows, inner), low),
+            pltpu.VMEM((rows, inner), low),
+            pltpu.VMEM((rows, inner), low),
+            pltpu.VMEM((rows, inner), low),
+            pltpu.VMEM((8, rows, wide), low),
+            pltpu.VMEM((4, rows, wide), low),
+            pltpu.VMEM((5, rows, wide), low),
+            dma((2,)),
+            dma,
+            dma((2,)),
+            dma((3,)),
+            dma((8,)),
+            dma((8,)),
+            dma((9,)),
+            dma((4, chunks)),
+            dma((4, chunks)),
+            dma((5, chunks)),
+            dma((3, chunks)),
+        ],
+        compiler_params=pltpu.CompilerParams(
+            collective_id=collective, has_side_effects=True, vmem_limit_bytes=60 << 20
+        ),
+        cost_estimate=pl.CostEstimate(
+            flops=2 * 4 * 8 * rows * width * inner, bytes_accessed=64 << 20, transcendentals=8 * rows * inner
+        ),
+    )(own_rows, raw_all, gate_w, up_w)
+
+
+def scatter_kernel(
+    parts, total, own, side_in, line_in, own_sem, side_recv, side_send, line_recv, line_send
+):
+    position = lax.axis_index("expert")
+    peer = lax.axis_index("tensor")
+    z = position // 2
+    x = position % 2
+    chunk = own.shape[1] // chunks
+    middle = (z == 1) | (z == 2)
+    line_slots = [
+        z,
+        pick(z, [1, 0, 3, 2]),
+        pick(z, [2, 2, 1, 1]),
+        pick(z, [3, 3, 0, 0]),
+    ]
+    mesh_ids = pl.DeviceIdType.MESH
+
+    def device(zz, xx):
+        return (zz * 2 + xx, peer)
+
+    own_copies = [
+        pltpu.make_async_copy(parts.at[line_slots[k] * 2 + x], own.at[k], own_sem.at[k]) for k in range(4)
+    ]
+    for k in (3, 2, 1, 0):
+        own_copies[k].start()
+
+    barrier = pltpu.get_barrier_semaphore()
+    pl.semaphore_signal(barrier, inc=1, device_id=device(z, 1 - x), device_id_type=mesh_ids)
+
+    @pl.when(z < 3)
+    def _():
+        pl.semaphore_signal(barrier, inc=1, device_id=device(z + 1, x), device_id_type=mesh_ids)
+
+    @pl.when(z > 0)
+    def _():
+        pl.semaphore_signal(barrier, inc=1, device_id=device(z - 1, x), device_id_type=mesh_ids)
+
+    pl.semaphore_wait(barrier, 2 + middle.astype(jnp.int32))
+
+    def side_copy(k, c):
+        area = pl.ds(c * chunk, chunk)
+        return pltpu.make_async_remote_copy(
+            src_ref=parts.at[pick(k, line_slots) * 2 + 1 - x, area],
+            dst_ref=side_in.at[k, area],
+            send_sem=side_send.at[k, c],
+            recv_sem=side_recv.at[k, c],
+            device_id=device(z, 1 - x),
+            device_id_type=mesh_ids,
+        )
+
+    def line_slot(k):
+        target = pick(k, line_slots)
+        return jnp.where(target < z, target, target + 1)
+
+    def line_copy(k, c):
+        area = pl.ds(c * chunk, chunk)
+        target = jnp.where(pick(k, line_slots) < z, z - 1, z + 1)
+        return pltpu.make_async_remote_copy(
+            src_ref=own.at[k, area],
+            dst_ref=line_in.at[line_slot(k), area],
+            send_sem=line_send.at[k - 1, c],
+            recv_sem=line_recv.at[line_slot(k), c],
+            device_id=device(jnp.clip(target, 0, 3), x),
+            device_id_type=mesh_ids,
+        )
+
+    def line_wait(slot, c):
+        area = pl.ds(c * chunk, chunk)
+        pltpu.make_async_remote_copy(
+            src_ref=own.at[0, area],
+            dst_ref=line_in.at[slot, area],
+            send_sem=line_send.at[0, c],
+            recv_sem=line_recv.at[slot, c],
+            device_id=device(z, 1 - x),
+            device_id_type=mesh_ids,
+        ).wait_recv()
+
+    def send_order(i):
+        return jnp.where(middle, pick(i, [3, 1, 2, 0]), pick(i, [3, 2, 1, 0]))
+
+    def start_side(i, carry):
+        for c in range(chunks):
+            side_copy(send_order(i), c).start()
+        return carry
+
+    lax.fori_loop(0, 4, start_side, 0)
+    for k in (3, 2, 1, 0):
+        own_copies[k].wait()
+
+    def relay(i, carry):
+        k = send_order(i // chunks)
+        c = i % chunks
+        area = pl.ds(c * chunk, chunk)
+        side_copy(k, c).wait_recv()
+        own[k, area] = (
+            own[k, area].astype(jnp.float32) + side_in[k, area].astype(jnp.float32)
+        ).astype(jnp.bfloat16)
+
+        @pl.when(middle)
+        def _():
+            line_wait(line_slot(k), c)
+            own[k, area] = (
+                own[k, area].astype(jnp.float32) + line_in[line_slot(k), area].astype(jnp.float32)
+            ).astype(jnp.bfloat16)
+
+        line_copy(k, c).start()
+        return carry
+
+    lax.fori_loop(0, 3 * chunks, relay, 0)
+
+    def finish(c, carry):
+        area = pl.ds(c * chunk, chunk)
+        side_copy(0, c).wait_recv()
+        total[area] = own[0, area].astype(jnp.float32) + side_in[0, area].astype(jnp.float32)
+
+        @pl.when(z < 3)
+        def _():
+            line_wait(z, c)
+            total[area] += line_in[z, area].astype(jnp.float32)
+
+        @pl.when(z > 0)
+        def _():
+            line_wait(z + 1, c)
+            total[area] += line_in[z + 1, area].astype(jnp.float32)
+
+        for k in range(4):
+            side_copy(k, c).wait_send()
+        for k in range(1, 4):
+            line_copy(k, c).wait_send()
+        return carry
+
+    lax.fori_loop(0, chunks, finish, 0)
+
+
+def scatter_parts(parts, collective):
+    rows, wide = parts.shape[1:]
+    low = jnp.bfloat16
+    dma = pltpu.SemaphoreType.DMA
+    return pl.pallas_call(
+        scatter_kernel,
+        name="scatter_parts",
+        out_shape=jax.ShapeDtypeStruct((rows, wide), jnp.float32),
+        in_specs=[pl.BlockSpec(memory_space=pl.ANY)],
+        out_specs=pl.BlockSpec(memory_space=pltpu.VMEM),
+        scratch_shapes=[
+            pltpu.VMEM((4, rows, wide), low),
+            pltpu.VMEM((4, rows, wide), low),
+            pltpu.VMEM((5, rows, wide), low),
+            dma((4,)),
+            dma((4, chunks)),
+            dma((4, chunks)),
+            dma((5, chunks)),
+            dma((3, chunks)),
+        ],
+        compiler_params=pltpu.CompilerParams(
+            collective_id=collective, has_side_effects=True, vmem_limit_bytes=40 << 20
+        ),
+        cost_estimate=pl.CostEstimate(flops=8 * rows * wide, bytes_accessed=300 << 20, transcendentals=0),
+    )(parts)
+
+
+def sum_kernel(own, total, incoming, recv, send):
+    position = lax.axis_index("expert")
+    peer = lax.axis_index("tensor")
+    mesh_ids = pl.DeviceIdType.MESH
+
+    def flip(index, bit):
+        return index + bit - 2 * bit * ((index // bit) % 2)
+
+    partners = [
+        (position, flip(peer, 1)),
+        (position, flip(peer, 2)),
+        (flip(position, 1), peer),
+        (flip(position, 2), peer),
+        (flip(position, 4), peer),
+    ]
+    barrier = pltpu.get_barrier_semaphore()
+    for partner in partners:
+        pl.semaphore_signal(barrier, inc=1, device_id=partner, device_id_type=mesh_ids)
+    pl.semaphore_wait(barrier, len(partners))
+    total[0] = own[...]
+    for i, partner in enumerate(partners):
+        copy = pltpu.make_async_remote_copy(
+            src_ref=total.at[i],
+            dst_ref=incoming.at[i],
+            send_sem=send.at[i],
+            recv_sem=recv.at[i],
+            device_id=partner,
+            device_id_type=mesh_ids,
+        )
+        copy.start()
+        copy.wait()
+        total[i + 1] = total[i] + incoming[i]
+
+
+def sum_everywhere(own, collective):
+    steps = 5
+    return pl.pallas_call(
+        sum_kernel,
+        name="sum_everywhere",
+        out_shape=jax.ShapeDtypeStruct((steps + 1,) + own.shape, jnp.float32),
+        in_specs=[pl.BlockSpec(memory_space=pltpu.VMEM)],
+        out_specs=pl.BlockSpec(memory_space=pltpu.VMEM),
+        scratch_shapes=[
+            pltpu.VMEM((steps,) + own.shape, jnp.float32),
+            pltpu.SemaphoreType.DMA((steps,)),
+            pltpu.SemaphoreType.DMA((steps,)),
+        ],
+        compiler_params=pltpu.CompilerParams(collective_id=collective, has_side_effects=True),
+        cost_estimate=pl.CostEstimate(flops=own.size * steps, bytes_accessed=40 << 20, transcendentals=0),
+    )(own)[steps]
+
+
+def weight_kernel(order, left, right, out):
+    wide = left.shape[1]
+    step = min(512, wide)
+    for d in range(out.shape[2] // step):
+        span = pl.ds(d * step, step)
+        out[0, 0, span, :] = lax.dot_general(
+            left[:, span], right[...], contract_first, preferred_element_type=jnp.float32
+        ).astype(out.dtype)
+
+
+def input_weight_parts(order, rows_all, grads, width, experts_local):
+    count, wide = rows_all.shape
+    hidden = grads.shape[1] // experts_local
+    part = hidden // 4
+    pieces = order.shape[0]
+    return pl.pallas_call(
+        weight_kernel,
+        name="input_weight_parts",
+        out_shape=jax.ShapeDtypeStruct((pieces, experts_local, width, part), jnp.bfloat16),
+        grid_spec=pltpu.PrefetchScalarGridSpec(
+            num_scalar_prefetch=1,
+            grid=(pieces, experts_local),
+            in_specs=[
+                pl.BlockSpec((count, width), lambda r, e, order: (0, 0), pipeline_mode=pl.Buffered(1)),
+                pl.BlockSpec((count, part), lambda r, e, order: (0, e * 4 + order[r])),
+            ],
+            out_specs=pl.BlockSpec((1, 1, width, part), lambda r, e, order: (r, e, 0, 0)),
+        ),
+        compiler_params=pltpu.CompilerParams(vmem_limit_bytes=48 << 20),
+        cost_estimate=pl.CostEstimate(
+            flops=2 * pieces * experts_local * count * width * part,
+            bytes_accessed=2 * count * width + 2 * pieces * experts_local * part * (count + width),
+            transcendentals=0,
+        ),
+    )(order, rows_all, grads)
+
+
+def output_weight_parts(order, hidden_all, grads, experts_local):
+    count, width = grads.shape
+    hidden = hidden_all.shape[1] // experts_local
+    part = hidden // 4
+    pieces = order.shape[0]
+    return pl.pallas_call(
+        weight_kernel,
+        name="output_weight_parts",
+        out_shape=jax.ShapeDtypeStruct((pieces, experts_local, part, width), jnp.bfloat16),
+        grid_spec=pltpu.PrefetchScalarGridSpec(
+            num_scalar_prefetch=1,
+            grid=(pieces, experts_local),
+            in_specs=[
+                pl.BlockSpec((count, part), lambda r, e, order: (0, e * 4 + order[r])),
+                pl.BlockSpec((count, width), lambda r, e, order: (0, 0), pipeline_mode=pl.Buffered(1)),
+            ],
+            out_specs=pl.BlockSpec((1, 1, part, width), lambda r, e, order: (r, e, 0, 0)),
+        ),
+        compiler_params=pltpu.CompilerParams(vmem_limit_bytes=48 << 20),
+        cost_estimate=pl.CostEstimate(
+            flops=2 * pieces * experts_local * count * width * part,
+            bytes_accessed=2 * count * width + 2 * pieces * experts_local * part * (count + width),
+            transcendentals=0,
+        ),
+    )(order, hidden_all, grads)
+
+
+def exchange(pieces_far, pieces_near):
+    swap_core = [(0, 1), (1, 0), (2, 3), (3, 2)]
+    swap_line = [(0, 2), (1, 3), (2, 0), (3, 1)]
+    arrived = lax.ppermute(pieces_far, "tensor", swap_core)
+    own = pieces_near[0].astype(jnp.float32) + arrived[0].astype(jnp.float32)
+    sent = (pieces_near[1].astype(jnp.float32) + arrived[1].astype(jnp.float32)).astype(jnp.bfloat16)
+    return own + lax.ppermute(sent, "tensor", swap_line).astype(jnp.float32)
+
+
 def per_device(
+    tokens,
+    cotangent,
+    routes,
+    norm_in,
+    query_w,
+    key_w,
+    value_w,
+    out_w,
+    query_gain,
+    key_gain,
+    norm_mid,
+    router_w,
+    gate_w,
+    up_w,
+    down_w,
+):
+    rows_own = tokens.shape[0]
+    model_width = tokens.shape[1]
+    expert_count = lax.axis_size("expert")
+    head_width = query_gain.shape[0]
+    local_heads = query_w.shape[1] // head_width
+    experts_local = gate_w.shape[0]
+    experts_all = router_w.shape[1]
+    top_count = routes.shape[1]
+    hidden_width = gate_w.shape[2]
+    factor = 1.0 / math.sqrt(head_width)
+    cot_all = lax.all_gather(cotangent, "expert", axis=0, tiled=True)
+    source = tokens.astype(jnp.float32)
+    scale_in = inverse_rms(source)
+    normed_low = (source * scale_in * norm_in).astype(jnp.bfloat16)
+    gathered = lax.all_gather(normed_low, "tensor", axis=0, tiled=True)
+    seq_len = gathered.shape[0]
+    query_pre = jnp.dot(gathered, query_w, preferred_element_type=jnp.float32)
+    key_pre = jnp.dot(gathered, key_w, preferred_element_type=jnp.float32)
+    value_low = jnp.dot(gathered, value_w, preferred_element_type=jnp.float32).astype(jnp.bfloat16)
+    cosine, sine_table = rotary_tables(seq_len, head_width)
+    query_heads = query_pre.reshape(seq_len, local_heads, head_width)
+    key_heads = key_pre.reshape(seq_len, local_heads, head_width)
+    query_scale = inverse_rms(query_heads)
+    key_scale = inverse_rms(key_heads)
+    query_low = rotate(query_heads * query_scale * query_gain, cosine, sine_table).astype(
+        jnp.bfloat16
+    )
+    key_low = rotate(key_heads * key_scale * key_gain, cosine, sine_table).astype(jnp.bfloat16)
+    value_heads = value_low.reshape(seq_len, local_heads, head_width)
+    block_rows = min(512, seq_len)
+    block_count = seq_len // block_rows
+    query_blocks = query_low.reshape(block_count, block_rows, local_heads, head_width)
+
+    def attend(query_block):
+        scores = (
+            jnp.einsum("qhd,khd->hqk", query_block, key_low, preferred_element_type=jnp.float32)
+            * factor
+        )
+        row_max = jnp.max(scores, axis=-1, keepdims=True)
+        shifted = jnp.exp(scores - row_max)
+        row_sum = jnp.sum(shifted, axis=-1, keepdims=True)
+        probs_low = (shifted / row_sum).astype(jnp.bfloat16)
+        mixture = jnp.einsum(
+            "hqk,khd->qhd", probs_low, value_heads, preferred_element_type=jnp.float32
+        )
+        return (mixture.astype(jnp.bfloat16), (row_max + jnp.log(row_sum))[..., 0])
+
+    attended_blocks, log_sums = lax.map(attend, query_blocks)
+    attended = attended_blocks.reshape(seq_len, local_heads * head_width)
+    attn_out = lax.psum_scatter(
+        jnp.dot(attended, out_w, preferred_element_type=jnp.float32).astype(jnp.bfloat16),
+        "tensor",
+        scatter_dimension=0,
+        tiled=True,
+    ).astype(jnp.float32)
+    middle = source + attn_out
+    scale_mid = inverse_rms(middle)
+    normed_mid = middle * scale_mid * norm_mid
+    mid_low = normed_mid.astype(jnp.bfloat16)
+    logits = jnp.dot(normed_mid, router_w, precision=highest, preferred_element_type=jnp.float32)
+    route_mask = routes[:, :, None] == jnp.arange(experts_all, dtype=jnp.int32)[None, None, :]
+    mask_float = route_mask.astype(jnp.float32)
+    chosen = jnp.sum(mask_float * logits[:, None, :], axis=-1)
+    gating = jax.nn.softmax(chosen, axis=-1)
+    upstream = cotangent.astype(jnp.float32)
+    gates = jnp.sum(mask_float * gating[:, :, None], axis=1)
+    gates_high = gates.astype(jnp.bfloat16)
+    gates_low = (gates - gates_high.astype(jnp.float32)).astype(jnp.bfloat16)
+    spare = jnp.zeros((rows_own, 128 - 2 * experts_all), jnp.bfloat16)
+    own_rows = jnp.concatenate([mid_low, gates_high, gates_low, spare], axis=1)
+    blocks = (expert_count, rows_own, experts_local * hidden_width)
+    raw_all = jnp.concatenate(
+        [
+            lax.dot_general(
+                cot_all, down_w[e], contract_last, preferred_element_type=jnp.float32
+            ).astype(jnp.bfloat16)
+            for e in range(experts_local)
+        ],
+        axis=1,
+    ).reshape(blocks)
+    rows_all, hidden_all, gate_all, up_all, row_total = expert_pass(
+        own_rows, raw_all, gate_w, up_w, experts_all, 1
+    )
+    expert_input_grad = row_total[:, :model_width]
+    gate_grad_dense = (
+        row_total[:, model_width : model_width + experts_all]
+        + row_total[:, model_width + experts_all : model_width + 2 * experts_all]
+    )
+    gate_grad = jnp.sum(mask_float * gate_grad_dense[:, None, :], axis=-1)
+    count = expert_count * rows_own
+    inner_all = experts_local * hidden_width
+    rows_all = rows_all.reshape(count, own_rows.shape[1])
+    hidden_all = hidden_all.reshape(count, inner_all)
+    gate_all = gate_all.reshape(count, inner_all)
+    up_all = up_all.reshape(count, inner_all)
+    y_part = jnp.dot(
+        hidden_all, down_w.reshape(inner_all, model_width), preferred_element_type=jnp.float32
+    ).astype(jnp.bfloat16)
+    y_sum = lax.psum_scatter(y_part, "expert", scatter_dimension=0, tiled=True)
+    output = (middle + y_sum.astype(jnp.float32)).astype(jnp.bfloat16)
+    me = lax.axis_index("tensor")
+    far = jnp.stack([me ^ 1, me ^ 3]).astype(jnp.int32)
+    near = jnp.stack([me, me ^ 2]).astype(jnp.int32)
+    gate_w_grad = exchange(
+        input_weight_parts(far, rows_all, gate_all, model_width, experts_local),
+        input_weight_parts(near, rows_all, gate_all, model_width, experts_local),
+    )
+    up_w_grad = exchange(
+        input_weight_parts(far, rows_all, up_all, model_width, experts_local),
+        input_weight_parts(near, rows_all, up_all, model_width, experts_local),
+    )
+    down_w_grad = exchange(
+        output_weight_parts(far, hidden_all, cot_all, experts_local),
+        output_weight_parts(near, hidden_all, cot_all, experts_local),
+    )
+    inner_gate = jnp.sum(gating * gate_grad, axis=-1, keepdims=True)
+    chosen_grad = gating * (gate_grad - inner_gate)
+    logit_grad = jnp.sum(chosen_grad[:, :, None] * mask_float, axis=1)
+    router_part = lax.dot_general(
+        normed_mid,
+        logit_grad,
+        contract_first,
+        precision=highest,
+        preferred_element_type=jnp.float32,
+    )
+    normed_mid_grad = expert_input_grad + lax.dot_general(
+        logit_grad, router_w, contract_last, precision=highest, preferred_element_type=jnp.float32
+    )
+    norm_mid_part = jnp.sum(normed_mid_grad * middle * scale_mid, axis=0)
+    middle_grad = upstream + norm_backward(normed_mid_grad, middle, scale_mid, norm_mid)
+    branch_low = middle_grad.astype(jnp.bfloat16)
+    branch_all = lax.all_gather(branch_low, "tensor", axis=0, tiled=True)
+    attended_grad = lax.dot_general(
+        branch_all, out_w, contract_last, preferred_element_type=jnp.float32
+    ).astype(jnp.bfloat16)
+    out_w_part = lax.dot_general(
+        attended, branch_all, contract_first, preferred_element_type=jnp.float32
+    )
+    grad_blocks = attended_grad.reshape(block_count, block_rows, local_heads, head_width)
+
+    def attend_back(carry, inputs):
+        key_total, value_total = carry
+        query_block, grad_block, log_block = inputs
+        scores = (
+            jnp.einsum("qhd,khd->hqk", query_block, key_low, preferred_element_type=jnp.float32)
+            * factor
+        )
+        probs = jnp.exp(scores - log_block[:, :, None])
+        probs_low = probs.astype(jnp.bfloat16)
+        value_total = value_total + jnp.einsum(
+            "hqk,qhd->khd", probs_low, grad_block, preferred_element_type=jnp.float32
+        )
+        prob_grad = jnp.einsum(
+            "qhd,khd->hqk", grad_block, value_heads, preferred_element_type=jnp.float32
+        )
+        delta = jnp.sum(probs * prob_grad, axis=-1, keepdims=True)
+        score_low = (probs * (prob_grad - delta)).astype(jnp.bfloat16)
+        query_part = (
+            jnp.einsum("hqk,khd->qhd", score_low, key_low, preferred_element_type=jnp.float32)
+            * factor
+        )
+        key_total = (
+            key_total
+            + jnp.einsum("hqk,qhd->khd", score_low, query_block, preferred_element_type=jnp.float32)
+            * factor
+        )
+        return ((key_total, value_total), query_part)
+
+    zero_heads = jnp.zeros((seq_len, local_heads, head_width), jnp.float32)
+    (key_grad, value_total), query_parts = lax.scan(
+        attend_back, (zero_heads, zero_heads), (query_blocks, grad_blocks, log_sums)
+    )
+    query_grad = query_parts.reshape(seq_len, local_heads, head_width)
+    value_grad_low = value_total.reshape(seq_len, local_heads * head_width).astype(jnp.bfloat16)
+    query_rot_grad = rotate_back(query_grad, cosine, sine_table)
+    key_rot_grad = rotate_back(key_grad, cosine, sine_table)
+    query_gain_part = jnp.sum(query_rot_grad * query_heads * query_scale, axis=(0, 1))
+    key_gain_part = jnp.sum(key_rot_grad * key_heads * key_scale, axis=(0, 1))
+    query_pre_grad = (
+        norm_backward(query_rot_grad, query_heads, query_scale, query_gain)
+        .reshape(seq_len, local_heads * head_width)
+        .astype(jnp.bfloat16)
+    )
+    key_pre_grad = (
+        norm_backward(key_rot_grad, key_heads, key_scale, key_gain)
+        .reshape(seq_len, local_heads * head_width)
+        .astype(jnp.bfloat16)
+    )
+    query_w_part = lax.dot_general(
+        gathered, query_pre_grad, contract_first, preferred_element_type=jnp.float32
+    )
+    key_w_part = lax.dot_general(
+        gathered, key_pre_grad, contract_first, preferred_element_type=jnp.float32
+    )
+    value_w_part = lax.dot_general(
+        gathered, value_grad_low, contract_first, preferred_element_type=jnp.float32
+    )
+    summed = lax.dot_general(
+        query_pre_grad, query_w, contract_last, preferred_element_type=jnp.float32
+    )
+    summed = summed + lax.dot_general(
+        key_pre_grad, key_w, contract_last, preferred_element_type=jnp.float32
+    )
+    rows_grad = lax.psum_scatter(
+        (
+            summed
+            + lax.dot_general(
+                value_grad_low, value_w, contract_last, preferred_element_type=jnp.float32
+            )
+        ).astype(jnp.bfloat16),
+        "tensor",
+        scatter_dimension=0,
+        tiled=True,
+    ).astype(jnp.float32)
+    norm_in_part = jnp.sum(rows_grad * source * scale_in, axis=0)
+    input_grad = middle_grad + norm_backward(rows_grad, source, scale_in, norm_in)
+    out_w_grad = lax.psum_scatter(
+        out_w_part.astype(jnp.bfloat16), "expert", scatter_dimension=1, tiled=True
+    ).astype(jnp.float32)
+    part_rows = model_width // expert_count
+    local_width = local_heads * head_width
+    weight_parts = jnp.concatenate(
+        [p.astype(jnp.bfloat16) for p in (query_w_part, key_w_part, value_w_part)], axis=1
+    ).reshape(expert_count, part_rows, 3 * local_width)
+    weight_sums = scatter_parts(weight_parts, 2)
+    query_w_grad = weight_sums[:, :local_width]
+    key_w_grad = weight_sums[:, local_width : 2 * local_width]
+    value_w_grad = weight_sums[:, 2 * local_width :]
+    norm_mid_grad, router_w_grad = lax.psum((norm_mid_part, router_part), ("expert", "tensor"))
+    small = jnp.concatenate(
+        [
+            norm_in_part,
+            query_gain_part,
+            key_gain_part,
+            jnp.zeros((-(model_width + 2 * head_width) % 1024,), jnp.float32),
+        ]
+    ).reshape(-1, 128)
+    sums = sum_everywhere(small, 3).reshape(-1)
+    norm_in_grad = sums[:model_width]
+    query_gain_grad = sums[model_width : model_width + head_width]
+    key_gain_grad = sums[model_width + head_width : model_width + 2 * head_width]
+    return (
+        output,
+        input_grad,
+        norm_in_grad,
+        query_w_grad,
+        key_w_grad,
+        value_w_grad,
+        out_w_grad,
+        query_gain_grad,
+        key_gain_grad,
+        norm_mid_grad,
+        router_w_grad,
+        gate_w_grad,
+        up_w_grad,
+        down_w_grad,
+    )
+
+
+def per_device_general(
     tokens,
     cotangent,
     routes,
@@ -379,7 +1372,7 @@
         P("expert", None, None),
     )
     return jax.shard_map(
-        per_device,
+        per_device if dict(mesh.shape) == {"expert": 8, "tensor": 4} else per_device_general,
         mesh=mesh,
         in_specs=placed,
         out_specs=(

time: 1700 us -> 1030 us (0.61)
  waiting for transfers between devices: 1060 us -> 191 us
  Pallas kernels: 0 us -> 441 us
  matrix products: 404 us -> 155 us
  blocking collectives: 70.1 us -> 40.2 us
    reduce_scatter x11 -> x1, waiting for transfers between devices: 559 us -> 0.01 us  [per_device(): y_sum = lax.psum_scatter(y_part, 'expert', scatter_dimension=0, tiled=True)]
    pallas_call x0 -> x9, Pallas kernels: none -> 441 us  [the longest x1 237 us: expert_pass(): pl.pallas_call(functools.partial(expert_kernel, experts_all), name='exper...]
    dot_general x16 -> x1, matrix products: 263 us -> 25.2 us  [per_device(): jnp.dot(hidden_all, down_w.reshape(inner_all, model_width), preferred_ele...]
    all_gather x1 -> x0, waiting for transfers between devices: 124 us -> none  [per_device(): x_all = lax.all_gather(mid_low, 'expert', axis=0, tiled=True)]
    psum x1, waiting for transfers between devices: 81.7 us -> 0.01 us  [per_device(): lax.psum((norm_mid_part, router_part), ('expert', 'tensor'))]
    reduce_scatter x1, waiting for transfers between devices: 67.9 us -> 0.01 us  [per_device(): lax.psum_scatter(out_w_part.astype(jnp.bfloat16), 'expert', scatter_dimen...]
    reduce_scatter x1, waiting for transfers between devices: 44.1 us -> 0.01 us  [per_device(): lax.psum_scatter((summed + lax.dot_general(value_grad_low, value_w, contr...]
    all_gather x1, waiting for transfers between devices: 0.02 us -> 34.6 us  [per_device(): branch_all = lax.all_gather(branch_low, 'tensor', axis=0, tiled=True)]
  transfers between devices with their start and end apart: 20 -> 14, of which waited for: 15 -> 4; matrix products, arithmetic and copies ran while one was open for 18% -> 11% of each run, Pallas kernels for 0% -> 20%
where the time goes in v2:
time: 1030 us
  Pallas kernels  441 us (43%)
  waiting for transfers between devices  191 us (19%)
  matrix products  155 us (15%)
  other arithmetic  114 us (11%)
  local copies, waits for them, and re-layouts  60.6 us (6%)
  blocking collectives  40.2 us (4%)
  between operations  16.6 us (2%)
    pallas_call x1, Pallas kernels, expert_pass(): pl.pallas_call(functools.partial(expert_kernel, experts_all), name='exper...  237 us
    pallas_call x1, Pallas kernels, scatter_parts(): pl.pallas_call(scatter_kernel, name='scatter_parts', out_shape=jax.ShapeD...  97.3 us
    all_gather x1, waiting for transfers between devices, per_device(): cot_all = lax.all_gather(cotangent, 'expert', axis=0, tiled=True)  76.9 us
    pallas_call x4, Pallas kernels, input_weight_parts(): pl.pallas_call(weight_kernel, name='input_weight_parts', out_shape=jax.Sh...  59 us
    reduce_scatter x1, waiting for transfers between devices, per_device(): lax.psum_scatter(jnp.dot(attended, out_w, preferred_element_type=jnp.floa...  44 us
    psum x1, blocking collectives, per_device(): lax.psum((norm_mid_part, router_part), ('expert', 'tensor'))  40.2 us
    all_gather x1, waiting for transfers between devices, per_device(): gathered = lax.all_gather(normed_low, 'tensor', axis=0, tiled=True)  35.3 us
    all_gather x1, waiting for transfers between devices, per_device(): branch_all = lax.all_gather(branch_low, 'tensor', axis=0, tiled=True)  34.6 us
  transfers between devices with their start and end apart: 14, of which 4 were waited for; matrix products, arithmetic and copies ran while one was open for 11% of the time, Pallas kernels for 20%

profile of v2, /device:TPU:0, one launch (start us, length us, event | category | flops | bytes accessed | tf_op | source)
XLA Modules:
  0.0 1025.1 jit_solution(2992059458135813416)
XLA Ops:
  10.3 2.5 fusion.42
  14.9 35.3 %all-gather.4.cloned.1.call-done = bf16[1024,2048]{1,0:T(8,128)(2,1)} async-done(((bf16[256,2048]{1,0:T(8,128)(2,1)}), bf16[1024,2048]{1,0:T(8,128)(2,1)}) %all-gather.4.cloned.1.call-update) | async-done | bytes 4194320 | tf_op jit(solution)/shard_map/all_gather | solution.py:816
  50.2 6.6 multiply_reduce_fusion.8
  56.7 3.0 copy.91
  59.8 5.9 multiply_reduce_fusion.7
  65.7 2.9 copy.94
  68.7 3.5 multiply_multiply_fusion
  72.3 2.8 subtract_convert_fusion
  82.6 15.9 %while.27 = (s32[]{:T(128)}, bf16[2,512,4,128]{3,2,1,0:T(4,128)(2,1)}, f32[2,4,512]{2,1,0:T(4,128)S(1)}, bf16[2,512,4,128]{3,1,2,0:T(8,128)(2,1)}, bf16[1024,4,1...) while((s32[]{:T(128)}, bf16[2,512,4,128]{3,2,1,0:T(4,128)(2,1)}, ...), condition=%wide.region_6.7_spmd, body=%wide.region_3.6_spmd.sunk | while | flops 1092876288 | bytes 33621100 | solution.py:849
  98.5 6.3 convolution_convert_fusion.1
  105.5 44.0 %reduce-scatter.5.cloned.1.call-done = bf16[256,2048]{1,0:T(8,128)(2,1)} async-done(((bf16[1024,2048]{1,0:T(8,128)(2,1)}), bf16[256,2048]{1,0:T(8,128)(2,1)}) %reduce-scatter.5.cloned.1.call-update) | async-done | bytes 1048592 | tf_op jit(solution)/shard_map/reduce_scatter | solution.py:851
  155.3 76.9 %all-gather.6.cloned.1.call-done.right = bf16[2048,2048]{1,0:T(8,128)(2,1)} async-done(((bf16[256,2048]{1,0:T(8,128)(2,1)}), bf16[2048,2048]{1,0:T(8,128)(2,1)}) %all-gather.6.cloned.1.call-update) | async-done | bytes 8388624 | tf_op jit(solution)/shard_map/all_gather | solution.py:812
  232.2 14.0 %fusion.33 = bf16[2048,1024]{0,1:T(8,128)(2,1)} fusion(bf16[2048,2048]{1,0:T(8,128)(2,1)} %all-gather.6.cloned.1.call-done.right, bf16[2,1024,2048]{2,1,0:T(8,128)(2,1)} %param.33), kind=kOutput, calls=%fused_computation.69 | convolution fusion | flops 8592031744 | bytes 16777216 | tf_op jit(solution)/shard_map/dot_general | solution.py:875
  246.2 12.0 %fusion.36 = bf16[2048,1024]{0,1:T(8,128)(2,1)} fusion(bf16[2048,2048]{1,0:T(8,128)(2,1)S(1)} %copy-done.68, bf16[2,1024,2048]{2,1,0:T(8,128)(2,1)} %param.33), kind=kOutput, calls=%fused_computation.70 | convolution fusion | flops 8592031744 | bytes 16777216 | tf_op jit(solution)/shard_map/dot_general | solution.py:875
  258.2 8.4 pad_maximum_fusion
  266.6 12.3 %copy.100 = bf16[2048,2048]{1,0:T(8,128)(2,1)} copy(bf16[2048,2048]{0,1:T(8,128)(2,1)} %pad_maximum_fusion) | data formatting | bytes 16777216 | tf_op jit(solution)/shard_map/concatenate | solution.py:873
  278.9 2.9 fusion.64
  281.8 3.0 concatenate.39.own_rows
  284.9 236.5 %expert_pass.1 = (bf16[8,256,2176]{2,1,0:T(8,128)(2,1)}, bf16[8,256,2048]{2,1,0:T(8,128)(2,1)}, bf16[8,256,2048]{2,1,0:T(8,128)(2,1)}, bf16[8,256,2048]{2,1,0:T(8,128)(2,1)}, f32[256,2176]{1,0:T(8,128)}) custom-call(bf16[256,2176]{1,0:T(8,128)(2,1)} %concatenate.39.own_rows, bf16[8,256,2048]{2,1,0:T(8,128)(2,1)} %bitcast.234, ...), custom_call_target="tpu_custom_call" | custom-call | flops 68719476736 | bytes 67108864 | tf_op jit(solution)/shard_map/expert_pass/pallas_call | solution.py:455
  522.8 5.5 multiply_reduce_fusion.2
  531.9 34.6 %all-gather.8.cloned.1.call-done = bf16[1024,2048]{1,0:T(8,128)(2,1)} async-done(((bf16[256,2048]{1,0:T(8,128)(2,1)}), bf16[1024,2048]{1,0:T(8,128)(2,1)}) %all-gather.8.cloned.1.call-update) | async-done | bytes 4194320 | tf_op jit(solution)/shard_map/all_gather | solution.py:933
  566.4 6.2 convolution_convert_fusion.6
  572.6 2.5 reshape.332
  575.2 40.7 %while.28 = (s32[]{:T(128)}, f32[1024,4,128]{0,2,1:T(8,128)}, f32[1024,4,128]{0,2,1:T(8,128)}, f32[2,512,4,128]{3,1,0,2:T(8,128)}, bf16[2,512,4,128]{3,1,2,0:T(8...) while((s32[]{:T(128)}, f32[1024,4,128]{0,2,1:T(8,128)}, ...), condition=%wide.region_20.21_spmd.clone, body=%wide.region_18.20_spmd.clone.sunk | while | flops 2712401920 | bytes 175171440 | solution.py:971
  575.2 2.4 fusion.144
  577.9 2.6 multiply_reduce_fusion.13
  581.1 3.3 multiply_convert_fusion.2
  584.4 4.8 bitcast_add_fusion.7
  591.5 3.1 bitcast_add_fusion.8
  597.3 2.6 multiply_reduce_fusion.13
  600.5 3.3 multiply_convert_fusion.2
  603.8 5.5 bitcast_add_fusion.7
  611.6 4.3 bitcast_add_fusion.8
  615.8 3.0 copy.109
  618.8 6.8 multiply_add_fusion
  628.0 2.9 copy.111
  631.0 5.2 multiply_reduce_fusion.4
  636.2 3.0 copy.106
  639.2 2.9 convert_element_type.197
  642.1 2.5 fusion.61
  651.2 6.4 add_convert_fusion
  657.7 6.2 convolution_convert_fusion.5
  664.0 25.2 %convolution_convert_fusion = bf16[2048,2048]{1,0:T(8,128)(2,1)} fusion(bf16[2048,2048]{1,0:T(8,128)(2,1)} %bitcast.247, bf16[2048,2048]{1,0:T(8,128)(2,1)} %bitcast.242), kind=kOutput, calls=%fused_computation.40 | convolution fusion | flops 17184063488 | bytes 25165824 | tf_op jit(solution)/shard_map/dot_general | solution.py:897
  689.3 15.0 %output_weight_parts.3 = bf16[2,2,256,2048]{3,2,1,0:T(8,128)(2,1)} custom-call(s32[2]{0:T(128)S(1)} %pad_add_fusion.1.order, bf16[2048,2048]{1,0:T(8,128)(2,1)} %bitcast.248, bf16[2048,2048]{1,0:T(8,128)(2,1)} %all-gather.6.cloned.1.call-done.right), custom_call_target="tpu_custom_call" | custom-call | flops 8589934592 | bytes 16777216 | tf_op jit(solution)/shard_map/output_weight_parts/pallas_call | solution.py:754
  704.5 15.0 %input_weight_parts.7 = bf16[2,2,2048,256]{3,2,1,0:T(8,128)(2,1)} custom-call(s32[2]{0:T(128)S(1)} %pad_add_fusion.1.order, bf16[2048,2176]{1,0:T(8,128)(2,1)} %bitcast.243, bf16[2048,2048]{1,0:T(8,128)(2,1)} %bitcast.252), custom_call_target="tpu_custom_call" | custom-call | flops 8589934592 | bytes 16777216 | tf_op jit(solution)/shard_map/input_weight_parts/pallas_call | solution.py:727
  719.8 15.0 %input_weight_parts.5 = bf16[2,2,2048,256]{3,2,1,0:T(8,128)(2,1)} custom-call(s32[2]{0:T(128)S(1)} %pad_add_fusion.1.order, bf16[2048,2176]{1,0:T(8,128)(2,1)} %bitcast.244, bf16[2048,2048]{1,0:T(8,128)(2,1)} %bitcast.250), custom_call_target="tpu_custom_call" | custom-call | flops 8589934592 | bytes 16777216 | tf_op jit(solution)/shard_map/input_weight_parts/pallas_call | solution.py:727
  735.1 3.5 fusion.62
  738.6 40.2 %psum.14 = f32[2048]{0:T(1024)} all-reduce(f32[2048]{0:T(1024)S(1)} %copy-done.52), channel_id=1, replica_groups=mesh['expert'=8,'tensor'=4] {'expert','tensor'}, use_global_device_ids=true, to_apply=%region_32.33 | all-reduce | flops 2048 | bytes 16384 | tf_op jit(solution)/shard_map/psum | solution.py:1030
  778.9 14.0 %input_weight_parts.6 = bf16[2,2,2048,256]{3,2,1,0:T(8,128)(2,1)S(1)} custom-call(s32[2]{0:T(128)S(1)} %pad_add_fusion.order, bf16[2048,2176]{1,0:T(8,128)(2,1)} %bitcast.245, bf16[2048,2048]{1,0:T(8,128)(2,1)} %bitcast.253), custom_call_target="tpu_custom_call" | custom-call | flops 8589934592 | bytes 16777216 | tf_op jit(solution)/shard_map/input_weight_parts/pallas_call | solution.py:727
  792.9 14.9 %input_weight_parts.4 = bf16[2,2,2048,256]{3,2,1,0:T(8,128)(2,1)S(1)} custom-call(s32[2]{0:T(128)S(1)} %pad_add_fusion.order, bf16[2048,2176]{1,0:T(8,128)(2,1)} %bitcast.246, bf16[2048,2048]{1,0:T(8,128)(2,1)} %bitcast.251), custom_call_target="tpu_custom_call" | custom-call | flops 8589934592 | bytes 16777216 | tf_op jit(solution)/shard_map/input_weight_parts/pallas_call | solution.py:727
  807.8 15.0 %output_weight_parts.2 = bf16[2,2,256,2048]{3,2,1,0:T(8,128)(2,1)S(1)} custom-call(s32[2]{0:T(128)S(1)} %pad_add_fusion.order, bf16[2048,2048]{1,0:T(8,128)(2,1)} %bitcast.249, bf16[2048,2048]{1,0:T(8,128)(2,1)} %all-gather.6.cloned.1.call-done.right), custom_call_target="tpu_custom_call" | custom-call | flops 8589934592 | bytes 16777216 | tf_op jit(solution)/shard_map/output_weight_parts/pallas_call | solution.py:754
  822.9 5.4 fusion.53
  828.3 2.6 collective-permute-start.5
  830.9 3.4 fusion.52
  834.4 3.7 fusion.51
  847.0 11.3 %pad_maximum_fusion.1 = bf16[2048,1536]{0,1:T(8,128)(2,1)} fusion(bf16[2048,512]{0,1:T(8,128)(2,1)S(1)} %convolution_convert_fusion.2, bf16[2048,512]{0,1:T(8,128)(2,1)S(1)} %convolution_convert_fusion.3, bf16[2048,512]{0,1:T(8,128)(2,1)S(1)} %convolution_convert_fusion.4), kind=kLoop, calls=%fused_computation.41 | loop fusion | flops 18874368 | bytes 12582912 | tf_op jit(solution)/shard_map/concatenate | solution.py:1023
  858.2 8.7 copy.113
  866.9 2.9 copy-done.1
  869.9 97.3 %scatter_parts.1 = f32[256,1536]{1,0:T(8,128)S(1)} custom-call(bf16[8,256,1536]{2,1,0:T(8,128)(2,1)S(1)} %bitcast.232), custom_call_target="tpu_custom_call" | custom-call | flops 3145728 | bytes 314572800 | tf_op jit(solution)/shard_map/scatter_parts/pallas_call | solution.py:637
  968.4 5.6 bitcast_add_fusion.2
  974.0 5.2 bitcast_add_fusion.3
  979.2 5.0 bitcast_add_fusion.4
  988.6 18.3 %sum_everywhere.1 = f32[6,24,128]{2,1,0:T(8,128)} custom-call(f32[24,128]{1,0:T(8,128)} %maximum_bitcast_fusion.own), custom_call_target="tpu_custom_call" | custom-call | flops 15360 | bytes 41943040 | tf_op jit(solution)/shard_map/sum_everywhere/pallas_call | solution.py:696
  1009.5 6.4 fusion.46
  (269 shorter events, 75.6 us)
Async XLA Ops:
  8.0 51.8 %copy-start = (bf16[2048,512]{1,0:T(8,128)(2,1)S(1)}, bf16[2048,512]{1,0:T(8,128)(2,1)}, u32[]{:S(2)}) copy-start(bf16[2048,512]{1,0:T(8,128)(2,1)} %param.24) | copy-start | bytes 6291460
  8.0 42.2 %all-gather.4.cloned.1.call-start = ((), (), s32[]{:S(2)}) async-start(), calls=%async_computation.4 | async-start | bytes 5242880 | tf_op jit(solution)/shard_map/all_gather | solution.py:816
  12.8 136.7 %reduce-scatter.5.cloned.1.call-start = ((), (), s32[]{:S(2)}) async-start(), calls=%async_computation.5 | async-start | bytes 5242880 | tf_op jit(solution)/shard_map/reduce_scatter | solution.py:851
  14.9 57.4 %copy-start.27 = (f32[1024,64]{1,0:T(8,128)}, f32[1024,64]{1,0:T(8,128)S(1)}, u32[]{:S(2)}) copy-start(f32[1024,64]{1,0:T(8,128)S(1)} %get-tuple-element.266) | copy-start | bytes 786436
  14.9 57.4 %copy-start.29 = (f32[1024,64]{1,0:T(8,128)}, f32[1024,64]{1,0:T(8,128)S(1)}, u32[]{:S(2)}) copy-start(f32[1024,64]{1,0:T(8,128)S(1)} %get-tuple-element.267) | copy-start | bytes 786436
  65.7 3.0 copy-start.64
  65.7 3.0 copy-start.66
  68.6 3.6 copy-start.39
  68.7 3.6 copy-start.37
  72.3 4.4 copy-start.69
  98.5 6.3 copy-start.47
  104.8 46.8 %copy-start.41 = (f32[2048]{0:T(1024)S(1)}, f32[2048]{0:T(1024)}, u32[]{:S(2)}) copy-start(f32[2048]{0:T(1024)} %param.29) | copy-start | bytes 24580
  104.9 46.8 %copy-start.43 = (f32[2048,16]{0,1:T(8,128)S(1)}, f32[2048,16]{0,1:T(8,128)}, u32[]{:S(2)}) copy-start(f32[2048,16]{0,1:T(8,128)} %param.30) | copy-start | bytes 393220
  104.9 127.3 %all-gather.6.cloned.1.call-start = ((), (), s32[]{:S(2)}) async-start(), calls=%async_computation.6 | async-start | bytes 9437184 | tf_op jit(solution)/shard_map/all_gather | solution.py:812
  104.9 48.8 %copy-start.45 = (s32[256,8]{0,1:T(8,128)S(1)}, s32[256,8]{0,1:T(8,128)}, u32[]{:S(2)}) copy-start(s32[256,8]{0,1:T(8,128)} %param.21) | copy-start | bytes 24580
  105.5 461.0 %all-gather.8.cloned.1.call-start = ((), (), s32[]{:S(2)}) async-start(), calls=%async_computation.8 | async-start | bytes 5242880 | tf_op jit(solution)/shard_map/all_gather | solution.py:933
  232.2 14.0 %copy-start.68 = (bf16[2048,2048]{1,0:T(8,128)(2,1)S(1)}, bf16[2048,2048]{1,0:T(8,128)(2,1)}, u32[]{:S(2)}) copy-start(bf16[2048,2048]{1,0:T(8,128)(2,1)} %all-gather.6.cloned.1.call-done.right) | copy-start | bytes 25165828
  284.9 237.7 %copy-start.46 = (s32[256,8]{0,1:T(8,128)S(1)}, s32[256,8]{0,1:T(8,128)}, u32[]{:S(2)}) copy-start(s32[256,8]{0,1:T(8,128)} %param.21) | copy-start | bytes 24580
  284.9 237.8 %copy-start.57 = (f32[256]{0:T(256)S(1)}, f32[256]{0:T(256)}, u32[]{:S(2)}) copy-start(f32[256]{0:T(256)} %copy-done.56) | copy-start | bytes 3076
  284.9 237.8 %copy-start.61 = (f32[256]{0:T(256)S(1)}, f32[256]{0:T(256)}, u32[]{:S(2)}) copy-start(f32[256]{0:T(256)} %copy-done.60) | copy-start | bytes 3076
  284.9 237.9 %copy-start.44 = (f32[2048,16]{0,1:T(8,128)S(1)}, f32[2048,16]{0,1:T(8,128)}, u32[]{:S(2)}) copy-start(f32[2048,16]{0,1:T(8,128)} %param.30) | copy-start | bytes 393220
  284.9 237.9 %copy-start.54 = (f32[256]{0:T(256)S(1)}, f32[256]{0:T(256)}, u32[]{:S(2)}) copy-start(f32[256]{0:T(256)} %copy-done.53) | copy-start | bytes 3076
  522.7 5.6 copy-start.50
  522.8 6.9 copy-start.14
  522.8 6.9 copy-start.19
  522.8 6.8 copy-start.23
  528.3 3.4 copy-start.62
  531.7 452.5 %reduce-scatter.9.cloned.1.call-start = ((), (), s32[]{:S(2)}) async-start(), calls=%async_computation.9 | async-start | bytes 5242880 | tf_op jit(solution)/shard_map/reduce_scatter | solution.py:1005
  577.6 3.5 copy-start.8
  584.4 4.8 copy-start.10
  584.4 7.1 copy-start.9
  597.0 3.5 copy-start.8
  603.8 5.5 copy-start.10
  603.8 7.7 copy-start.9
  615.8 3.0 copy-start.28
  615.8 3.0 copy-start.30
  618.8 6.8 copy-start.21
  648.1 3.1 copy-start.35
  657.6 329.1 %reduce-scatter.11.cloned.1.call-start = ((), (), s32[]{:S(2)}) async-start(), calls=%async_computation.10 | async-start | bytes 2359296 | tf_op jit(solution)/shard_map/reduce_scatter | solution.py:1018
  663.9 345.5 %reduce-scatter.7.cloned.1.call-start = ((), (), s32[]{:S(2)}) async-start(), calls=%async_computation.7 | async-start | bytes 9437184 | tf_op jit(solution)/shard_map/reduce_scatter | solution.py:900
  689.2 326.7 %all-reduce.2.cloned.1.call-start = ((), (), s32[]{:S(2)}) async-start(), calls=%async_computation.11 | async-start | bytes 262144 | tf_op jit(solution)/shard_map/psum | solution.py:1030
  704.3 118.6 %collective-permute-start.4 = (bf16[2,2,256,2048]{3,2,1,0:T(8,128)(2,1)}, bf16[2,2,256,2048]{3,2,1,0:T(8,128)(2,1)}, u32[]{:S(2)}, u32[]{:S(2)}) collective-permute-start(bf16[2,2,256,2048]{3,2,1,0:T(8,128)(2,1)} %output_weight_parts.3), channel_id=1, source_target_pairs={{0,1},{1,0},{2,3},{3,2},{4,5},{5,4},{6,7},{7,6},{8,9},{9,8},{10,11... | collective-permute-start | bytes 12582920 | tf_op jit(solution)/shard_map/ppermute | solution.py:779
  719.5 111.4 %collective-permute-start.2 = (bf16[2,2,2048,256]{3,2,1,0:T(8,128)(2,1)}, bf16[2,2,2048,256]{3,2,1,0:T(8,128)(2,1)}, u32[]{:S(2)}, u32[]{:S(2)}) collective-permute-start(bf16[2,2,2048,256]{3,2,1,0:T(8,128)(2,1)} %input_weight_parts.7), channel_id=1, source_target_pairs={{0,1},{1,0},{2,3},{3,2},{4,5},{5,4},{6,7},{7,6},{8,9},{9,8},{10,11... | collective-permute-start | bytes 12582920 | tf_op jit(solution)/shard_map/ppermute | solution.py:779
  719.8 15.3 %copy-start.15 = (bf16[256,2048]{1,0:T(8,128)(2,1)S(1)}, bf16[256,2048]{1,0:T(8,128)(2,1)}, u32[]{:S(2)}) copy-start(bf16[256,2048]{1,0:T(8,128)(2,1)} %param.19) | copy-start | bytes 3145732
  719.8 15.3 %copy-start.42 = (f32[2048]{0:T(1024)S(1)}, f32[2048]{0:T(1024)}, u32[]{:S(2)}) copy-start(f32[2048]{0:T(1024)} %param.29) | copy-start | bytes 24580
  719.8 15.3 %copy-start.51 = (f32[256,16]{0,1:T(8,128)S(1)}, f32[256,16]{0,1:T(8,128)}, u32[]{:S(2)}) copy-start(f32[256,16]{0,1:T(8,128)} %copy-done.50) | copy-start | bytes 49156
  719.8 15.3 %copy-start.55 = (f32[256]{0:T(256)S(1)}, f32[256]{0:T(256)}, u32[]{:S(2)}) copy-start(f32[256]{0:T(256)} %copy-done.53) | copy-start | bytes 3076
  734.8 3.8 copy-start.52
  734.9 99.5 %collective-permute-start = (bf16[2,2,2048,256]{3,2,1,0:T(8,128)(2,1)}, bf16[2,2,2048,256]{3,2,1,0:T(8,128)(2,1)}, u32[]{:S(2)}, u32[]{:S(2)}) collective-permute-start(bf16[2,2,2048,256]{3,2,1,0:T(8,128)(2,1)} %input_weight_parts.5), channel_id=1, source_target_pairs={{0,1},{1,0},{2,3},{3,2},{4,5},{5,4},{6,7},{7,6},{8,9},{9,8},{10,11... | collective-permute-start | bytes 12582920 | tf_op jit(solution)/shard_map/ppermute | solution.py:779
  792.9 38.0 %copy-start.4 = (bf16[2,2,2048,256]{3,2,1,0:T(8,128)(2,1)}, bf16[2,2,2048,256]{3,2,1,0:T(8,128)(2,1)S(1)}, u32[]{:S(2)}) copy-start(bf16[2,2,2048,256]{3,2,1,0:T(8,128)(2,1)S(1)} %input_weight_parts.6) | copy-start | bytes 12582916
  807.8 26.6 %copy-start.2 = (bf16[2,2,2048,256]{3,2,1,0:T(8,128)(2,1)}, bf16[2,2,2048,256]{3,2,1,0:T(8,128)(2,1)S(1)}, u32[]{:S(2)}) copy-start(bf16[2,2,2048,256]{3,2,1,0:T(8,128)(2,1)S(1)} %input_weight_parts.4) | copy-start | bytes 12582916
  822.9 5.4 copy-start.6
  828.3 140.1 %collective-permute-start.5 = (bf16[2,256,2048]{2,1,0:T(8,128)(2,1)}, bf16[2,256,2048]{2,1,0:T(8,128)(2,1)}, u32[]{:S(2)}, u32[]{:S(2)}) collective-permute-start(bf16[2,256,2048]{2,1,0:T(8,128)(2,1)} %fusion.53), channel_id=1, source_target_pairs={{0,2},{1,3},{2,0},{3,1},{4,6},{5,7},{6,4},{7,5},{8,10},{9,11},{10,... | collective-permute-start | bytes 6291464 | tf_op jit(solution)/shard_map/ppermute | solution.py:782
  834.3 5.6 copy-start.34
  834.3 5.6 copy-start.70
  834.3 139.7 %collective-permute-start.3 = (bf16[2,2048,256]{2,1,0:T(8,128)(2,1)}, bf16[2,2048,256]{2,1,0:T(8,128)(2,1)}, u32[]{:S(2)}, u32[]{:S(2)}) collective-permute-start(bf16[2,2048,256]{2,1,0:T(8,128)(2,1)} %fusion.52), channel_id=1, source_target_pairs={{0,2},{1,3},{2,0},{3,1},{4,6},{5,7},{6,4},{7,5},{8,10},{9,11},{10,... | collective-permute-start | bytes 6291464 | tf_op jit(solution)/shard_map/ppermute | solution.py:782
  838.1 4.2 copy-start.36
  838.1 141.1 %collective-permute-start.1 = (bf16[2,2048,256]{2,1,0:T(8,128)(2,1)}, bf16[2,2048,256]{2,1,0:T(8,128)(2,1)}, u32[]{:S(2)}, u32[]{:S(2)}) collective-permute-start(bf16[2,2048,256]{2,1,0:T(8,128)(2,1)} %fusion.51), channel_id=1, source_target_pairs={{0,2},{1,3},{2,0},{3,1},{4,6},{5,7},{6,4},{7,5},{8,10},{9,11},{10,... | collective-permute-start | bytes 6291464 | tf_op jit(solution)/shard_map/ppermute | solution.py:782
  869.9 98.5 %copy-start.7 = (bf16[2,2,256,2048]{3,2,1,0:T(8,128)(2,1)S(1)}, bf16[2,2,256,2048]{3,2,1,0:T(8,128)(2,1)}, u32[]{:S(2)}) copy-start(bf16[2,2,256,2048]{3,2,1,0:T(8,128)(2,1)} %copy-done.6) | copy-start | bytes 12582916
  968.3 5.6 copy-start.5
  974.0 5.2 copy-start.3
  979.2 5.1 copy-start.49
  979.2 5.1 copy-start.59
  984.2 25.2 %copy-start.63 = (f32[256]{0:T(256)S(1)}, f32[256]{0:T(256)}, u32[]{:S(2)}) copy-start(f32[256]{0:T(256)} %copy-done.62) | copy-start | bytes 3076
  (30 other events, 65.1 us)
Sparse Core Ops, SparseCore 0:
  13.0 37.1 all-gather.3
  105.0 44.5 reduce-scatter.4
  531.9 34.5 all-gather.7
  657.8 44.4 reduce-scatter.8
  706.2 68.4 reduce-scatter.10
  778.3 187.3 reduce-scatter.6
Sparse Core Ops, SparseCore 1:
  107.7 124.5 all-gather.5
  738.7 208.8 all-reduce.1

commit v3 on v2

--- a/solution.py
+++ b/solution.py
@@ -81,27 +81,32 @@
 def expert_kernel(
     experts_all,
     own_rows,
-    raw_all,
+    cot_all,
     gate_hbm,
     up_hbm,
+    down_hbm,
     rows_all,
     hidden_all,
     gate_all,
     up_all,
+    y_all,
     total,
     gate_v,
     up_v,
+    down_v,
     rows_v,
-    raw_v,
+    cot_v,
     hidden_v,
     gate_b,
     up_b,
+    y_v,
+    stage,
     parts,
     side_in,
     line_in,
     weight_sem,
     own_sem,
-    raw_sem,
+    cot_sem,
     out_sem,
     rows_sem,
     gather_recv,
@@ -136,6 +141,7 @@
     weight_copies = [
         pltpu.make_async_copy(gate_hbm, gate_v, weight_sem.at[0]),
         pltpu.make_async_copy(up_hbm, up_v, weight_sem.at[1]),
+        pltpu.make_async_copy(down_hbm, down_v, weight_sem.at[2]),
     ]
     own_copy = pltpu.make_async_copy(own_rows, rows_v.at[position], own_sem)
     own_copy.start()
@@ -265,8 +271,11 @@
         side = pick(step, [0, 0, 1, 0, 1, 0, 1, 1])
         return k, side, slot_z(k) * 2 + jnp.where(side == 1, 1 - x, x)
 
-    def raw_copy(step, slot):
-        return pltpu.make_async_copy(raw_all.at[block_of(step)[2]], raw_v.at[slot], raw_sem.at[slot])
+    def cot_copy(step):
+        return pltpu.make_async_copy(cot_all.at[block_of(step)[2]], cot_v, cot_sem)
+
+    def y_copy(block):
+        return pltpu.make_async_copy(y_v, y_all.at[block], out_sem.at[3])
 
     def out_copies(block):
         return [
@@ -275,7 +284,7 @@
             pltpu.make_async_copy(up_b, up_all.at[block], out_sem.at[2]),
         ]
 
-    raw_copy(0, 0).start()
+    cot_copy(0).start()
     own_copy.wait()
     pltpu.make_async_copy(rows_v.at[position], rows_all.at[position], rows_sem.at[position]).start()
     for copy in weight_copies:
@@ -283,7 +292,6 @@
 
     def one_step(step, carry):
         k, side, block = block_of(step)
-        slot = step % 2
 
         @pl.when(step == 1)
         def _():
@@ -319,16 +327,12 @@
 
             lax.fori_loop(0, chunks, one, 0)
 
-        @pl.when(step < 7)
-        def _():
-            raw_copy(step + 1, 1 - slot).start()
-
         @pl.when(step > 0)
         def _():
             for copy in out_copies(block):
                 copy.wait()
 
-        raw_copy(step, slot).wait()
+        cot_copy(step).wait()
         rows_low = rows_v[block, :, :width]
         extra = rows_v[block, :, width:].astype(jnp.float32)
         lane = lax.broadcasted_iota(jnp.int32, extra.shape, 1)
@@ -344,7 +348,12 @@
                 gate_pre = jnp.dot(rows_low, gate_v[e, :, columns], preferred_element_type=jnp.float32)
                 up_pre = jnp.dot(rows_low, up_v[e, :, columns], preferred_element_type=jnp.float32)
                 target = pl.ds(e * hidden + f * 512, 512)
-                raw = raw_v[slot, :, target].astype(jnp.float32)
+                raw = lax.dot_general(
+                    cot_v[...],
+                    down_v[e, columns, :],
+                    contract_last,
+                    preferred_element_type=jnp.float32,
+                )
                 sig = jax.nn.sigmoid(gate_pre)
                 act = gate_pre * sig
                 hid = act * up_pre
@@ -356,6 +365,11 @@
             grad_high = gate_grad.astype(jnp.bfloat16).astype(jnp.float32)
             ext = jnp.where(high, grad_high, ext)
             ext = jnp.where(low, gate_grad - grad_high, ext)
+
+        @pl.when(step < 7)
+        def _():
+            cot_copy(step + 1).start()
+
         place = side * 4 + k
         parts[place, :, width:] = ext.astype(jnp.bfloat16)
         for copy in out_copies(block):
@@ -378,6 +392,21 @@
             for c in range(chunks):
                 side_copy(k, c).start()
 
+        @pl.when(step > 0)
+        def _():
+            y_copy(block).wait()
+
+        for d in range(width // 1024):
+            span = pl.ds(d * 1024, 1024)
+            summed = jnp.zeros((rows, 1024), jnp.float32)
+            for e in range(experts_local):
+                summed = summed + jnp.dot(
+                    hidden_v[:, pl.ds(e * hidden, hidden)],
+                    down_v[e, :, span],
+                    preferred_element_type=jnp.float32,
+                )
+            y_v[:, span] = summed.astype(jnp.bfloat16)
+        y_copy(block).start()
         return carry
 
     lax.fori_loop(0, 8, one_step, 0)
@@ -402,18 +431,21 @@
     def finish(c, carry):
         area = pl.ds(c * chunk, chunk)
         side_copy(0, c).wait_recv()
-        total[area] = parts[0, area].astype(jnp.float32) + side_in[0, area].astype(jnp.float32)
+        stage[...] = parts[0, area].astype(jnp.float32) + side_in[0, area].astype(jnp.float32)
 
         @pl.when(z < 3)
         def _():
             line_wait(z, c)
-            total[area] += line_in[z, area].astype(jnp.float32)
+            stage[...] += line_in[z, area].astype(jnp.float32)
 
         @pl.when(z > 0)
         def _():
             line_wait(z + 1, c)
-            total[area] += line_in[z + 1, area].astype(jnp.float32)
-
+            stage[...] += line_in[z + 1, area].astype(jnp.float32)
+
+        result = pltpu.make_async_copy(stage, total.at[area], own_sem)
+        result.start()
+        result.wait()
         for k in range(4):
             side_copy(k, c).wait_send()
         for k in range(1, 4):
@@ -441,11 +473,12 @@
 
     for copy in out_copies(position):
         copy.wait()
+    y_copy(position).wait()
     for block in range(8):
         pltpu.make_async_copy(rows_v.at[block], rows_all.at[block], rows_sem.at[block]).wait()
 
 
-def expert_pass(own_rows, raw_all, gate_w, up_w, experts_all, collective):
+def expert_pass(own_rows, cot_all, gate_w, up_w, down_w, experts_all, collective):
     rows, wide = own_rows.shape
     experts_local, width, hidden = gate_w.shape
     inner = experts_local * hidden
@@ -460,25 +493,29 @@
             jax.ShapeDtypeStruct((8, rows, inner), low),
             jax.ShapeDtypeStruct((8, rows, inner), low),
             jax.ShapeDtypeStruct((8, rows, inner), low),
+            jax.ShapeDtypeStruct((8, rows, width), low),
             jax.ShapeDtypeStruct((rows, wide), jnp.float32),
         ),
-        in_specs=[any_space] * 4,
-        out_specs=(any_space,) * 4 + (pl.BlockSpec(memory_space=pltpu.VMEM),),
+        in_specs=[any_space] * 5,
+        out_specs=(any_space,) * 6,
         scratch_shapes=[
             pltpu.VMEM((experts_local, width, hidden), low),
             pltpu.VMEM((experts_local, width, hidden), low),
+            pltpu.VMEM((experts_local, hidden, width), low),
             pltpu.VMEM((8, rows, wide), low),
-            pltpu.VMEM((2, rows, inner), low),
+            pltpu.VMEM((rows, width), low),
             pltpu.VMEM((rows, inner), low),
             pltpu.VMEM((rows, inner), low),
             pltpu.VMEM((rows, inner), low),
+            pltpu.VMEM((rows, width), low),
+            pltpu.VMEM((rows // chunks, wide), jnp.float32),
             pltpu.VMEM((8, rows, wide), low),
             pltpu.VMEM((4, rows, wide), low),
             pltpu.VMEM((5, rows, wide), low),
-            dma((2,)),
+            dma((3,)),
             dma,
-            dma((2,)),
-            dma((3,)),
+            dma,
+            dma((4,)),
             dma((8,)),
             dma((8,)),
             dma((9,)),
@@ -491,19 +528,398 @@
             collective_id=collective, has_side_effects=True, vmem_limit_bytes=60 << 20
         ),
         cost_estimate=pl.CostEstimate(
-            flops=2 * 4 * 8 * rows * width * inner, bytes_accessed=64 << 20, transcendentals=8 * rows * inner
+            flops=2 * 6 * 8 * rows * width * inner, bytes_accessed=64 << 20, transcendentals=8 * rows * inner
         ),
-    )(own_rows, raw_all, gate_w, up_w)
-
-
-def scatter_kernel(
-    parts, total, own, side_in, line_in, own_sem, side_recv, side_send, line_recv, line_send
-):
+    )(own_rows, cot_all, gate_w, up_w, down_w)
+
+
+def line_gather(source, target, recv, send):
     position = lax.axis_index("expert")
     peer = lax.axis_index("tensor")
     z = position // 2
     x = position % 2
-    chunk = own.shape[1] // chunks
+    middle = (z == 1) | (z == 2)
+    slots = [z, pick(z, [1, 0, 3, 2]), pick(z, [2, 2, 1, 1]), pick(z, [3, 3, 0, 0])]
+
+    def copy(block_source, block, index, zz, xx):
+        return pltpu.make_async_remote_copy(
+            src_ref=block_source,
+            dst_ref=target.at[block],
+            send_sem=send.at[index],
+            recv_sem=recv.at[block],
+            device_id=(zz * 2 + xx, peer),
+            device_id_type=pl.DeviceIdType.MESH,
+        )
+
+    def own_up():
+        return copy(source, position, 1, z + 1, x)
+
+    def own_down():
+        return copy(source, position, 2, z - 1, x)
+
+    def own_side():
+        return copy(source, position, 0, z, 1 - x)
+
+    def side(k):
+        block = slots[k] * 2 + x
+        return copy(target.at[block], block, 2 + k, z, 1 - x)
+
+    def line(k):
+        block = slots[k] * 2 + x
+        onward = jnp.where(slots[k] < z, z + 1, z - 1)
+        return copy(target.at[block], block, 5 + k, jnp.clip(onward, 0, 3), x)
+
+    def start():
+        own_side().start()
+
+        @pl.when(z < 3)
+        def _():
+            own_up().start()
+
+        @pl.when(z > 0)
+        def _():
+            own_down().start()
+
+    def wait_block(block):
+        copy(source, block, 0, z, 1 - x).wait_recv()
+
+    def arrive(k):
+        wait_block(slots[k] * 2 + x)
+        side(k).start()
+
+        @pl.when(middle)
+        def _():
+            line(k).start()
+
+    def arrive_side(k):
+        wait_block(slots[k] * 2 + 1 - x)
+
+    def drain():
+        own_side().wait_send()
+
+        @pl.when(z < 3)
+        def _():
+            own_up().wait_send()
+
+        @pl.when(z > 0)
+        def _():
+            own_down().wait_send()
+
+        for k in range(1, 4):
+            side(k).wait_send()
+
+            @pl.when(middle)
+            def _(k=k):
+                line(k).wait_send()
+
+    return middle, start, arrive, arrive_side, drain
+
+
+def attention_kernel(
+    own,
+    cot,
+    query_w,
+    key_w,
+    value_w,
+    out_w,
+    query_gain,
+    key_gain,
+    cosine,
+    sine,
+    gathered,
+    query_pre,
+    key_pre,
+    query_low,
+    key_low,
+    value_low,
+    attended,
+    log_sums,
+    attn_sum,
+    cot_all,
+    rows_v,
+    weights_v,
+    out_v,
+    pre_v,
+    low_v,
+    mixed_v,
+    log_v,
+    parts,
+    own_part,
+    core_in,
+    line_in,
+    load_sem,
+    store_sem,
+    rows_recv,
+    rows_send,
+    part_recv,
+    part_send,
+    cot_recv,
+    cot_send,
+    cot_sem,
+):
+    position = lax.axis_index("expert")
+    t = lax.axis_index("tensor")
+    z = position // 2
+    x = position % 2
+    y = t // 2
+    c = t % 2
+    near = y * 2 + 1 - c
+    across = (1 - y) * 2 + c
+    opposite = (1 - y) * 2 + 1 - c
+    rows = own.shape[0]
+    heads = low_v.shape[2] // 128
+    factor = 1.0 / math.sqrt(128.0)
+    mesh_ids = pl.DeviceIdType.MESH
+    middle, gather_start, gather_arrive, gather_side, gather_drain = line_gather(
+        cot, cot_all, cot_recv, cot_send
+    )
+
+    loads = [
+        pltpu.make_async_copy(own, rows_v.at[t], load_sem.at[0]),
+        pltpu.make_async_copy(query_w, weights_v.at[0], load_sem.at[1]),
+        pltpu.make_async_copy(key_w, weights_v.at[1], load_sem.at[2]),
+        pltpu.make_async_copy(value_w, weights_v.at[2], load_sem.at[3]),
+        pltpu.make_async_copy(out_w, out_v, load_sem.at[4]),
+    ]
+    for load in loads:
+        load.start()
+    cot_copy = pltpu.make_async_copy(cot, cot_all.at[position], cot_sem)
+    cot_copy.start()
+
+    barrier = pltpu.get_barrier_semaphore()
+    for place in ((position, near), (position, across), (z * 2 + 1 - x, t)):
+        pl.semaphore_signal(barrier, inc=1, device_id=place, device_id_type=mesh_ids)
+
+    @pl.when(z < 3)
+    def _():
+        pl.semaphore_signal(barrier, inc=1, device_id=(position + 2, t), device_id_type=mesh_ids)
+
+    @pl.when(z > 0)
+    def _():
+        pl.semaphore_signal(barrier, inc=1, device_id=(position - 2, t), device_id_type=mesh_ids)
+
+    pl.semaphore_wait(barrier, 4 + middle.astype(jnp.int32))
+
+    def rows_copy(source, block, index, to):
+        return pltpu.make_async_remote_copy(
+            src_ref=source,
+            dst_ref=rows_v.at[block],
+            send_sem=rows_send.at[index - 1],
+            recv_sem=rows_recv.at[index - 1],
+            device_id=(position, to),
+            device_id_type=mesh_ids,
+        )
+
+    to_across = rows_copy(own, t, 2, across)
+    to_near = rows_copy(own, t, 1, near)
+    forward = rows_copy(rows_v.at[across], across, 3, near)
+    to_across.start()
+    to_near.start()
+    gather_start()
+    for load in loads:
+        load.wait()
+
+    def project(i, carry):
+        block = pick(i, [t, near, across, opposite])
+
+        @pl.when(i == 1)
+        def _():
+            to_near.wait_recv()
+
+        @pl.when(i == 2)
+        def _():
+            to_across.wait_recv()
+            forward.start()
+            gather_arrive(1)
+
+            @pl.when(middle)
+            def _():
+                gather_arrive(2)
+
+        @pl.when(i == 3)
+        def _():
+            forward.wait_recv()
+
+        area = pl.ds(block * rows, rows)
+        values = rows_v[block]
+        for which, gain in ((0, query_gain), (1, key_gain)):
+            pre = jnp.dot(values, weights_v[which], preferred_element_type=jnp.float32)
+            pre_v[which, area] = pre
+            for h in range(heads):
+                span = slice(h * 128, (h + 1) * 128)
+                head = pre[:, span]
+                scale = lax.rsqrt(jnp.mean(head * head, axis=-1, keepdims=True) + epsilon)
+                normed = head * scale * gain[...]
+                turned = normed * cosine[area] + pltpu.roll(normed, 64, 1) * sine[area]
+                low_v[which, area, span] = turned.astype(jnp.bfloat16)
+        low_v[2, area] = jnp.dot(
+            values, weights_v[2], preferred_element_type=jnp.float32
+        ).astype(jnp.bfloat16)
+        return carry
+
+    lax.fori_loop(0, 4, project, 0)
+    stores = [
+        pltpu.make_async_copy(rows_v, gathered, store_sem.at[0]),
+        pltpu.make_async_copy(pre_v.at[0], query_pre, store_sem.at[1]),
+        pltpu.make_async_copy(pre_v.at[1], key_pre, store_sem.at[2]),
+        pltpu.make_async_copy(low_v.at[0], query_low, store_sem.at[3]),
+        pltpu.make_async_copy(low_v.at[1], key_low, store_sem.at[4]),
+        pltpu.make_async_copy(low_v.at[2], value_low, store_sem.at[5]),
+    ]
+    for store in stores:
+        store.start()
+
+    def part_copy(source, target, index, to):
+        return pltpu.make_async_remote_copy(
+            src_ref=source,
+            dst_ref=target,
+            send_sem=part_send.at[index],
+            recv_sem=part_recv.at[index],
+            device_id=(position, to),
+            device_id_type=mesh_ids,
+        )
+
+    core_first = part_copy(parts.at[0], core_in.at[0], 0, near)
+    line_copy = part_copy(parts.at[1], line_in, 1, across)
+    core_second = part_copy(parts.at[2], core_in.at[1], 2, near)
+
+    def attend(i, carry):
+        block = pick(i, [opposite, across, near, t])
+        area = pl.ds(block * rows, rows)
+        for h in range(heads):
+            span = slice(h * 128, (h + 1) * 128)
+            scores = lax.dot_general(
+                low_v[0, area, span], low_v[1, :, span], contract_last, preferred_element_type=jnp.float32
+            )
+            highest_score = jnp.max(scores, axis=-1, keepdims=True)
+            weights = jnp.exp((scores - highest_score) * factor)
+            total = jnp.sum(weights, axis=-1, keepdims=True)
+            mixed = jnp.dot(
+                weights.astype(jnp.bfloat16), low_v[2, :, span], preferred_element_type=jnp.float32
+            )
+            mixed_v[area, span] = (mixed / total).astype(jnp.bfloat16)
+            log_v[area, h : h + 1] = highest_score * factor + jnp.log(total)
+        own_part[...] = jnp.dot(mixed_v[area], out_v[...], preferred_element_type=jnp.float32)
+
+        @pl.when(i == 0)
+        def _():
+            parts[0] = own_part[...].astype(jnp.bfloat16)
+            core_first.start()
+
+        @pl.when(i == 1)
+        def _():
+            core_first.wait_recv()
+            parts[1] = (own_part[...] + core_in[0].astype(jnp.float32)).astype(jnp.bfloat16)
+            line_copy.start()
+
+            @pl.when(middle)
+            def _():
+                gather_arrive(3)
+
+        @pl.when(i == 2)
+        def _():
+            parts[2] = own_part[...].astype(jnp.bfloat16)
+            core_second.start()
+
+            @pl.when(middle == False)
+            def _():
+                gather_arrive(2)
+
+        return carry
+
+    lax.fori_loop(0, 4, attend, 0)
+    more = [
+        pltpu.make_async_copy(mixed_v, attended, store_sem.at[6]),
+        pltpu.make_async_copy(log_v, log_sums, store_sem.at[7]),
+    ]
+    for store in more:
+        store.start()
+    core_second.wait_recv()
+    own_part[...] += core_in[1].astype(jnp.float32)
+    line_copy.wait_recv()
+    own_part[...] += line_in[...].astype(jnp.float32)
+    last = pltpu.make_async_copy(own_part, attn_sum, store_sem.at[8])
+    last.start()
+
+    @pl.when(middle == False)
+    def _():
+        gather_arrive(3)
+
+    for k in range(4):
+        gather_side(k)
+    gather_drain()
+    for copy in (to_across, to_near, forward, core_first, line_copy, core_second):
+        copy.wait_send()
+    for store in [*stores, *more, last, cot_copy]:
+        store.wait()
+
+
+def attention_forward(own, cot, weights, out_w, gains, tables, collective):
+    rows, width = own.shape
+    local = out_w.shape[0]
+    length = 4 * rows
+    any_space = pl.BlockSpec(memory_space=pl.ANY)
+    vector = pl.BlockSpec(memory_space=pltpu.VMEM)
+    low, full = jnp.bfloat16, jnp.float32
+    dma = pltpu.SemaphoreType.DMA
+    return pl.pallas_call(
+        attention_kernel,
+        name="attention_forward",
+        out_shape=(
+            jax.ShapeDtypeStruct((4, rows, width), low),
+            jax.ShapeDtypeStruct((length, local), full),
+            jax.ShapeDtypeStruct((length, local), full),
+            jax.ShapeDtypeStruct((length, local), low),
+            jax.ShapeDtypeStruct((length, local), low),
+            jax.ShapeDtypeStruct((length, local), low),
+            jax.ShapeDtypeStruct((length, local), low),
+            jax.ShapeDtypeStruct((length, 128), full),
+            jax.ShapeDtypeStruct((rows, width), full),
+            jax.ShapeDtypeStruct((8, rows, width), low),
+        ),
+        in_specs=[any_space] * 6 + [vector] * 4,
+        out_specs=(any_space,) * 10,
+        scratch_shapes=[
+            pltpu.VMEM((4, rows, width), low),
+            pltpu.VMEM((3, width, local), low),
+            pltpu.VMEM((local, width), low),
+            pltpu.VMEM((2, length, local), full),
+            pltpu.VMEM((3, length, local), low),
+            pltpu.VMEM((length, local), low),
+            pltpu.VMEM((length, 128), full),
+            pltpu.VMEM((3, rows, width), low),
+            pltpu.VMEM((rows, width), full),
+            pltpu.VMEM((2, rows, width), low),
+            pltpu.VMEM((rows, width), low),
+            dma((5,)),
+            dma((9,)),
+            dma((3,)),
+            dma((3,)),
+            dma((3,)),
+            dma((3,)),
+            dma((8,)),
+            dma((9,)),
+            dma,
+        ],
+        compiler_params=pltpu.CompilerParams(
+            collective_id=collective, has_side_effects=True, vmem_limit_bytes=60 << 20
+        ),
+        cost_estimate=pl.CostEstimate(
+            flops=8 * length * width * local, bytes_accessed=64 << 20, transcendentals=length * length * 4
+        ),
+    )(own, cot, *weights, out_w, *gains, *tables)
+
+
+def scatter_kernel(
+    count,
+    *refs,
+):
+    parts, totals = refs[:count], refs[count : 2 * count]
+    own, side_in, line_in, own_sem, side_recv, side_send, line_recv, line_send = refs[2 * count :]
+    position = lax.axis_index("expert")
+    peer = lax.axis_index("tensor")
+    z = position // 2
+    x = position % 2
     middle = (z == 1) | (z == 2)
     line_slots = [
         z,
@@ -517,10 +933,12 @@
         return (zz * 2 + xx, peer)
 
     own_copies = [
-        pltpu.make_async_copy(parts.at[line_slots[k] * 2 + x], own.at[k], own_sem.at[k]) for k in range(4)
+        pltpu.make_async_copy(parts[c].at[line_slots[k] * 2 + x], own.at[k, c], own_sem.at[k, c])
+        for k in (3, 2, 1, 0)
+        for c in range(count)
     ]
-    for k in (3, 2, 1, 0):
-        own_copies[k].start()
+    for copy in own_copies:
+        copy.start()
 
     barrier = pltpu.get_barrier_semaphore()
     pl.semaphore_signal(barrier, inc=1, device_id=device(z, 1 - x), device_id_type=mesh_ids)
@@ -536,10 +954,9 @@
     pl.semaphore_wait(barrier, 2 + middle.astype(jnp.int32))
 
     def side_copy(k, c):
-        area = pl.ds(c * chunk, chunk)
         return pltpu.make_async_remote_copy(
-            src_ref=parts.at[pick(k, line_slots) * 2 + 1 - x, area],
-            dst_ref=side_in.at[k, area],
+            src_ref=parts[c].at[pick(k, line_slots) * 2 + 1 - x],
+            dst_ref=side_in.at[k, c],
             send_sem=side_send.at[k, c],
             recv_sem=side_recv.at[k, c],
             device_id=device(z, 1 - x),
@@ -551,11 +968,10 @@
         return jnp.where(target < z, target, target + 1)
 
     def line_copy(k, c):
-        area = pl.ds(c * chunk, chunk)
         target = jnp.where(pick(k, line_slots) < z, z - 1, z + 1)
         return pltpu.make_async_remote_copy(
-            src_ref=own.at[k, area],
-            dst_ref=line_in.at[line_slot(k), area],
+            src_ref=own.at[k, c],
+            dst_ref=line_in.at[line_slot(k), c],
             send_sem=line_send.at[k - 1, c],
             recv_sem=line_recv.at[line_slot(k), c],
             device_id=device(jnp.clip(target, 0, 3), x),
@@ -563,10 +979,9 @@
         )
 
     def line_wait(slot, c):
-        area = pl.ds(c * chunk, chunk)
         pltpu.make_async_remote_copy(
-            src_ref=own.at[0, area],
-            dst_ref=line_in.at[slot, area],
+            src_ref=own.at[0, c],
+            dst_ref=line_in.at[slot, c],
             send_sem=line_send.at[0, c],
             recv_sem=line_recv.at[slot, c],
             device_id=device(z, 1 - x),
@@ -577,84 +992,82 @@
         return jnp.where(middle, pick(i, [3, 1, 2, 0]), pick(i, [3, 2, 1, 0]))
 
     def start_side(i, carry):
-        for c in range(chunks):
+        for c in range(count):
             side_copy(send_order(i), c).start()
         return carry
 
     lax.fori_loop(0, 4, start_side, 0)
-    for k in (3, 2, 1, 0):
-        own_copies[k].wait()
+    for copy in own_copies:
+        copy.wait()
 
     def relay(i, carry):
-        k = send_order(i // chunks)
-        c = i % chunks
-        area = pl.ds(c * chunk, chunk)
-        side_copy(k, c).wait_recv()
-        own[k, area] = (
-            own[k, area].astype(jnp.float32) + side_in[k, area].astype(jnp.float32)
-        ).astype(jnp.bfloat16)
-
-        @pl.when(middle)
-        def _():
-            line_wait(line_slot(k), c)
-            own[k, area] = (
-                own[k, area].astype(jnp.float32) + line_in[line_slot(k), area].astype(jnp.float32)
+        k = send_order(i)
+        for c in range(count):
+            side_copy(k, c).wait_recv()
+            own[k, c] = (
+                own[k, c].astype(jnp.float32) + side_in[k, c].astype(jnp.float32)
             ).astype(jnp.bfloat16)
 
-        line_copy(k, c).start()
+            @pl.when(middle)
+            def _(c=c):
+                line_wait(line_slot(k), c)
+                own[k, c] = (
+                    own[k, c].astype(jnp.float32) + line_in[line_slot(k), c].astype(jnp.float32)
+                ).astype(jnp.bfloat16)
+
+            line_copy(k, c).start()
         return carry
 
-    lax.fori_loop(0, 3 * chunks, relay, 0)
-
-    def finish(c, carry):
-        area = pl.ds(c * chunk, chunk)
+    lax.fori_loop(0, 3, relay, 0)
+    for c in range(count):
+        total = totals[c]
         side_copy(0, c).wait_recv()
-        total[area] = own[0, area].astype(jnp.float32) + side_in[0, area].astype(jnp.float32)
+        total[...] = own[0, c].astype(jnp.float32) + side_in[0, c].astype(jnp.float32)
 
         @pl.when(z < 3)
-        def _():
+        def _(c=c, total=total):
             line_wait(z, c)
-            total[area] += line_in[z, area].astype(jnp.float32)
+            total[...] += line_in[z, c].astype(jnp.float32)
 
         @pl.when(z > 0)
-        def _():
+        def _(c=c, total=total):
             line_wait(z + 1, c)
-            total[area] += line_in[z + 1, area].astype(jnp.float32)
+            total[...] += line_in[z + 1, c].astype(jnp.float32)
 
         for k in range(4):
             side_copy(k, c).wait_send()
         for k in range(1, 4):
             line_copy(k, c).wait_send()
-        return carry
-
-    lax.fori_loop(0, chunks, finish, 0)
 
 
 def scatter_parts(parts, collective):
-    rows, wide = parts.shape[1:]
+    count = len(parts)
+    rows, wide = parts[0].shape[1:]
     low = jnp.bfloat16
     dma = pltpu.SemaphoreType.DMA
     return pl.pallas_call(
-        scatter_kernel,
+        functools.partial(scatter_kernel, count),
         name="scatter_parts",
-        out_shape=jax.ShapeDtypeStruct((rows, wide), jnp.float32),
-        in_specs=[pl.BlockSpec(memory_space=pl.ANY)],
-        out_specs=pl.BlockSpec(memory_space=pltpu.VMEM),
+        out_shape=(jax.ShapeDtypeStruct((rows, wide), jnp.float32),) * count,
+        in_specs=[pl.BlockSpec(memory_space=pl.ANY)] * count,
+        out_specs=(pl.BlockSpec(memory_space=pltpu.VMEM),) * count,
         scratch_shapes=[
-            pltpu.VMEM((4, rows, wide), low),
-            pltpu.VMEM((4, rows, wide), low),
-            pltpu.VMEM((5, rows, wide), low),
-            dma((4,)),
-            dma((4, chunks)),
-            dma((4, chunks)),
-            dma((5, chunks)),
-            dma((3, chunks)),
+            pltpu.VMEM((4, count, rows, wide), low),
+            pltpu.VMEM((4, count, rows, wide), low),
+            pltpu.VMEM((5, count, rows, wide), low),
+            dma((4, count)),
+            dma((4, count)),
+            dma((4, count)),
+            dma((5, count)),
+            dma((3, count)),
         ],
         compiler_params=pltpu.CompilerParams(
             collective_id=collective, has_side_effects=True, vmem_limit_bytes=40 << 20
         ),
-        cost_estimate=pl.CostEstimate(flops=8 * rows * wide, bytes_accessed=300 << 20, transcendentals=0),
-    )(parts)
+        cost_estimate=pl.CostEstimate(
+            flops=8 * rows * wide * count, bytes_accessed=300 << 20, transcendentals=0
+        ),
+    )(*parts)
 
 
 def sum_kernel(own, total, incoming, recv, send):
@@ -809,51 +1222,47 @@
     top_count = routes.shape[1]
     hidden_width = gate_w.shape[2]
     factor = 1.0 / math.sqrt(head_width)
-    cot_all = lax.all_gather(cotangent, "expert", axis=0, tiled=True)
     source = tokens.astype(jnp.float32)
     scale_in = inverse_rms(source)
     normed_low = (source * scale_in * norm_in).astype(jnp.bfloat16)
-    gathered = lax.all_gather(normed_low, "tensor", axis=0, tiled=True)
-    seq_len = gathered.shape[0]
-    query_pre = jnp.dot(gathered, query_w, preferred_element_type=jnp.float32)
-    key_pre = jnp.dot(gathered, key_w, preferred_element_type=jnp.float32)
-    value_low = jnp.dot(gathered, value_w, preferred_element_type=jnp.float32).astype(jnp.bfloat16)
+    seq_len = 4 * rows_own
     cosine, sine_table = rotary_tables(seq_len, head_width)
-    query_heads = query_pre.reshape(seq_len, local_heads, head_width)
-    key_heads = key_pre.reshape(seq_len, local_heads, head_width)
+    turn_cosine = jnp.concatenate([cosine[:, 0], cosine[:, 0]], axis=1)
+    turn_sine = jnp.concatenate([-sine_table[:, 0], sine_table[:, 0]], axis=1)
+    (
+        gathered,
+        query_pre,
+        key_pre,
+        query_low,
+        key_low,
+        value_low,
+        attended,
+        log_rows,
+        attn_out,
+        cot_all,
+    ) = attention_forward(
+        normed_low,
+        cotangent,
+        (query_w, key_w, value_w),
+        out_w,
+        (query_gain[None], key_gain[None]),
+        (turn_cosine, turn_sine),
+        4,
+    )
+    gathered = gathered.reshape(seq_len, model_width)
+    heads_shape = (seq_len, local_heads, head_width)
+    query_heads = query_pre.reshape(heads_shape)
+    key_heads = key_pre.reshape(heads_shape)
     query_scale = inverse_rms(query_heads)
     key_scale = inverse_rms(key_heads)
-    query_low = rotate(query_heads * query_scale * query_gain, cosine, sine_table).astype(
-        jnp.bfloat16
-    )
-    key_low = rotate(key_heads * key_scale * key_gain, cosine, sine_table).astype(jnp.bfloat16)
-    value_heads = value_low.reshape(seq_len, local_heads, head_width)
+    key_low = key_low.reshape(heads_shape)
+    value_heads = value_low.reshape(heads_shape)
     block_rows = min(512, seq_len)
     block_count = seq_len // block_rows
     query_blocks = query_low.reshape(block_count, block_rows, local_heads, head_width)
-
-    def attend(query_block):
-        scores = (
-            jnp.einsum("qhd,khd->hqk", query_block, key_low, preferred_element_type=jnp.float32)
-            * factor
-        )
-        row_max = jnp.max(scores, axis=-1, keepdims=True)
-        shifted = jnp.exp(scores - row_max)
-        row_sum = jnp.sum(shifted, axis=-1, keepdims=True)
-        probs_low = (shifted / row_sum).astype(jnp.bfloat16)
-        mixture = jnp.einsum(
-            "hqk,khd->qhd", probs_low, value_heads, preferred_element_type=jnp.float32
-        )
-        return (mixture.astype(jnp.bfloat16), (row_max + jnp.log(row_sum))[..., 0])
-
-    attended_blocks, log_sums = lax.map(attend, query_blocks)
-    attended = attended_blocks.reshape(seq_len, local_heads * head_width)
-    attn_out = lax.psum_scatter(
-        jnp.dot(attended, out_w, preferred_element_type=jnp.float32).astype(jnp.bfloat16),
-        "tensor",
-        scatter_dimension=0,
-        tiled=True,
-    ).astype(jnp.float32)
+    log_sums = (
+        log_rows[:, :local_heads].T.reshape(local_heads, block_count, block_rows).transpose(1, 0, 2)
+    )
     middle = source + attn_out
     scale_mid = inverse_rms(middle)
     normed_mid = middle * scale_mid * norm_mid
@@ -869,20 +1278,11 @@
     gates_low = (gates - gates_high.astype(jnp.float32)).astype(jnp.bfloat16)
     spare = jnp.zeros((rows_own, 128 - 2 * experts_all), jnp.bfloat16)
     own_rows = jnp.concatenate([mid_low, gates_high, gates_low, spare], axis=1)
-    blocks = (expert_count, rows_own, experts_local * hidden_width)
-    raw_all = jnp.concatenate(
-        [
-            lax.dot_general(
-                cot_all, down_w[e], contract_last, preferred_element_type=jnp.float32
-            ).astype(jnp.bfloat16)
-            for e in range(experts_local)
-        ],
-        axis=1,
-    ).reshape(blocks)
-    rows_all, hidden_all, gate_all, up_all, row_total = expert_pass(
-        own_rows, raw_all, gate_w, up_w, experts_all, 1
+    rows_all, hidden_all, gate_all, up_all, y_all, row_total = expert_pass(
+        own_rows, cot_all, gate_w, up_w, down_w, experts_all, 1
     )
     expert_input_grad = row_total[:, :model_width]
+    cot_all = cot_all.reshape(expert_count * rows_own, model_width)
     gate_grad_dense = (
         row_total[:, model_width : model_width + experts_all]
         + row_total[:, model_width + experts_all : model_width + 2 * experts_all]
@@ -894,26 +1294,18 @@
     hidden_all = hidden_all.reshape(count, inner_all)
     gate_all = gate_all.reshape(count, inner_all)
     up_all = up_all.reshape(count, inner_all)
-    y_part = jnp.dot(
-        hidden_all, down_w.reshape(inner_all, model_width), preferred_element_type=jnp.float32
-    ).astype(jnp.bfloat16)
+    y_part = y_all.reshape(count, model_width)
     y_sum = lax.psum_scatter(y_part, "expert", scatter_dimension=0, tiled=True)
     output = (middle + y_sum.astype(jnp.float32)).astype(jnp.bfloat16)
     me = lax.axis_index("tensor")
     far = jnp.stack([me ^ 1, me ^ 3]).astype(jnp.int32)
     near = jnp.stack([me, me ^ 2]).astype(jnp.int32)
-    gate_w_grad = exchange(
-        input_weight_parts(far, rows_all, gate_all, model_width, experts_local),
-        input_weight_parts(near, rows_all, gate_all, model_width, experts_local),
-    )
-    up_w_grad = exchange(
-        input_weight_parts(far, rows_all, up_all, model_width, experts_local),
-        input_weight_parts(near, rows_all, up_all, model_width, experts_local),
-    )
-    down_w_grad = exchange(
-        output_weight_parts(far, hidden_all, cot_all, experts_local),
-        output_weight_parts(near, hidden_all, cot_all, experts_local),
-    )
+    gate_far = input_weight_parts(far, rows_all, gate_all, model_width, experts_local)
+    up_far = input_weight_parts(far, rows_all, up_all, model_width, experts_local)
+    down_far = output_weight_parts(far, hidden_all, cot_all, experts_local)
+    gate_near = input_weight_parts(near, rows_all, gate_all, model_width, experts_local)
+    up_near = input_weight_parts(near, rows_all, up_all, model_width, experts_local)
+    down_near = output_weight_parts(near, hidden_all, cot_all, experts_local)
     inner_gate = jnp.sum(gating * gate_grad, axis=-1, keepdims=True)
     chosen_grad = gating * (gate_grad - inner_gate)
     logit_grad = jnp.sum(chosen_grad[:, :, None] * mask_float, axis=1)
@@ -931,6 +1323,7 @@
     middle_grad = upstream + norm_backward(normed_mid_grad, middle, scale_mid, norm_mid)
     branch_low = middle_grad.astype(jnp.bfloat16)
     branch_all = lax.all_gather(branch_low, "tensor", axis=0, tiled=True)
+    branch_all, gate_far, up_far = lax.optimization_barrier((branch_all, gate_far, up_far))
     attended_grad = lax.dot_general(
         branch_all, out_w, contract_last, preferred_element_type=jnp.float32
     ).astype(jnp.bfloat16)
@@ -1020,26 +1413,31 @@
     ).astype(jnp.float32)
     part_rows = model_width // expert_count
     local_width = local_heads * head_width
-    weight_parts = jnp.concatenate(
-        [p.astype(jnp.bfloat16) for p in (query_w_part, key_w_part, value_w_part)], axis=1
-    ).reshape(expert_count, part_rows, 3 * local_width)
-    weight_sums = scatter_parts(weight_parts, 2)
-    query_w_grad = weight_sums[:, :local_width]
-    key_w_grad = weight_sums[:, local_width : 2 * local_width]
-    value_w_grad = weight_sums[:, 2 * local_width :]
-    norm_mid_grad, router_w_grad = lax.psum((norm_mid_part, router_part), ("expert", "tensor"))
+    query_w_grad, key_w_grad, value_w_grad = scatter_parts(
+        [
+            p.astype(jnp.bfloat16).reshape(expert_count, part_rows, local_width)
+            for p in (query_w_part, key_w_part, value_w_part)
+        ],
+        2,
+    )
+    gate_w_grad = exchange(gate_far, gate_near)
+    up_w_grad = exchange(up_far, up_near)
+    down_w_grad = exchange(down_far, down_near)
+    router_w_grad = lax.psum(router_part, ("expert", "tensor"))
     small = jnp.concatenate(
         [
             norm_in_part,
             query_gain_part,
             key_gain_part,
-            jnp.zeros((-(model_width + 2 * head_width) % 1024,), jnp.float32),
+            norm_mid_part,
+            jnp.zeros((-(2 * model_width + 2 * head_width) % 1024,), jnp.float32),
         ]
     ).reshape(-1, 128)
     sums = sum_everywhere(small, 3).reshape(-1)
     norm_in_grad = sums[:model_width]
     query_gain_grad = sums[model_width : model_width + head_width]
     key_gain_grad = sums[model_width + head_width : model_width + 2 * head_width]
+    norm_mid_grad = sums[model_width + 2 * head_width : 2 * model_width + 2 * head_width]
     return (
         output,
         input_grad,

time: 1030 us -> 859 us (0.83)
  Pallas kernels: 441 us -> 554 us
  waiting for transfers between devices: 191 us -> 82.1 us
  matrix products: 155 us -> 68.7 us
  blocking collectives: 40.2 us -> 0 us
  other arithmetic: 114 us -> 79 us
  local copies, waits for them, and re-layouts: 60.6 us -> 44.5 us
    all_gather x2 -> x0, waiting for transfers between devices: 112 us -> none  [the longest x1 76.9 us: per_device(): cot_all = lax.all_gather(cotangent, 'expert', axis=0, tiled=True)]
    pallas_call x1 -> x2, Pallas kernels: 97.3 us -> 209 us  [the longest x1 109 us: scatter_parts(): pl.pallas_call(functools.partial(scatter_kernel, count), name='scatter_pa...]
    dot_general x11 -> x0, matrix products: 81.6 us -> none  [the longest x2 26 us: per_device(): lax.dot_general(cot_all, down_w[e], contract_last, preferred_element_type...]
    reduce_scatter x1 -> x0, waiting for transfers between devices: 44 us -> none  [per_device(): lax.psum_scatter(jnp.dot(attended, out_w, preferred_element_type=jnp.floa...]
    psum x1 -> x0, blocking collectives: 40.2 us -> none  [per_device(): lax.psum((norm_mid_part, router_part), ('expert', 'tensor'))]
    ppermute x3, waiting for transfers between devices: 0.01 us -> 36.4 us  [exchange(): return own + lax.ppermute(sent, 'tensor', swap_line).astype(jnp.float32)]
    all_gather x1, waiting for transfers between devices: 34.6 us -> 0.01 us  [per_device(): branch_all = lax.all_gather(branch_low, 'tensor', axis=0, tiled=True)]
    concatenate x5 -> x1, local copies, waits for them, and re-layouts: 28 us -> 0.01 us  [per_device(): jnp.concatenate([norm_in_part, query_gain_part, key_gain_part, norm_mid_p...]
  transfers between devices with their start and end apart: 14 -> 11, of which waited for: 4 -> 3; matrix products, arithmetic and copies ran while one was open for 11% -> 12% of each run, Pallas kernels for 20% -> 26%
where the time goes in v3:
time: 859 us; the launch traced here: 851 us
  Pallas kernels  554 us (64%)
  waiting for transfers between devices  82.1 us (10%)
  other arithmetic  79 us (9%)
  matrix products  68.7 us (8%)
  local copies, waits for them, and re-layouts  44.5 us (5%)
  between operations  16.7 us (2%)
    pallas_call x1, Pallas kernels, expert_pass(): pl.pallas_call(functools.partial(expert_kernel, experts_all), name='exper...  236 us
    pallas_call x1, Pallas kernels, scatter_parts(): pl.pallas_call(functools.partial(scatter_kernel, count), name='scatter_pa...  109 us
    pallas_call x1, Pallas kernels, attention_forward(): pl.pallas_call(attention_kernel, name='attention_forward', out_shape=(jax...  100 us
    pallas_call x4, Pallas kernels, input_weight_parts(): pl.pallas_call(weight_kernel, name='input_weight_parts', out_shape=jax.Sh...  59.8 us
    ppermute x3, waiting for transfers between devices, exchange(): return own + lax.ppermute(sent, 'tensor', swap_line).astype(jnp.float32)  36.4 us
    pallas_call x2, Pallas kernels, output_weight_parts(): pl.pallas_call(weight_kernel, name='output_weight_parts', out_shape=jax.S...  29 us
    reduce_scatter x1, waiting for transfers between devices, per_device(): y_sum = lax.psum_scatter(y_part, 'expert', scatter_dimension=0, tiled=True)  26.7 us
    pallas_call x1, Pallas kernels, sum_everywhere(): pl.pallas_call(sum_kernel, name='sum_everywhere', out_shape=jax.ShapeDtyp...  20.1 us
  transfers between devices with their start and end apart: 11, of which 3 were waited for; matrix products, arithmetic and copies ran while one was open for 12% of the time, Pallas kernels for 26%

profile of v3, /device:TPU:0, one launch (start us, length us, event | category | flops | bytes accessed | tf_op | source)
XLA Modules:
  0.0 850.8 jit_solution(2017021895243182115)
XLA Ops:
  8.1 2.0 fusion.48
  13.0 100.0 %attention_forward.1 = (bf16[4,256,2048]{2,1,0:T(8,128)(2,1)}, f32[1024,512]{1,0:T(8,128)}, f32[1024,512]{1,0:T(8,128)}, bf16[1024,512]{1,0:T(8,128)(2,1)}, bf16...) custom-call(bf16[256,2048]{1,0:T(8,128)(2,1)} %fusion.15.own, ...), custom_call_target="tpu_custom_call" | custom-call | flops 8589934592 | bytes 67108864 | tf_op jit(solution)/shard_map/attention_forward/pallas_call | solution.py:865
  113.1 2.0 multiply_reduce_fusion.5
  115.1 1.8 fusion.38
  120.1 2.6 concatenate.24.own_rows
  122.7 236.0 %expert_pass.1 = (bf16[8,256,2176]{2,1,0:T(8,128)(2,1)}, bf16[8,256,2048]{2,1,0:T(8,128)(2,1)}, bf16[8,256,2048]{2,1,0:T(8,128)(2,1)}, bf16[8,256,2048]{2,1,0:T(...) custom-call(bf16[256,2176]{1,0:T(8,128)(2,1)} %concatenate.24.own_rows, ...), custom_call_target="tpu_custom_call" | custom-call | flops 103079215104 | bytes 67108864 | tf_op jit(solution)/shard_map/expert_pass/pallas_call | solution.py:488
  360.0 4.6 multiply_reduce_fusion.1
  366.0 1.8 fusion.51
  370.3 2.9 reshape.325
  373.2 2.9 reshape.315
  376.2 2.9 multiply_reduce_fusion.2
  385.5 14.0 %input_weight_parts.5 = bf16[2,2,2048,256]{3,2,1,0:T(8,128)(2,1)S(1)} custom-call(s32[2]{0:T(128)S(1)} %pad_add_fusion.order, bf16[2048,2176]{1,0:T(8,128)(2,1)} %bitcast.209, bf16[2048,2048]{1,0:T(8,128)(2,1)} %bitcast.217), custom_call_target="tpu_custom_call" | custom-call | flops 8589934592 | bytes 16777216 | tf_op jit(solution)/shard_map/input_weight_parts/pallas_call | solution.py:1140
  399.5 2.0 copy-done.7
  401.5 15.0 %input_weight_parts.4 = bf16[2,2,2048,256]{3,2,1,0:T(8,128)(2,1)} custom-call(s32[2]{0:T(128)S(1)} %pad_add_fusion.order, bf16[2048,2176]{1,0:T(8,128)(2,1)} %bitcast.210, bf16[2048,2048]{1,0:T(8,128)(2,1)} %bitcast.215), custom_call_target="tpu_custom_call" | custom-call | flops 8589934592 | bytes 16777216 | tf_op jit(solution)/shard_map/input_weight_parts/pallas_call | solution.py:1140
  416.5 5.2 convolution_convert_fusion.4
  422.9 42.6 %while.15 = (s32[]{:T(128)}, f32[1024,4,128]{0,2,1:T(8,128)S(1)}, f32[1024,4,128]{0,2,1:T(8,128)}, f32[2,512,4,128]{3,1,0,2:T(8,128)}, bf16[2,512,4,128]{3,2,1,0...) while((s32[]{:T(128)}, f32[1024,4,128]{0,2,1:T(8,128)S(1)}, ...), condition=%wide.region_14.15_spmd.clone, body=%wide.region_12.14_spmd.clone.sunk | while | flops 2712401920 | bytes 172024624 | solution.py:1364
  423.3 1.7 constant_dynamic-slice_fusion.3
  426.3 2.7 multiply_reduce_fusion.8
  429.6 3.3 multiply_convert_fusion.2
  432.9 3.6 bitcast_add_fusion.7
  436.6 4.2 fusion.98
  440.8 3.0 bitcast_add_fusion.8
  443.8 1.6 constant_dynamic-slice_fusion.3
  446.8 2.6 multiply_reduce_fusion.8
  450.1 3.3 multiply_convert_fusion.2
  453.5 3.6 bitcast_add_fusion.7
  457.1 4.2 fusion.98
  461.3 4.2 bitcast_add_fusion.8
  465.5 1.8 copy.140
  467.3 6.3 convolution_convert_fusion
  473.7 1.5 copy-done.17
  475.2 5.5 multiply_add_fusion
  480.8 2.5 fusion.44
  484.3 4.7 fusion.45
  490.0 1.8 convert_element_type.162
  491.8 2.5 mul.575
  497.7 2.4 fusion.53
  504.2 2.4 fusion.52
  506.6 6.0 add_convert_fusion
  513.3 15.1 %output_weight_parts.3 = bf16[2,2,256,2048]{3,2,1,0:T(8,128)(2,1)} custom-call(s32[2]{0:T(128)S(1)} %pad_add_fusion.order, bf16[2048,2048]{1,0:T(8,128)(2,1)} %bitcast.219, bf16[2048,2048]{1,0:T(8,128)(2,1)} %bitcast.213), custom_call_target="tpu_custom_call" | custom-call | flops 8589934592 | bytes 16777216 | tf_op jit(solution)/shard_map/output_weight_parts/pallas_call | solution.py:1167
  529.0 13.8 %output_weight_parts.2 = bf16[2,2,256,2048]{3,2,1,0:T(8,128)(2,1)S(1)} custom-call(s32[2]{0:T(128)S(1)} %pad_add_fusion.1.order, bf16[2048,2048]{1,0:T(8,128)(2,1)} %bitcast.220, bf16[2048,2048]{1,0:T(8,128)(2,1)} %bitcast.214), custom_call_target="tpu_custom_call" | custom-call | flops 8589934592 | bytes 16777216 | tf_op jit(solution)/shard_map/output_weight_parts/pallas_call | solution.py:1167
  543.0 5.4 fusion.32
  548.4 2.0 collective-permute-start.5
  550.4 2.0 fusion.37
  552.5 14.0 %input_weight_parts.7 = bf16[2,2,2048,256]{3,2,1,0:T(8,128)(2,1)S(1)} custom-call(s32[2]{0:T(128)S(1)} %pad_add_fusion.1.order, bf16[2048,2176]{1,0:T(8,128)(2,1)} %bitcast.211, bf16[2048,2048]{1,0:T(8,128)(2,1)} %bitcast.218), custom_call_target="tpu_custom_call" | custom-call | flops 8589934592 | bytes 16777216 | tf_op jit(solution)/shard_map/input_weight_parts/pallas_call | solution.py:1140
  566.5 16.7 %input_weight_parts.6 = bf16[2,2,2048,256]{3,2,1,0:T(8,128)(2,1)S(1)} custom-call(s32[2]{0:T(128)S(1)} %pad_add_fusion.1.order, bf16[2048,2176]{1,0:T(8,128)(2,1)} %bitcast.212, bf16[2048,2048]{1,0:T(8,128)(2,1)} %bitcast.216), custom_call_target="tpu_custom_call" | custom-call | flops 8589934592 | bytes 16777216 | tf_op jit(solution)/shard_map/input_weight_parts/pallas_call | solution.py:1140
  583.3 36.4 %collective-permute-done.5 = bf16[2,256,2048]{2,1,0:T(8,128)(2,1)S(1)} collective-permute-done((bf16[2,256,2048]{2,1,0:T(8,128)(2,1)}, bf16[2,256,2048]{2,1,0:T(8,128)(2,1)S(1)}, u32[]{:S(2)}, u32[]{:S(2)}) %collective-permute-start.5) | collective-permute-done | bytes 2097184 | tf_op jit(solution)/shard_map/ppermute | solution.py:1195
  619.6 4.7 bitcast_add_fusion.2
  624.4 3.6 fusion.31
  628.0 1.7 collective-permute-start.3
  629.8 2.4 convolution_convert_fusion.2
  632.2 3.5 fusion.30
  636.2 2.4 convolution_convert_fusion.3
  638.6 2.4 convolution_convert_fusion.1
  641.0 109.4 %scatter_parts.1 = (f32[256,512]{1,0:T(8,128)S(1)}, f32[256,512]{1,0:T(8,128)S(1)}, f32[256,512]{1,0:T(8,128)S(1)}) custom-call(bf16[8,256,512]{2,1,0:T(8,128)(2,1)S(1)} %bitcast.194, bf16[8,256,512]{2,1,0:T(8,128)(2,1)S(1)} %bitcast.193, bf16[8,256,512]{2,1,0:T(8,128)(2,1)S(1)} %bitcast.195), custom_call_target="tpu_custom_call" | custom-call | flops 3145728 | bytes 314572800 | tf_op jit(solution)/shard_map/scatter_parts/pallas_call | solution.py:1048
  750.5 1.8 convert_element_type.170
  752.3 5.9 bitcast_add_fusion.3
  758.2 5.1 bitcast_add_fusion.4
  763.4 1.9 fusion.29
  765.9 20.1 %sum_everywhere.1 = f32[6,40,128]{2,1,0:T(8,128)} custom-call(f32[40,128]{1,0:T(8,128)} %bitcast.206), custom_call_target="tpu_custom_call" | custom-call | flops 25600 | bytes 41943040 | tf_op jit(solution)/shard_map/sum_everywhere/pallas_call | solution.py:1109
  786.1 1.3 slice_bitcast_fusion
  788.7 26.7 %reduce-scatter.4.cloned.1.call-done = bf16[256,2048]{1,0:T(8,128)(2,1)} async-done(((bf16[2048,2048]{1,0:T(8,128)(2,1)}), bf16[256,2048]{1,0:T(8,128)(2,1)}) %reduce-scatter.4.cloned.1.call-update) | async-done | bytes 1048592 | tf_op jit(solution)/shard_map/reduce_scatter | solution.py:1298
  815.3 6.2 fusion.19
  821.6 18.5 %all-reduce.2.cloned.1.call-done = f32[2048,16]{0,1:T(8,128)} async-done(((f32[2048,16]{0,1:T(8,128)}), f32[2048,16]{0,1:T(8,128)}) %all-reduce.2.cloned.1.call-update) | async-done | bytes 131088 | tf_op jit(solution)/shard_map/psum | solution.py:1426
  (238 shorter events, 39.1 us)
Async XLA Ops:
  8.0 107.1 %copy-start = (f32[2048,16]{0,1:T(8,128)S(1)}, f32[2048,16]{0,1:T(8,128)}, u32[]{:S(2)}) copy-start(f32[2048,16]{0,1:T(8,128)} %param.28) | copy-start | bytes 393220
  8.1 408.5 %all-gather.2.cloned.1.call-start = ((), (), s32[]{:S(2)}) async-start(), calls=%async_computation.4 | async-start | bytes 5242880 | tf_op jit(solution)/shard_map/all_gather | solution.py:1325
  10.1 2.9 copy-start.25
  10.1 2.9 copy-start.27
  10.4 2.6 copy-start.58
  115.0 249.7 %copy-start.11 = (f32[256,2048]{1,0:T(8,128)}, f32[256,2048]{1,0:T(8,128)S(1)}, u32[]{:S(2)}) copy-start(f32[256,2048]{1,0:T(8,128)S(1)} %get-tuple-element.217) | copy-start | bytes 6291460
  122.7 237.1 %copy-start.46 = (s32[256,8]{0,1:T(8,128)S(1)}, s32[256,8]{0,1:T(8,128)}, u32[]{:S(2)}) copy-start(s32[256,8]{0,1:T(8,128)} %param.19) | copy-start | bytes 24580
  122.7 237.2 %copy-start.55 = (f32[256]{0:T(256)S(1)}, f32[256]{0:T(256)}, u32[]{:S(2)}) copy-start(f32[256]{0:T(256)} %copy-done.54) | copy-start | bytes 3076
  122.7 237.2 %copy-start.57 = (f32[256]{0:T(256)S(1)}, f32[256]{0:T(256)}, u32[]{:S(2)}) copy-start(f32[256]{0:T(256)} %copy-done.56) | copy-start | bytes 3076
  122.7 237.3 %copy-start.50 = (f32[256]{0:T(256)S(1)}, f32[256]{0:T(256)}, u32[]{:S(2)}) copy-start(f32[256]{0:T(256)} %copy-done.49) | copy-start | bytes 3076
  360.0 4.7 copy-start.42
  360.0 6.0 copy-start.29
  364.7 3.2 copy-start.60
  367.9 382.6 %reduce-scatter.8.cloned.1.call-start = ((), (), s32[]{:S(2)}) async-start(), calls=%async_computation.6 | async-start | bytes 2359296 | tf_op jit(solution)/shard_map/reduce_scatter | solution.py:1411
  376.1 3.0 copy-start.22
  376.2 4.1 copy-start.64
  376.2 4.7 copy-start.66
  379.1 4.1 copy-start.38
  381.4 2.9 copy-start.37
  426.2 3.4 copy-start.8
  432.9 3.6 copy-start.10
  432.9 7.9 copy-start.9
  446.7 3.4 copy-start.8
  453.5 3.6 copy-start.10
  453.5 7.8 copy-start.9
  467.3 6.4 copy-start.26
  467.3 6.4 copy-start.28
  473.7 289.7 %reduce-scatter.6.cloned.1.call-start = ((), (), s32[]{:S(2)}) async-start(), calls=%async_computation.5 | async-start | bytes 5242880 | tf_op jit(solution)/shard_map/reduce_scatter | solution.py:1398
  475.2 5.5 copy-start.20
  475.2 5.5 copy-start.65
  480.8 3.5 copy-start.19
  480.8 3.5 copy-start.67
  490.0 4.4 copy-start.31
  491.8 3.8 copy-start.21
  491.8 3.8 copy-start.24
  491.8 3.8 copy-start.63
  500.1 2.5 copy-start.23
  500.1 2.5 copy-start.62
  503.7 3.0 copy-start.35
  512.7 302.6 %reduce-scatter.4.cloned.1.call-start = ((), (), s32[]{:S(2)}) async-start(), calls=%async_computation.3 | async-start | bytes 9437184 | tf_op jit(solution)/shard_map/reduce_scatter | solution.py:1298
  513.3 326.8 %all-reduce.2.cloned.1.call-start = ((), (), s32[]{:S(2)}) async-start(), calls=%async_computation.7 | async-start | bytes 262144 | tf_op jit(solution)/shard_map/psum | solution.py:1426
  528.5 14.6 %collective-permute-start.4 = (bf16[2,2,256,2048]{3,2,1,0:T(8,128)(2,1)}, bf16[2,2,256,2048]{3,2,1,0:T(8,128)(2,1)}, u32[]{:S(2)}, u32[]{:S(2)}) collective-permute-start(bf16[2,2,256,2048]{3,2,1,0:T(8,128)(2,1)} %output_weight_parts.3), channel_id=1, source_target_pairs={{0,1},{1,0},{2,3},{3,2},{4,5},{5,4},{6,7},{7,6},{8,9},{9,8},{10,11... | collective-permute-start | bytes 12582920 | tf_op jit(solution)/shard_map/ppermute | solution.py:1192
  528.5 95.9 %collective-permute-start.2 = (bf16[2,2,2048,256]{3,2,1,0:T(8,128)(2,1)}, bf16[2,2,2048,256]{3,2,1,0:T(8,128)(2,1)}, u32[]{:S(2)}, u32[]{:S(2)}) collective-permute-start(bf16[2,2,2048,256]{3,2,1,0:T(8,128)(2,1)} %copy-done.7), channel_id=1, source_target_pairs={{0,1},{1,0},{2,3},{3,2},{4,5},{5,4},{6,7},{7,6},{8,9},{9,8},{10,11... | collective-permute-start | bytes 12582920 | tf_op jit(solution)/shard_map/ppermute | solution.py:1192
  542.9 5.6 copy-start.5
  542.9 7.5 copy-start.12
  542.9 7.5 copy-start.41
  542.9 7.5 copy-start.43
  542.9 7.5 copy-start.51
  542.9 89.2 %collective-permute-start = (bf16[2,2,2048,256]{3,2,1,0:T(8,128)(2,1)}, bf16[2,2,2048,256]{3,2,1,0:T(8,128)(2,1)}, u32[]{:S(2)}, u32[]{:S(2)}) collective-permute-start(bf16[2,2,2048,256]{3,2,1,0:T(8,128)(2,1)} %input_weight_parts.4), channel_id=1, source_target_pairs={{0,1},{1,0},{2,3},{3,2},{4,5},{5,4},{6,7},{7,6},{8,9},{9,8},{10,11... | collective-permute-start | bytes 12582920 | tf_op jit(solution)/shard_map/ppermute | solution.py:1192
  548.4 71.2 %collective-permute-start.5 = (bf16[2,256,2048]{2,1,0:T(8,128)(2,1)}, bf16[2,256,2048]{2,1,0:T(8,128)(2,1)S(1)}, u32[]{:S(2)}, u32[]{:S(2)}) collective-permute-start(bf16[2,256,2048]{2,1,0:T(8,128)(2,1)} %fusion.32), channel_id=1, source_target_pairs={{0,2},{1,3},{2,0},{3,1},{4,6},{5,7},{6,4},{7,5},{8,10},{9,11},{10,... | collective-permute-start | bytes 6291464 | tf_op jit(solution)/shard_map/ppermute | solution.py:1195
  566.5 57.9 %copy-start.4 = (bf16[2,2,2048,256]{3,2,1,0:T(8,128)(2,1)}, bf16[2,2,2048,256]{3,2,1,0:T(8,128)(2,1)S(1)}, u32[]{:S(2)}) copy-start(bf16[2,2,2048,256]{3,2,1,0:T(8,128)(2,1)S(1)} %input_weight_parts.7) | copy-start | bytes 12582916
  566.5 53.1 %copy-start.6 = (bf16[2,2,256,2048]{3,2,1,0:T(8,128)(2,1)S(1)}, bf16[2,2,256,2048]{3,2,1,0:T(8,128)(2,1)}, u32[]{:S(2)}) copy-start(bf16[2,2,256,2048]{3,2,1,0:T(8,128)(2,1)} %copy-done.5) | copy-start | bytes 12582916
  583.3 48.9 %copy-start.2 = (bf16[2,2,2048,256]{3,2,1,0:T(8,128)(2,1)}, bf16[2,2,2048,256]{3,2,1,0:T(8,128)(2,1)S(1)}, u32[]{:S(2)}) copy-start(bf16[2,2,2048,256]{3,2,1,0:T(8,128)(2,1)S(1)} %input_weight_parts.6) | copy-start | bytes 12582916
  624.4 5.4 copy-start.34
  624.4 5.4 copy-start.70
  628.0 124.2 %collective-permute-start.3 = (bf16[2,2048,256]{2,1,0:T(8,128)(2,1)}, bf16[2,2048,256]{2,1,0:T(8,128)(2,1)}, u32[]{:S(2)}, u32[]{:S(2)}) collective-permute-start(bf16[2,2048,256]{2,1,0:T(8,128)(2,1)} %fusion.31), channel_id=1, source_target_pairs={{0,2},{1,3},{2,0},{3,1},{4,6},{5,7},{6,4},{7,5},{8,10},{9,11},{10,... | collective-permute-start | bytes 6291464 | tf_op jit(solution)/shard_map/ppermute | solution.py:1195
  632.2 4.1 copy-start.36
  635.7 122.5 %collective-permute-start.1 = (bf16[2,2048,256]{2,1,0:T(8,128)(2,1)}, bf16[2,2048,256]{2,1,0:T(8,128)(2,1)}, u32[]{:S(2)}, u32[]{:S(2)}) collective-permute-start(bf16[2,2048,256]{2,1,0:T(8,128)(2,1)} %fusion.30), channel_id=1, source_target_pairs={{0,2},{1,3},{2,0},{3,1},{4,6},{5,7},{6,4},{7,5},{8,10},{9,11},{10,... | collective-permute-start | bytes 6291464 | tf_op jit(solution)/shard_map/ppermute | solution.py:1195
  752.3 5.9 copy-start.3
  758.2 5.2 copy-start.16
  758.2 5.2 copy-start.48
  758.2 5.2 copy-start.59
  763.3 52.0 %copy-start.61 = (f32[256]{0:T(256)S(1)}, f32[256]{0:T(256)}, u32[]{:S(2)}) copy-start(f32[256]{0:T(256)} %copy-done.60) | copy-start | bytes 3076
  815.3 27.8 %copy-start.1 = (f32[2048,16]{0,1:T(8,128)S(1)}, f32[2048,16]{0,1:T(8,128)}, u32[]{:S(2)}) copy-start(f32[2048,16]{0,1:T(8,128)} %param.28) | copy-start | bytes 393220
  (23 other events, 37.5 us)
Sparse Core Ops, SparseCore 0:
  368.0 42.9 all-gather.1
  473.8 77.2 reduce-scatter.7
  553.6 66.1 reduce-scatter.5
  623.7 191.5 reduce-scatter.3
Sparse Core Ops, SparseCore 1:
  552.6 287.4 all-reduce.1

commit v4 on v3

--- a/solution.py
+++ b/solution.py
@@ -85,12 +85,14 @@
     gate_hbm,
     up_hbm,
     down_hbm,
-    rows_all,
     hidden_all,
-    gate_all,
-    up_all,
+    grads_all,
     y_all,
     total,
+    far_input,
+    near_input,
+    far_output,
+    near_output,
     gate_v,
     up_v,
     down_v,
@@ -103,16 +105,20 @@
     stage,
     parts,
     side_in,
+    cross_in,
     line_in,
     weight_sem,
     own_sem,
     cot_sem,
     out_sem,
-    rows_sem,
+    item_in,
+    item_out,
     gather_recv,
     gather_send,
     side_recv,
     side_send,
+    cross_recv,
+    cross_send,
     line_recv,
     line_send,
 ):
@@ -121,10 +127,14 @@
     z = position // 2
     x = position % 2
     experts_local, width, hidden = gate_v.shape
-    rows = rows_v.shape[1]
+    rows = cot_v.shape[0]
+    part = hidden // 4
+    y = peer // 2
+    core = peer % 2
     chunk = rows // chunks
     middle = (z == 1) | (z == 2)
     ends = (z == 0) | (z == 3)
+    pair = z + 1 - 2 * (z % 2)
     line_slots = [
         z,
         pick(z, [1, 0, 3, 2]),
@@ -132,6 +142,9 @@
         pick(z, [3, 3, 0, 0]),
     ]
 
+    def block_rows(block):
+        return pl.ds(pl.multiple_of(block * rows, rows), rows)
+
     def device(zz, xx):
         return (zz * 2 + xx, peer)
 
@@ -143,7 +156,7 @@
         pltpu.make_async_copy(up_hbm, up_v, weight_sem.at[1]),
         pltpu.make_async_copy(down_hbm, down_v, weight_sem.at[2]),
     ]
-    own_copy = pltpu.make_async_copy(own_rows, rows_v.at[position], own_sem)
+    own_copy = pltpu.make_async_copy(own_rows, rows_v.at[block_rows(position)], own_sem)
     own_copy.start()
     for copy in weight_copies:
         copy.start()
@@ -164,7 +177,7 @@
     def gather_copy(source, block, index, zz, xx):
         return pltpu.make_async_remote_copy(
             src_ref=source,
-            dst_ref=rows_v.at[block],
+            dst_ref=rows_v.at[block_rows(block)],
             send_sem=gather_send.at[index],
             recv_sem=gather_recv.at[block],
             device_id=device(zz, xx),
@@ -186,32 +199,63 @@
 
     def forward_side(k):
         block = slot_z(k) * 2 + x
-        return gather_copy(rows_v.at[block], block, 2 + k, z, 1 - x)
+        return gather_copy(rows_v.at[block_rows(block)], block, 2 + k, z, 1 - x)
 
     def forward_line(k):
         block = slot_z(k) * 2 + x
         target = jnp.where(slot_z(k) < z, z + 1, z - 1)
-        return gather_copy(rows_v.at[block], block, 5 + k, jnp.clip(target, 0, 3), x)
+        return gather_copy(rows_v.at[block_rows(block)], block, 5 + k, jnp.clip(target, 0, 3), x)
 
     def arrived(block):
         gather_copy(own_rows, block, 0, z, 1 - x).wait_recv()
-        pltpu.make_async_copy(rows_v.at[block], rows_all.at[block], rows_sem.at[block]).start()
 
     def arrive(k):
         arrived(slot_z(k) * 2 + x)
-        forward_side(k).start()
+        if k < 3:
+
+            @pl.when(ends)
+            def _():
+                forward_side(k).start()
 
         @pl.when(middle)
         def _():
+            if k > 1:
+                forward_side(k).start()
             forward_line(k).start()
+
+    def forward_cross():
+        block = jnp.where(ends, z, slot_z(3)) * 2 + 1 - x
+        return gather_copy(rows_v.at[block_rows(block)], block, 9, pair, x)
+
+    def cross_copy(c):
+        area = pl.ds(c * chunk, chunk)
+        return pltpu.make_async_remote_copy(
+            src_ref=parts.at[5, area],
+            dst_ref=cross_in.at[area],
+            send_sem=cross_send.at[c],
+            recv_sem=cross_recv.at[c],
+            device_id=device(pair, x),
+            device_id_type=pl.DeviceIdType.MESH,
+        )
+
+    def cross_add(c):
+        area = pl.ds(c * chunk, chunk)
+        cross_copy(c).wait_recv()
+        parts[4, area] = (
+            parts[4, area].astype(jnp.float32) + cross_in[area].astype(jnp.float32)
+        ).astype(jnp.bfloat16)
+        side_copy(0, c).start()
+
+    def side_slot(k):
+        return jnp.maximum(k - 1, 0)
 
     def side_copy(k, c):
         area = pl.ds(c * chunk, chunk)
         return pltpu.make_async_remote_copy(
             src_ref=parts.at[4 + k, area],
-            dst_ref=side_in.at[k, area],
-            send_sem=side_send.at[k, c],
-            recv_sem=side_recv.at[k, c],
+            dst_ref=side_in.at[side_slot(k), area],
+            send_sem=side_send.at[side_slot(k), c],
+            recv_sem=side_recv.at[side_slot(k), c],
             device_id=device(z, 1 - x),
             device_id_type=pl.DeviceIdType.MESH,
         )
@@ -243,50 +287,43 @@
             device_id_type=pl.DeviceIdType.MESH,
         ).wait_recv()
 
-    def relay(k, c, has_line):
+    def relay(k, c):
         area = pl.ds(c * chunk, chunk)
-        side_copy(k, c).wait_recv()
-        summed = parts[k, area].astype(jnp.float32) + side_in[k, area].astype(jnp.float32)
-        if has_line is False:
-            parts[k, area] = summed.astype(jnp.bfloat16)
-        else:
-
-            @pl.when(middle)
-            def _():
-                line_wait(line_slot(k), c)
-                parts[k, area] = (
-                    summed + line_in[line_slot(k), area].astype(jnp.float32)
-                ).astype(jnp.bfloat16)
-
-            if has_line is None:
-
-                @pl.when(ends)
-                def _():
-                    parts[k, area] = summed.astype(jnp.bfloat16)
+        if k > 1:
+            side_copy(k, c).wait_recv()
+            parts[k, area] = (
+                parts[k, area].astype(jnp.float32) + side_in[k - 1, area].astype(jnp.float32)
+            ).astype(jnp.bfloat16)
+
+        @pl.when(middle)
+        def _():
+            line_wait(line_slot(k), c)
+            parts[k, area] = (
+                parts[k, area].astype(jnp.float32) + line_in[line_slot(k), area].astype(jnp.float32)
+            ).astype(jnp.bfloat16)
 
         line_copy(k, c).start()
 
     def block_of(step):
-        k = pick(step, [0, 1, 0, 2, 1, 3, 2, 3])
-        side = pick(step, [0, 0, 1, 0, 1, 0, 1, 1])
+        k = pick(step, [0, 1, 0, 1, 2, 2, 3, 3])
+        side = pick(step, [0, 0, 1, 1, 0, 1, 1, 0])
         return k, side, slot_z(k) * 2 + jnp.where(side == 1, 1 - x, x)
 
     def cot_copy(step):
-        return pltpu.make_async_copy(cot_all.at[block_of(step)[2]], cot_v, cot_sem)
+        return pltpu.make_async_copy(cot_all.at[block_rows(block_of(step)[2])], cot_v, cot_sem)
 
     def y_copy(block):
         return pltpu.make_async_copy(y_v, y_all.at[block], out_sem.at[3])
 
     def out_copies(block):
         return [
-            pltpu.make_async_copy(hidden_v, hidden_all.at[block], out_sem.at[0]),
-            pltpu.make_async_copy(gate_b, gate_all.at[block], out_sem.at[1]),
-            pltpu.make_async_copy(up_b, up_all.at[block], out_sem.at[2]),
+            pltpu.make_async_copy(hidden_v, hidden_all.at[block_rows(block)], out_sem.at[0]),
+            pltpu.make_async_copy(gate_b, grads_all.at[0, block_rows(block)], out_sem.at[1]),
+            pltpu.make_async_copy(up_b, grads_all.at[1, block_rows(block)], out_sem.at[2]),
         ]
 
     cot_copy(0).start()
     own_copy.wait()
-    pltpu.make_async_copy(rows_v.at[position], rows_all.at[position], rows_sem.at[position]).start()
     for copy in weight_copies:
         copy.wait()
 
@@ -301,6 +338,12 @@
             def _():
                 arrive(2)
 
+            arrived(z * 2 + 1 - x)
+
+            @pl.when(ends)
+            def _():
+                forward_cross().start()
+
         @pl.when(step == 3)
         def _():
             @pl.when(ends)
@@ -311,21 +354,19 @@
             def _():
                 arrive(3)
 
-        @pl.when((step == 5) & ends)
+            arrived(slot_z(1) * 2 + 1 - x)
+
+        @pl.when(step == 5)
+        def _():
+            arrived(slot_z(2) * 2 + 1 - x)
+
+        @pl.when((step == 6) & ends)
+        def _():
+            arrived(slot_z(3) * 2 + 1 - x)
+
+        @pl.when((step == 7) & ends)
         def _():
             arrive(3)
-
-        @pl.when(side == 1)
-        def _():
-            arrived(block)
-
-        @pl.when((step == 7) & ends)
-        def _():
-            def one(c, carry):
-                relay(1, c, False)
-                return carry
-
-            lax.fori_loop(0, chunks, one, 0)
 
         @pl.when(step > 0)
         def _():
@@ -333,8 +374,8 @@
                 copy.wait()
 
         cot_copy(step).wait()
-        rows_low = rows_v[block, :, :width]
-        extra = rows_v[block, :, width:].astype(jnp.float32)
+        rows_low = rows_v[block_rows(block), :width]
+        extra = rows_v[block_rows(block), width:].astype(jnp.float32)
         lane = lax.broadcasted_iota(jnp.int32, extra.shape, 1)
         ext = jnp.zeros(extra.shape, jnp.float32)
         for e in range(experts_local):
@@ -370,6 +411,11 @@
         def _():
             cot_copy(step + 1).start()
 
+        @pl.when((step == 4) & middle)
+        def _():
+            arrived(slot_z(3) * 2 + 1 - x)
+            forward_cross().start()
+
         place = side * 4 + k
         parts[place, :, width:] = ext.astype(jnp.bfloat16)
         for copy in out_copies(block):
@@ -387,10 +433,20 @@
                 )
             parts[place, :, span] = summed.astype(jnp.bfloat16)
 
-        @pl.when(side == 1)
+        @pl.when((side == 1) & (k > 1))
         def _():
             for c in range(chunks):
                 side_copy(k, c).start()
+
+        @pl.when(step == 3)
+        def _():
+            for c in range(chunks):
+                cross_copy(c).start()
+
+        @pl.when((step == 1) & ends)
+        def _():
+            for c in range(chunks):
+                line_copy(1, c).start()
 
         @pl.when(step > 0)
         def _():
@@ -411,22 +467,142 @@
 
     lax.fori_loop(0, 8, one_step, 0)
 
-    def relay_two(c, carry):
-        relay(2, c, None)
+    for copy in out_copies(position):
+        copy.wait()
+    y_copy(position).wait()
+    whole_cot = [
+        pltpu.make_async_copy(cot_all.at[:, pl.ds(h * hidden, hidden)], up_v.at[h], weight_sem.at[h])
+        for h in range(2)
+    ]
+    for copy in whole_cot:
+        copy.start()
+
+    def columns_of(pair, q):
+        column_y = jnp.where(q == 0, y, 1 - y)
+        column_core = jnp.where(pair == 0, 1 - core, core)
+        return column_y * 2 + column_core
+
+    def item_source(i):
+        pair = i // 6
+        kind = (i % 6) // 2
+        e = i % 2
+        return pair, kind, e
+
+    def item_loads(i, act):
+        pair, kind, e = item_source(i)
+        slot = i % 2
+        for q in range(2):
+            start = pl.multiple_of(e * hidden + columns_of(pair, q) * part, part)
+            place = gate_v.at[0, :, pl.ds(pl.multiple_of(slot * 2 * part + q * part, part), part)]
+            sem = item_in.at[slot, q]
+
+            @pl.when(kind < 2)
+            def _(start=start, place=place, sem=sem):
+                act(
+                    pltpu.make_async_copy(
+                        grads_all.at[jnp.minimum(kind, 1), :, pl.ds(start, part)], place, sem
+                    )
+                )
+
+            @pl.when(kind == 2)
+            def _(start=start, place=place, sem=sem):
+                act(pltpu.make_async_copy(hidden_all.at[:, pl.ds(start, part)], place, sem))
+
+    def item_stores(i, act):
+        pair, kind, e = item_source(i)
+        slot = i % 2
+        for q in range(2):
+            wide_place = gate_v.at[1, :, pl.ds(pl.multiple_of(slot * 2 * part + q * part, part), part)]
+            tall_place = down_v.at[slot, pl.ds(q * part, part)]
+            sem = item_out.at[slot, q]
+            for which, wide_out, tall_out in (
+                (0, far_input, far_output),
+                (1, near_input, near_output),
+            ):
+
+                @pl.when((pair == which) & (kind < 2))
+                def _(wide_place=wide_place, sem=sem, wide_out=wide_out, q=q):
+                    act(
+                        pltpu.make_async_copy(wide_place, wide_out.at[jnp.minimum(kind, 1), q, e], sem)
+                    )
+
+                @pl.when((pair == which) & (kind == 2))
+                def _(tall_place=tall_place, sem=sem, tall_out=tall_out, q=q):
+                    act(pltpu.make_async_copy(tall_place, tall_out.at[q, e], sem))
+
+    item_loads(0, lambda copy: copy.start())
+    for copy in whole_cot:
+        copy.wait()
+
+    def at(index, first, gap):
+        return (index >= first) & (index < first + gap * chunks) & ((index - first) % gap == 0)
+
+    def item(index, carry):
+        i = index // 4
+        d = index % 4
+        kind = (i % 6) // 2
+        slot = i % 2
+
+        @pl.when(d == 0)
+        def _():
+            item_loads(i, lambda copy: copy.wait())
+
+            @pl.when(i < 11)
+            def _():
+                item_loads(i + 1, lambda copy: copy.start())
+
+            @pl.when(i > 1)
+            def _():
+                item_stores(i - 2, lambda copy: copy.wait())
+
+        columns = pl.ds(pl.multiple_of(slot * 2 * part, 2 * part), 2 * part)
+        span = pl.ds(pl.multiple_of(d * (width // 4), width // 4), width // 4)
+
+        @pl.when(kind < 2)
+        def _():
+            gate_v[1, span, columns] = lax.dot_general(
+                rows_v[:, span], gate_v[0, :, columns], contract_first, preferred_element_type=jnp.float32
+            ).astype(jnp.bfloat16)
+
+        @pl.when(kind == 2)
+        def _():
+            half = pl.ds(pl.multiple_of((d % 2) * (hidden // 2), hidden // 2), hidden // 2)
+            down_v[slot, : 2 * part, span] = lax.dot_general(
+                gate_v[0, :, columns],
+                up_v[d // 2, :, half],
+                contract_first,
+                preferred_element_type=jnp.float32,
+            ).astype(jnp.bfloat16)
+
+        @pl.when(d == 3)
+        def _():
+            item_stores(i, lambda copy: copy.start())
+
+        @pl.when(at(index, 1, 1))
+        def _():
+            cross_add(index - 1)
+
+        @pl.when(at(index, 5, 4))
+        def _():
+            relay(3, (index - 5) // 4)
+
+        @pl.when(at(index, 11, 4) & middle)
+        def _():
+            relay(1, (index - 11) // 4)
+
+        @pl.when(at(index, 18, 1) & ends)
+        def _():
+            relay(2, index - 18)
+
+        @pl.when(at(index, 24, 4) & middle)
+        def _():
+            relay(2, (index - 24) // 4)
+
         return carry
 
-    lax.fori_loop(0, chunks, relay_two, 0)
-
-    def relay_rest(c, carry):
-        relay(3, c, None)
-
-        @pl.when(middle)
-        def _():
-            relay(1, c, True)
-
-        return carry
-
-    lax.fori_loop(0, chunks, relay_rest, 0)
+    lax.fori_loop(0, 48, item, 0)
+    for last in (10, 11):
+        item_stores(last, lambda copy: copy.wait())
 
     def finish(c, carry):
         area = pl.ds(c * chunk, chunk)
@@ -446,8 +622,9 @@
         result = pltpu.make_async_copy(stage, total.at[area], own_sem)
         result.start()
         result.wait()
-        for k in range(4):
+        for k in (0, 2, 3):
             side_copy(k, c).wait_send()
+        cross_copy(c).wait_send()
         for k in range(1, 4):
             line_copy(k, c).wait_send()
         return carry
@@ -464,18 +641,18 @@
     def _():
         own_send(2, z - 1, x).wait_send()
 
-    for k in range(1, 4):
-        forward_side(k).wait_send()
-
-        @pl.when(middle)
-        def _(k=k):
+    forward_cross().wait_send()
+    forward_side(2).wait_send()
+
+    @pl.when(ends)
+    def _():
+        forward_side(1).wait_send()
+
+    @pl.when(middle)
+    def _():
+        forward_side(3).wait_send()
+        for k in range(1, 4):
             forward_line(k).wait_send()
-
-    for copy in out_copies(position):
-        copy.wait()
-    y_copy(position).wait()
-    for block in range(8):
-        pltpu.make_async_copy(rows_v.at[block], rows_all.at[block], rows_sem.at[block]).wait()
 
 
 def expert_pass(own_rows, cot_all, gate_w, up_w, down_w, experts_all, collective):
@@ -489,20 +666,20 @@
         functools.partial(expert_kernel, experts_all),
         name="expert_pass",
         out_shape=(
-            jax.ShapeDtypeStruct((8, rows, wide), low),
-            jax.ShapeDtypeStruct((8, rows, inner), low),
-            jax.ShapeDtypeStruct((8, rows, inner), low),
-            jax.ShapeDtypeStruct((8, rows, inner), low),
+            jax.ShapeDtypeStruct((8 * rows, inner), low),
+            jax.ShapeDtypeStruct((2, 8 * rows, inner), low),
             jax.ShapeDtypeStruct((8, rows, width), low),
             jax.ShapeDtypeStruct((rows, wide), jnp.float32),
+            *(jax.ShapeDtypeStruct((2, 2, experts_local, width, hidden // 4), low),) * 2,
+            *(jax.ShapeDtypeStruct((2, experts_local, hidden // 4, width), low),) * 2,
         ),
         in_specs=[any_space] * 5,
-        out_specs=(any_space,) * 6,
+        out_specs=(any_space,) * 8,
         scratch_shapes=[
             pltpu.VMEM((experts_local, width, hidden), low),
             pltpu.VMEM((experts_local, width, hidden), low),
             pltpu.VMEM((experts_local, hidden, width), low),
-            pltpu.VMEM((8, rows, wide), low),
+            pltpu.VMEM((8 * rows, wide), low),
             pltpu.VMEM((rows, width), low),
             pltpu.VMEM((rows, inner), low),
             pltpu.VMEM((rows, inner), low),
@@ -510,17 +687,21 @@
             pltpu.VMEM((rows, width), low),
             pltpu.VMEM((rows // chunks, wide), jnp.float32),
             pltpu.VMEM((8, rows, wide), low),
-            pltpu.VMEM((4, rows, wide), low),
+            pltpu.VMEM((3, rows, wide), low),
+            pltpu.VMEM((rows, wide), low),
             pltpu.VMEM((5, rows, wide), low),
             dma((3,)),
             dma,
             dma,
             dma((4,)),
+            dma((2, 2)),
+            dma((2, 2)),
             dma((8,)),
-            dma((8,)),
-            dma((9,)),
-            dma((4, chunks)),
-            dma((4, chunks)),
+            dma((10,)),
+            dma((3, chunks)),
+            dma((3, chunks)),
+            dma((chunks,)),
+            dma((chunks,)),
             dma((5, chunks)),
             dma((3, chunks)),
         ],
@@ -528,7 +709,7 @@
             collective_id=collective, has_side_effects=True, vmem_limit_bytes=60 << 20
         ),
         cost_estimate=pl.CostEstimate(
-            flops=2 * 6 * 8 * rows * width * inner, bytes_accessed=64 << 20, transcendentals=8 * rows * inner
+            flops=2 * 9 * 8 * rows * width * inner, bytes_accessed=64 << 20, transcendentals=8 * rows * inner
         ),
     )(own_rows, cot_all, gate_w, up_w, down_w)
 
@@ -627,8 +808,8 @@
     cosine,
     sine,
     gathered,
-    query_pre,
-    key_pre,
+    query_unit,
+    key_unit,
     query_low,
     key_low,
     value_low,
@@ -744,12 +925,15 @@
         values = rows_v[block]
         for which, gain in ((0, query_gain), (1, key_gain)):
             pre = jnp.dot(values, weights_v[which], preferred_element_type=jnp.float32)
-            pre_v[which, area] = pre
             for h in range(heads):
                 span = slice(h * 128, (h + 1) * 128)
                 head = pre[:, span]
                 scale = lax.rsqrt(jnp.mean(head * head, axis=-1, keepdims=True) + epsilon)
-                normed = head * scale * gain[...]
+                unit = head * scale
+                pre_v[which, area, span] = unit.astype(jnp.bfloat16)
+                lane = 4 + which * 4 + h
+                log_v[area, lane : lane + 1] = scale
+                normed = unit * gain[...]
                 turned = normed * cosine[area] + pltpu.roll(normed, 64, 1) * sine[area]
                 low_v[which, area, span] = turned.astype(jnp.bfloat16)
         low_v[2, area] = jnp.dot(
@@ -760,8 +944,8 @@
     lax.fori_loop(0, 4, project, 0)
     stores = [
         pltpu.make_async_copy(rows_v, gathered, store_sem.at[0]),
-        pltpu.make_async_copy(pre_v.at[0], query_pre, store_sem.at[1]),
-        pltpu.make_async_copy(pre_v.at[1], key_pre, store_sem.at[2]),
+        pltpu.make_async_copy(pre_v.at[0], query_unit, store_sem.at[1]),
+        pltpu.make_async_copy(pre_v.at[1], key_unit, store_sem.at[2]),
         pltpu.make_async_copy(low_v.at[0], query_low, store_sem.at[3]),
         pltpu.make_async_copy(low_v.at[1], key_low, store_sem.at[4]),
         pltpu.make_async_copy(low_v.at[2], value_low, store_sem.at[5]),
@@ -867,8 +1051,8 @@
         name="attention_forward",
         out_shape=(
             jax.ShapeDtypeStruct((4, rows, width), low),
-            jax.ShapeDtypeStruct((length, local), full),
-            jax.ShapeDtypeStruct((length, local), full),
+            jax.ShapeDtypeStruct((length, local), low),
+            jax.ShapeDtypeStruct((length, local), low),
             jax.ShapeDtypeStruct((length, local), low),
             jax.ShapeDtypeStruct((length, local), low),
             jax.ShapeDtypeStruct((length, local), low),
@@ -883,7 +1067,7 @@
             pltpu.VMEM((4, rows, width), low),
             pltpu.VMEM((3, width, local), low),
             pltpu.VMEM((local, width), low),
-            pltpu.VMEM((2, length, local), full),
+            pltpu.VMEM((2, length, local), low),
             pltpu.VMEM((3, length, local), low),
             pltpu.VMEM((length, local), low),
             pltpu.VMEM((length, 128), full),
@@ -910,164 +1094,423 @@
     )(own, cot, *weights, out_w, *gains, *tables)
 
 
-def scatter_kernel(
-    count,
-    *refs,
+def attention_back_kernel(
+    branch,
+    gathered,
+    query_unit,
+    key_unit,
+    query_low,
+    key_low,
+    value_low,
+    attended,
+    log_sums,
+    query_w,
+    key_w,
+    value_w,
+    out_w,
+    query_gain,
+    key_gain,
+    cosine,
+    sine,
+    rows_grad,
+    out_total,
+    value_total,
+    key_total,
+    query_total,
+    gain_sums,
+    branch_v,
+    rows_v,
+    weights_v,
+    out_v,
+    unit_v,
+    low_v,
+    log_v,
+    grads_v,
+    key_acc,
+    value_acc,
+    scattered,
+    side_in,
+    line_in,
+    own_part,
+    core_in,
+    across_in,
+    load_sem,
+    store_sem,
+    branch_recv,
+    branch_send,
+    part_recv,
+    part_send,
+    side_recv,
+    side_send,
+    line_recv,
+    line_send,
 ):
-    parts, totals = refs[:count], refs[count : 2 * count]
-    own, side_in, line_in, own_sem, side_recv, side_send, line_recv, line_send = refs[2 * count :]
     position = lax.axis_index("expert")
-    peer = lax.axis_index("tensor")
+    t = lax.axis_index("tensor")
     z = position // 2
     x = position % 2
+    y = t // 2
+    core = t % 2
+    near = y * 2 + 1 - core
+    across = (1 - y) * 2 + core
+    opposite = (1 - y) * 2 + 1 - core
+    rows = branch.shape[0]
+    local = out_v.shape[0]
+    heads = local // 128
+    kinds = scattered.shape[0]
+    factor = 1.0 / math.sqrt(128.0)
     middle = (z == 1) | (z == 2)
-    line_slots = [
-        z,
-        pick(z, [1, 0, 3, 2]),
-        pick(z, [2, 2, 1, 1]),
-        pick(z, [3, 3, 0, 0]),
+    mesh_ids = pl.DeviceIdType.MESH
+    slots = [z, pick(z, [1, 0, 3, 2]), pick(z, [2, 2, 1, 1]), pick(z, [3, 3, 0, 0])]
+
+    loads = [
+        pltpu.make_async_copy(branch, branch_v.at[t], load_sem.at[0]),
+        pltpu.make_async_copy(out_w, out_v, load_sem.at[1]),
+        pltpu.make_async_copy(query_low, low_v.at[0], load_sem.at[2]),
+        pltpu.make_async_copy(key_low, low_v.at[1], load_sem.at[3]),
+        pltpu.make_async_copy(value_low, low_v.at[2], load_sem.at[4]),
+        pltpu.make_async_copy(log_sums, log_v, load_sem.at[5]),
+        pltpu.make_async_copy(query_unit, unit_v.at[0], load_sem.at[6]),
+        pltpu.make_async_copy(key_unit, unit_v.at[1], load_sem.at[7]),
+        pltpu.make_async_copy(attended, low_v.at[3], load_sem.at[8]),
+        pltpu.make_async_copy(gathered, rows_v, load_sem.at[9]),
+        pltpu.make_async_copy(query_w, weights_v.at[0], load_sem.at[10]),
+        pltpu.make_async_copy(key_w, weights_v.at[1], load_sem.at[11]),
+        pltpu.make_async_copy(value_w, weights_v.at[2], load_sem.at[12]),
     ]
-    mesh_ids = pl.DeviceIdType.MESH
-
-    def device(zz, xx):
-        return (zz * 2 + xx, peer)
-
-    own_copies = [
-        pltpu.make_async_copy(parts[c].at[line_slots[k] * 2 + x], own.at[k, c], own_sem.at[k, c])
-        for k in (3, 2, 1, 0)
-        for c in range(count)
-    ]
-    for copy in own_copies:
-        copy.start()
+    for load in loads:
+        load.start()
 
     barrier = pltpu.get_barrier_semaphore()
-    pl.semaphore_signal(barrier, inc=1, device_id=device(z, 1 - x), device_id_type=mesh_ids)
+    for place in ((position, near), (position, across), (z * 2 + 1 - x, t)):
+        pl.semaphore_signal(barrier, inc=1, device_id=place, device_id_type=mesh_ids)
 
     @pl.when(z < 3)
     def _():
-        pl.semaphore_signal(barrier, inc=1, device_id=device(z + 1, x), device_id_type=mesh_ids)
+        pl.semaphore_signal(barrier, inc=1, device_id=(position + 2, t), device_id_type=mesh_ids)
 
     @pl.when(z > 0)
     def _():
-        pl.semaphore_signal(barrier, inc=1, device_id=device(z - 1, x), device_id_type=mesh_ids)
-
-    pl.semaphore_wait(barrier, 2 + middle.astype(jnp.int32))
+        pl.semaphore_signal(barrier, inc=1, device_id=(position - 2, t), device_id_type=mesh_ids)
+
+    pl.semaphore_wait(barrier, 4 + middle.astype(jnp.int32))
+
+    def branch_copy(source, block, index, to):
+        return pltpu.make_async_remote_copy(
+            src_ref=source,
+            dst_ref=branch_v.at[block],
+            send_sem=branch_send.at[index - 1],
+            recv_sem=branch_recv.at[index - 1],
+            device_id=(position, to),
+            device_id_type=mesh_ids,
+        )
+
+    to_across = branch_copy(branch, t, 2, across)
+    to_near = branch_copy(branch, t, 1, near)
+    forward = branch_copy(branch_v.at[across], across, 3, near)
+    to_across.start()
+    to_near.start()
 
     def side_copy(k, c):
         return pltpu.make_async_remote_copy(
-            src_ref=parts[c].at[pick(k, line_slots) * 2 + 1 - x],
-            dst_ref=side_in.at[k, c],
-            send_sem=side_send.at[k, c],
-            recv_sem=side_recv.at[k, c],
-            device_id=device(z, 1 - x),
+            src_ref=scattered.at[c, pick(k, slots) * 2 + 1 - x],
+            dst_ref=side_in.at[c, k],
+            send_sem=side_send.at[c, k],
+            recv_sem=side_recv.at[c, k],
+            device_id=(z * 2 + 1 - x, t),
             device_id_type=mesh_ids,
         )
 
     def line_slot(k):
-        target = pick(k, line_slots)
+        target = pick(k, slots)
         return jnp.where(target < z, target, target + 1)
 
     def line_copy(k, c):
-        target = jnp.where(pick(k, line_slots) < z, z - 1, z + 1)
+        target = jnp.where(pick(k, slots) < z, z - 1, z + 1)
         return pltpu.make_async_remote_copy(
-            src_ref=own.at[k, c],
-            dst_ref=line_in.at[line_slot(k), c],
-            send_sem=line_send.at[k - 1, c],
-            recv_sem=line_recv.at[line_slot(k), c],
-            device_id=device(jnp.clip(target, 0, 3), x),
+            src_ref=scattered.at[c, pick(k, slots) * 2 + x],
+            dst_ref=line_in.at[c, line_slot(k)],
+            send_sem=line_send.at[c, k - 1],
+            recv_sem=line_recv.at[c, line_slot(k)],
+            device_id=(jnp.clip(target, 0, 3) * 2 + x, t),
             device_id_type=mesh_ids,
         )
 
     def line_wait(slot, c):
         pltpu.make_async_remote_copy(
-            src_ref=own.at[0, c],
-            dst_ref=line_in.at[slot, c],
-            send_sem=line_send.at[0, c],
-            recv_sem=line_recv.at[slot, c],
-            device_id=device(z, 1 - x),
+            src_ref=scattered.at[c, position],
+            dst_ref=line_in.at[c, slot],
+            send_sem=line_send.at[c, 0],
+            recv_sem=line_recv.at[c, slot],
+            device_id=(z * 2 + 1 - x, t),
             device_id_type=mesh_ids,
         ).wait_recv()
 
     def send_order(i):
         return jnp.where(middle, pick(i, [3, 1, 2, 0]), pick(i, [3, 2, 1, 0]))
 
-    def start_side(i, carry):
-        for c in range(count):
+    def start_side(c):
+        def one(i, carry):
             side_copy(send_order(i), c).start()
+            return carry
+
+        lax.fori_loop(0, 4, one, 0)
+
+    def weight_part(c, left, right):
+        for d in range(8 // 2):
+            span = pl.ds(d * 512, 512)
+            product = jnp.zeros((512, local), jnp.float32)
+            for b in range(4):
+                product = product + lax.dot_general(
+                    left[b, :, span],
+                    right[pl.ds(b * rows, rows)],
+                    contract_first,
+                    preferred_element_type=jnp.float32,
+                )
+            scattered[c, 2 * d] = product[:256].astype(jnp.bfloat16)
+            scattered[c, 2 * d + 1] = product[256:].astype(jnp.bfloat16)
+
+    gain_sums[...] = jnp.zeros_like(gain_sums)
+    for load in loads[:9]:
+        load.wait()
+
+    def norm_back(turned, which, area, h, gain):
+        span = slice(h * 128, (h + 1) * 128)
+        grad = turned * cosine[area] - pltpu.roll(turned, 64, 1) * sine[area]
+        unit = unit_v[which, area, span].astype(jnp.float32)
+        gain_sums[which : which + 1] += jnp.sum(grad * unit, axis=0, keepdims=True)
+        weighted = grad * gain[...]
+        inner = jnp.mean(weighted * unit, axis=-1, keepdims=True)
+        lane = 4 + which * 4 + h
+        grads_v[which, area, span] = (
+            log_v[area, lane : lane + 1] * (weighted - unit * inner)
+        ).astype(jnp.bfloat16)
+
+    def attend(i, carry):
+        block = pick(i, [t, near, across, opposite])
+
+        @pl.when(i == 1)
+        def _():
+            to_near.wait_recv()
+
+        @pl.when(i == 2)
+        def _():
+            to_across.wait_recv()
+            forward.start()
+
+        @pl.when(i == 3)
+        def _():
+            forward.wait_recv()
+            weight_part(0, branch_v, low_v.at[3])
+            start_side(0)
+
+        area = pl.ds(block * rows, rows)
+        mixed_grad = lax.dot_general(
+            branch_v[block], out_v[...], contract_last, preferred_element_type=jnp.float32
+        ).astype(jnp.bfloat16)
+        for h in range(heads):
+            span = slice(h * 128, (h + 1) * 128)
+            query = low_v[0, area, span]
+            key = low_v[1, :, span]
+            grad = mixed_grad[:, span]
+            scores = lax.dot_general(query, key, contract_last, preferred_element_type=jnp.float32)
+            probs = jnp.exp(scores * factor - log_v[area, h : h + 1])
+            prob_grad = lax.dot_general(
+                grad, low_v[2, :, span], contract_last, preferred_element_type=jnp.float32
+            )
+            delta = jnp.sum(probs * prob_grad, axis=-1, keepdims=True)
+            score_grad = (probs * (prob_grad - delta)).astype(jnp.bfloat16)
+            query_grad = jnp.dot(score_grad, key, preferred_element_type=jnp.float32) * factor
+            key_part = lax.dot_general(
+                score_grad, query, contract_first, preferred_element_type=jnp.float32
+            )
+            value_part = lax.dot_general(
+                probs.astype(jnp.bfloat16), grad, contract_first, preferred_element_type=jnp.float32
+            )
+            first = i == 0
+            key_acc[:, span] = jnp.where(first, 0.0, key_acc[:, span]) + key_part
+            value_acc[:, span] = jnp.where(first, 0.0, value_acc[:, span]) + value_part
+            norm_back(query_grad, 0, area, h, query_gain)
         return carry
 
-    lax.fori_loop(0, 4, start_side, 0)
-    for copy in own_copies:
-        copy.wait()
-
-    def relay(i, carry):
-        k = send_order(i)
-        for c in range(count):
-            side_copy(k, c).wait_recv()
-            own[k, c] = (
-                own[k, c].astype(jnp.float32) + side_in[k, c].astype(jnp.float32)
+    key_acc[...] = jnp.zeros_like(key_acc)
+    value_acc[...] = jnp.zeros_like(value_acc)
+    lax.fori_loop(0, 4, attend, 0)
+    for load in loads[9:]:
+        load.wait()
+    grads_v[2] = value_acc[...].astype(jnp.bfloat16)
+    weight_part(1, rows_v, grads_v.at[2])
+    start_side(1)
+
+    def key_back(b, carry):
+        area = pl.ds(b * rows, rows)
+        for h in range(heads):
+            norm_back(key_acc[area, h * 128 : (h + 1) * 128] * factor, 1, area, h, key_gain)
+        return carry
+
+    lax.fori_loop(0, 4, key_back, 0)
+    weight_part(2, rows_v, grads_v.at[1])
+    start_side(2)
+    weight_part(3, rows_v, grads_v.at[0])
+    start_side(3)
+
+    def part_copy(source, target, index, to):
+        return pltpu.make_async_remote_copy(
+            src_ref=source,
+            dst_ref=target,
+            send_sem=part_send.at[index],
+            recv_sem=part_recv.at[index],
+            device_id=(position, to),
+            device_id_type=mesh_ids,
+        )
+
+    for copy in (to_across, to_near, forward):
+        copy.wait_send()
+    core_first = part_copy(branch_v.at[0], core_in.at[0], 0, near)
+    across_copy = part_copy(branch_v.at[1], across_in, 1, across)
+    core_second = part_copy(branch_v.at[2], core_in.at[1], 2, near)
+
+    def relay(k, c):
+        block = pick(k, slots) * 2 + x
+        side_copy(k, c).wait_recv()
+        scattered[c, block] = (
+            scattered[c, block].astype(jnp.float32) + side_in[c, k].astype(jnp.float32)
+        ).astype(jnp.bfloat16)
+
+        @pl.when(middle)
+        def _():
+            line_wait(line_slot(k), c)
+            scattered[c, block] = (
+                scattered[c, block].astype(jnp.float32) + line_in[c, line_slot(k)].astype(jnp.float32)
             ).astype(jnp.bfloat16)
 
-            @pl.when(middle)
-            def _(c=c):
-                line_wait(line_slot(k), c)
-                own[k, c] = (
-                    own[k, c].astype(jnp.float32) + line_in[line_slot(k), c].astype(jnp.float32)
-                ).astype(jnp.bfloat16)
-
-            line_copy(k, c).start()
+        line_copy(k, c).start()
+
+    def relays(c):
+        def one(i, carry):
+            relay(send_order(i), c)
+            return carry
+
+        lax.fori_loop(0, 3, one, 0)
+
+    def rows_part(i, carry):
+        block = pick(i, [opposite, across, near, t])
+        area = pl.ds(block * rows, rows)
+        for d in range(2):
+            span = pl.ds(d * 1024, 1024)
+            product = jnp.zeros((rows, 1024), jnp.float32)
+            for which in range(3):
+                product = product + lax.dot_general(
+                    grads_v[which, area],
+                    weights_v[which, span],
+                    contract_last,
+                    preferred_element_type=jnp.float32,
+                )
+            own_part[:, span] = product
+
+        @pl.when(i == 0)
+        def _():
+            branch_v[0] = own_part[...].astype(jnp.bfloat16)
+            core_first.start()
+
+        @pl.when(i == 1)
+        def _():
+            core_first.wait_recv()
+            branch_v[1] = (own_part[...] + core_in[0].astype(jnp.float32)).astype(jnp.bfloat16)
+            across_copy.start()
+
+        @pl.when(i == 2)
+        def _():
+            branch_v[2] = own_part[...].astype(jnp.bfloat16)
+            core_second.start()
+
         return carry
 
-    lax.fori_loop(0, 3, relay, 0)
-    for c in range(count):
-        total = totals[c]
+    lax.fori_loop(0, 4, rows_part, 0)
+    relays(0)
+    relays(1)
+    core_second.wait_recv()
+    own_part[...] += core_in[1].astype(jnp.float32)
+    across_copy.wait_recv()
+    own_part[...] += across_in[...].astype(jnp.float32)
+    last = pltpu.make_async_copy(own_part, rows_grad, store_sem)
+    last.start()
+    relays(2)
+    relays(3)
+    for c, total in enumerate((out_total, value_total, key_total, query_total)):
         side_copy(0, c).wait_recv()
-        total[...] = own[0, c].astype(jnp.float32) + side_in[0, c].astype(jnp.float32)
+        total[...] = scattered[c, position].astype(jnp.float32) + side_in[c, 0].astype(jnp.float32)
 
         @pl.when(z < 3)
         def _(c=c, total=total):
             line_wait(z, c)
-            total[...] += line_in[z, c].astype(jnp.float32)
+            total[...] += line_in[c, z].astype(jnp.float32)
 
         @pl.when(z > 0)
         def _(c=c, total=total):
             line_wait(z + 1, c)
-            total[...] += line_in[z + 1, c].astype(jnp.float32)
+            total[...] += line_in[c, z + 1].astype(jnp.float32)
 
         for k in range(4):
             side_copy(k, c).wait_send()
         for k in range(1, 4):
             line_copy(k, c).wait_send()
-
-
-def scatter_parts(parts, collective):
-    count = len(parts)
-    rows, wide = parts[0].shape[1:]
-    low = jnp.bfloat16
+    for copy in (core_first, across_copy, core_second):
+        copy.wait_send()
+    last.wait()
+
+
+def attention_backward(branch, saved, weights, out_w, gains, tables, collective):
+    rows, width = branch.shape
+    local = out_w.shape[0]
+    length = 4 * rows
+    any_space = pl.BlockSpec(memory_space=pl.ANY)
+    vector = pl.BlockSpec(memory_space=pltpu.VMEM)
+    low, full = jnp.bfloat16, jnp.float32
     dma = pltpu.SemaphoreType.DMA
     return pl.pallas_call(
-        functools.partial(scatter_kernel, count),
-        name="scatter_parts",
-        out_shape=(jax.ShapeDtypeStruct((rows, wide), jnp.float32),) * count,
-        in_specs=[pl.BlockSpec(memory_space=pl.ANY)] * count,
-        out_specs=(pl.BlockSpec(memory_space=pltpu.VMEM),) * count,
+        attention_back_kernel,
+        name="attention_backward",
+        out_shape=(jax.ShapeDtypeStruct((rows, width), full),)
+        + (jax.ShapeDtypeStruct((width // 8, local), full),) * 4
+        + (jax.ShapeDtypeStruct((8, 128), full),),
+        in_specs=[any_space] * 13 + [vector] * 4,
+        out_specs=(any_space,) + (vector,) * 5,
         scratch_shapes=[
-            pltpu.VMEM((4, count, rows, wide), low),
-            pltpu.VMEM((4, count, rows, wide), low),
-            pltpu.VMEM((5, count, rows, wide), low),
-            dma((4, count)),
-            dma((4, count)),
-            dma((4, count)),
-            dma((5, count)),
-            dma((3, count)),
+            pltpu.VMEM((4, rows, width), low),
+            pltpu.VMEM((4, rows, width), low),
+            pltpu.VMEM((3, width, local), low),
+            pltpu.VMEM((local, width), low),
+            pltpu.VMEM((2, length, local), low),
+            pltpu.VMEM((4, length, local), low),
+            pltpu.VMEM((length, 128), full),
+            pltpu.VMEM((3, length, local), low),
+            pltpu.VMEM((length, local), full),
+            pltpu.VMEM((length, local), full),
+            pltpu.VMEM((4, 8, width // 8, local), low),
+            pltpu.VMEM((4, 4, width // 8, local), low),
+            pltpu.VMEM((4, 5, width // 8, local), low),
+            pltpu.VMEM((rows, width), full),
+            pltpu.VMEM((2, rows, width), low),
+            pltpu.VMEM((rows, width), low),
+            dma((13,)),
+            dma,
+            dma((3,)),
+            dma((3,)),
+            dma((3,)),
+            dma((3,)),
+            dma((4, 4)),
+            dma((4, 4)),
+            dma((4, 5)),
+            dma((4, 3)),
         ],
         compiler_params=pltpu.CompilerParams(
-            collective_id=collective, has_side_effects=True, vmem_limit_bytes=40 << 20
+            collective_id=collective, has_side_effects=True, vmem_limit_bytes=60 << 20
         ),
         cost_estimate=pl.CostEstimate(
-            flops=8 * rows * wide * count, bytes_accessed=300 << 20, transcendentals=0
+            flops=16 * length * width * local, bytes_accessed=64 << 20, transcendentals=length * length * 4
         ),
-    )(*parts)
+    )(branch, *saved, *weights, out_w, *gains, *tables)
 
 
 def sum_kernel(own, total, incoming, recv, send):
@@ -1122,76 +1565,13 @@
     )(own)[steps]
 
 
-def weight_kernel(order, left, right, out):
-    wide = left.shape[1]
-    step = min(512, wide)
-    for d in range(out.shape[2] // step):
-        span = pl.ds(d * step, step)
-        out[0, 0, span, :] = lax.dot_general(
-            left[:, span], right[...], contract_first, preferred_element_type=jnp.float32
-        ).astype(out.dtype)
-
-
-def input_weight_parts(order, rows_all, grads, width, experts_local):
-    count, wide = rows_all.shape
-    hidden = grads.shape[1] // experts_local
-    part = hidden // 4
-    pieces = order.shape[0]
-    return pl.pallas_call(
-        weight_kernel,
-        name="input_weight_parts",
-        out_shape=jax.ShapeDtypeStruct((pieces, experts_local, width, part), jnp.bfloat16),
-        grid_spec=pltpu.PrefetchScalarGridSpec(
-            num_scalar_prefetch=1,
-            grid=(pieces, experts_local),
-            in_specs=[
-                pl.BlockSpec((count, width), lambda r, e, order: (0, 0), pipeline_mode=pl.Buffered(1)),
-                pl.BlockSpec((count, part), lambda r, e, order: (0, e * 4 + order[r])),
-            ],
-            out_specs=pl.BlockSpec((1, 1, width, part), lambda r, e, order: (r, e, 0, 0)),
-        ),
-        compiler_params=pltpu.CompilerParams(vmem_limit_bytes=48 << 20),
-        cost_estimate=pl.CostEstimate(
-            flops=2 * pieces * experts_local * count * width * part,
-            bytes_accessed=2 * count * width + 2 * pieces * experts_local * part * (count + width),
-            transcendentals=0,
-        ),
-    )(order, rows_all, grads)
-
-
-def output_weight_parts(order, hidden_all, grads, experts_local):
-    count, width = grads.shape
-    hidden = hidden_all.shape[1] // experts_local
-    part = hidden // 4
-    pieces = order.shape[0]
-    return pl.pallas_call(
-        weight_kernel,
-        name="output_weight_parts",
-        out_shape=jax.ShapeDtypeStruct((pieces, experts_local, part, width), jnp.bfloat16),
-        grid_spec=pltpu.PrefetchScalarGridSpec(
-            num_scalar_prefetch=1,
-            grid=(pieces, experts_local),
-            in_specs=[
-                pl.BlockSpec((count, part), lambda r, e, order: (0, e * 4 + order[r])),
-                pl.BlockSpec((count, width), lambda r, e, order: (0, 0), pipeline_mode=pl.Buffered(1)),
-            ],
-            out_specs=pl.BlockSpec((1, 1, part, width), lambda r, e, order: (r, e, 0, 0)),
-        ),
-        compiler_params=pltpu.CompilerParams(vmem_limit_bytes=48 << 20),
-        cost_estimate=pl.CostEstimate(
-            flops=2 * pieces * experts_local * count * width * part,
-            bytes_accessed=2 * count * width + 2 * pieces * experts_local * part * (count + width),
-            transcendentals=0,
-        ),
-    )(order, hidden_all, grads)
-
-
-def exchange(pieces_far, pieces_near):
+def exchange(pieces_far, pieces_near, axis):
     swap_core = [(0, 1), (1, 0), (2, 3), (3, 2)]
     swap_line = [(0, 2), (1, 3), (2, 0), (3, 1)]
     arrived = lax.ppermute(pieces_far, "tensor", swap_core)
-    own = pieces_near[0].astype(jnp.float32) + arrived[0].astype(jnp.float32)
-    sent = (pieces_near[1].astype(jnp.float32) + arrived[1].astype(jnp.float32)).astype(jnp.bfloat16)
+    summed = pieces_near.astype(jnp.float32) + arrived.astype(jnp.float32)
+    own = lax.index_in_dim(summed, 0, axis, keepdims=False)
+    sent = lax.index_in_dim(summed, 1, axis, keepdims=False).astype(jnp.bfloat16)
     return own + lax.ppermute(sent, "tensor", swap_line).astype(jnp.float32)
 
 
@@ -1216,52 +1596,18 @@
     model_width = tokens.shape[1]
     expert_count = lax.axis_size("expert")
     head_width = query_gain.shape[0]
-    local_heads = query_w.shape[1] // head_width
-    experts_local = gate_w.shape[0]
     experts_all = router_w.shape[1]
-    top_count = routes.shape[1]
-    hidden_width = gate_w.shape[2]
-    factor = 1.0 / math.sqrt(head_width)
     source = tokens.astype(jnp.float32)
     scale_in = inverse_rms(source)
     normed_low = (source * scale_in * norm_in).astype(jnp.bfloat16)
-    seq_len = 4 * rows_own
-    cosine, sine_table = rotary_tables(seq_len, head_width)
-    turn_cosine = jnp.concatenate([cosine[:, 0], cosine[:, 0]], axis=1)
-    turn_sine = jnp.concatenate([-sine_table[:, 0], sine_table[:, 0]], axis=1)
-    (
-        gathered,
-        query_pre,
-        key_pre,
-        query_low,
-        key_low,
-        value_low,
-        attended,
-        log_rows,
-        attn_out,
-        cot_all,
-    ) = attention_forward(
-        normed_low,
-        cotangent,
-        (query_w, key_w, value_w),
-        out_w,
-        (query_gain[None], key_gain[None]),
-        (turn_cosine, turn_sine),
-        4,
-    )
-    gathered = gathered.reshape(seq_len, model_width)
-    heads_shape = (seq_len, local_heads, head_width)
-    query_heads = query_pre.reshape(heads_shape)
-    key_heads = key_pre.reshape(heads_shape)
-    query_scale = inverse_rms(query_heads)
-    key_scale = inverse_rms(key_heads)
-    key_low = key_low.reshape(heads_shape)
-    value_heads = value_low.reshape(heads_shape)
-    block_rows = min(512, seq_len)
-    block_count = seq_len // block_rows
-    query_blocks = query_low.reshape(block_count, block_rows, local_heads, head_width)
-    log_sums = (
-        log_rows[:, :local_heads].T.reshape(local_heads, block_count, block_rows).transpose(1, 0, 2)
+    cosine, sine_table = rotary_tables(4 * rows_own, head_width)
+    tables = (
+        jnp.concatenate([cosine[:, 0], cosine[:, 0]], axis=1),
+        jnp.concatenate([-sine_table[:, 0], sine_table[:, 0]], axis=1),
+    )
+    gains = (query_gain[None], key_gain[None])
+    *saved, attn_out, cot_all = attention_forward(
+        normed_low, cotangent, (query_w, key_w, value_w), out_w, gains, tables, 1
     )
     middle = source + attn_out
     scale_mid = inverse_rms(middle)
@@ -1272,43 +1618,34 @@
     mask_float = route_mask.astype(jnp.float32)
     chosen = jnp.sum(mask_float * logits[:, None, :], axis=-1)
     gating = jax.nn.softmax(chosen, axis=-1)
-    upstream = cotangent.astype(jnp.float32)
     gates = jnp.sum(mask_float * gating[:, :, None], axis=1)
     gates_high = gates.astype(jnp.bfloat16)
     gates_low = (gates - gates_high.astype(jnp.float32)).astype(jnp.bfloat16)
     spare = jnp.zeros((rows_own, 128 - 2 * experts_all), jnp.bfloat16)
     own_rows = jnp.concatenate([mid_low, gates_high, gates_low, spare], axis=1)
-    rows_all, hidden_all, gate_all, up_all, y_all, row_total = expert_pass(
-        own_rows, cot_all, gate_w, up_w, down_w, experts_all, 1
+    _, _, y_all, row_total, far_input, near_input, far_output, near_output = expert_pass(
+        own_rows, cot_all.reshape(-1, model_width), gate_w, up_w, down_w, experts_all, 2
     )
     expert_input_grad = row_total[:, :model_width]
-    cot_all = cot_all.reshape(expert_count * rows_own, model_width)
     gate_grad_dense = (
         row_total[:, model_width : model_width + experts_all]
         + row_total[:, model_width + experts_all : model_width + 2 * experts_all]
     )
     gate_grad = jnp.sum(mask_float * gate_grad_dense[:, None, :], axis=-1)
-    count = expert_count * rows_own
-    inner_all = experts_local * hidden_width
-    rows_all = rows_all.reshape(count, own_rows.shape[1])
-    hidden_all = hidden_all.reshape(count, inner_all)
-    gate_all = gate_all.reshape(count, inner_all)
-    up_all = up_all.reshape(count, inner_all)
-    y_part = y_all.reshape(count, model_width)
-    y_sum = lax.psum_scatter(y_part, "expert", scatter_dimension=0, tiled=True)
-    output = (middle + y_sum.astype(jnp.float32)).astype(jnp.bfloat16)
-    me = lax.axis_index("tensor")
-    far = jnp.stack([me ^ 1, me ^ 3]).astype(jnp.int32)
-    near = jnp.stack([me, me ^ 2]).astype(jnp.int32)
-    gate_far = input_weight_parts(far, rows_all, gate_all, model_width, experts_local)
-    up_far = input_weight_parts(far, rows_all, up_all, model_width, experts_local)
-    down_far = output_weight_parts(far, hidden_all, cot_all, experts_local)
-    gate_near = input_weight_parts(near, rows_all, gate_all, model_width, experts_local)
-    up_near = input_weight_parts(near, rows_all, up_all, model_width, experts_local)
-    down_near = output_weight_parts(near, hidden_all, cot_all, experts_local)
     inner_gate = jnp.sum(gating * gate_grad, axis=-1, keepdims=True)
     chosen_grad = gating * (gate_grad - inner_gate)
     logit_grad = jnp.sum(chosen_grad[:, :, None] * mask_float, axis=1)
+    normed_mid_grad = expert_input_grad + lax.dot_general(
+        logit_grad, router_w, contract_last, precision=highest, preferred_element_type=jnp.float32
+    )
+    norm_mid_part = jnp.sum(normed_mid_grad * middle * scale_mid, axis=0)
+    upstream = cotangent.astype(jnp.float32)
+    middle_grad = upstream + norm_backward(normed_mid_grad, middle, scale_mid, norm_mid)
+    branch_low = middle_grad.astype(jnp.bfloat16)
+    rows_grad, out_w_turned, value_w_grad, key_w_grad, query_w_grad, gain_sums = attention_backward(
+        branch_low, saved, (query_w, key_w, value_w), out_w, gains, tables, 3
+    )
+    out_w_grad = out_w_turned.T
     router_part = lax.dot_general(
         normed_mid,
         logit_grad,
@@ -1316,128 +1653,33 @@
         precision=highest,
         preferred_element_type=jnp.float32,
     )
-    normed_mid_grad = expert_input_grad + lax.dot_general(
-        logit_grad, router_w, contract_last, precision=highest, preferred_element_type=jnp.float32
-    )
-    norm_mid_part = jnp.sum(normed_mid_grad * middle * scale_mid, axis=0)
-    middle_grad = upstream + norm_backward(normed_mid_grad, middle, scale_mid, norm_mid)
-    branch_low = middle_grad.astype(jnp.bfloat16)
-    branch_all = lax.all_gather(branch_low, "tensor", axis=0, tiled=True)
-    branch_all, gate_far, up_far = lax.optimization_barrier((branch_all, gate_far, up_far))
-    attended_grad = lax.dot_general(
-        branch_all, out_w, contract_last, preferred_element_type=jnp.float32
-    ).astype(jnp.bfloat16)
-    out_w_part = lax.dot_general(
-        attended, branch_all, contract_first, preferred_element_type=jnp.float32
-    )
-    grad_blocks = attended_grad.reshape(block_count, block_rows, local_heads, head_width)
-
-    def attend_back(carry, inputs):
-        key_total, value_total = carry
-        query_block, grad_block, log_block = inputs
-        scores = (
-            jnp.einsum("qhd,khd->hqk", query_block, key_low, preferred_element_type=jnp.float32)
-            * factor
-        )
-        probs = jnp.exp(scores - log_block[:, :, None])
-        probs_low = probs.astype(jnp.bfloat16)
-        value_total = value_total + jnp.einsum(
-            "hqk,qhd->khd", probs_low, grad_block, preferred_element_type=jnp.float32
-        )
-        prob_grad = jnp.einsum(
-            "qhd,khd->hqk", grad_block, value_heads, preferred_element_type=jnp.float32
-        )
-        delta = jnp.sum(probs * prob_grad, axis=-1, keepdims=True)
-        score_low = (probs * (prob_grad - delta)).astype(jnp.bfloat16)
-        query_part = (
-            jnp.einsum("hqk,khd->qhd", score_low, key_low, preferred_element_type=jnp.float32)
-            * factor
-        )
-        key_total = (
-            key_total
-            + jnp.einsum("hqk,qhd->khd", score_low, query_block, preferred_element_type=jnp.float32)
-            * factor
-        )
-        return ((key_total, value_total), query_part)
-
-    zero_heads = jnp.zeros((seq_len, local_heads, head_width), jnp.float32)
-    (key_grad, value_total), query_parts = lax.scan(
-        attend_back, (zero_heads, zero_heads), (query_blocks, grad_blocks, log_sums)
-    )
-    query_grad = query_parts.reshape(seq_len, local_heads, head_width)
-    value_grad_low = value_total.reshape(seq_len, local_heads * head_width).astype(jnp.bfloat16)
-    query_rot_grad = rotate_back(query_grad, cosine, sine_table)
-    key_rot_grad = rotate_back(key_grad, cosine, sine_table)
-    query_gain_part = jnp.sum(query_rot_grad * query_heads * query_scale, axis=(0, 1))
-    key_gain_part = jnp.sum(key_rot_grad * key_heads * key_scale, axis=(0, 1))
-    query_pre_grad = (
-        norm_backward(query_rot_grad, query_heads, query_scale, query_gain)
-        .reshape(seq_len, local_heads * head_width)
-        .astype(jnp.bfloat16)
-    )
-    key_pre_grad = (
-        norm_backward(key_rot_grad, key_heads, key_scale, key_gain)
-        .reshape(seq_len, local_heads * head_width)
-        .astype(jnp.bfloat16)
-    )
-    query_w_part = lax.dot_general(
-        gathered, query_pre_grad, contract_first, preferred_element_type=jnp.float32
-    )
-    key_w_part = lax.dot_general(
-        gathered, key_pre_grad, contract_first, preferred_element_type=jnp.float32
-    )
-    value_w_part = lax.dot_general(
-        gathered, value_grad_low, contract_first, preferred_element_type=jnp.float32
-    )
-    summed = lax.dot_general(
-        query_pre_grad, query_w, contract_last, preferred_element_type=jnp.float32
-    )
-    summed = summed + lax.dot_general(
-        key_pre_grad, key_w, contract_last, preferred_element_type=jnp.float32
-    )
-    rows_grad = lax.psum_scatter(
-        (
-            summed
-            + lax.dot_general(
-                value_grad_low, value_w, contract_last, preferred_element_type=jnp.float32
-            )
-        ).astype(jnp.bfloat16),
-        "tensor",
+    y_sum = lax.psum_scatter(
+        y_all.reshape(expert_count * rows_own, model_width),
+        "expert",
         scatter_dimension=0,
         tiled=True,
-    ).astype(jnp.float32)
+    )
+    output = (middle + y_sum.astype(jnp.float32)).astype(jnp.bfloat16)
+    input_parts = exchange(far_input, near_input, 1)
+    gate_w_grad, up_w_grad = input_parts[0], input_parts[1]
+    down_w_grad = exchange(far_output, near_output, 0)
     norm_in_part = jnp.sum(rows_grad * source * scale_in, axis=0)
     input_grad = middle_grad + norm_backward(rows_grad, source, scale_in, norm_in)
-    out_w_grad = lax.psum_scatter(
-        out_w_part.astype(jnp.bfloat16), "expert", scatter_dimension=1, tiled=True
-    ).astype(jnp.float32)
-    part_rows = model_width // expert_count
-    local_width = local_heads * head_width
-    query_w_grad, key_w_grad, value_w_grad = scatter_parts(
-        [
-            p.astype(jnp.bfloat16).reshape(expert_count, part_rows, local_width)
-            for p in (query_w_part, key_w_part, value_w_part)
-        ],
-        2,
-    )
-    gate_w_grad = exchange(gate_far, gate_near)
-    up_w_grad = exchange(up_far, up_near)
-    down_w_grad = exchange(down_far, down_near)
     router_w_grad = lax.psum(router_part, ("expert", "tensor"))
     small = jnp.concatenate(
         [
             norm_in_part,
-            query_gain_part,
-            key_gain_part,
             norm_mid_part,
+            gain_sums[0],
+            gain_sums[1],
             jnp.zeros((-(2 * model_width + 2 * head_width) % 1024,), jnp.float32),
         ]
     ).reshape(-1, 128)
-    sums = sum_everywhere(small, 3).reshape(-1)
+    sums = sum_everywhere(small, 4).reshape(-1)
     norm_in_grad = sums[:model_width]
-    query_gain_grad = sums[model_width : model_width + head_width]
-    key_gain_grad = sums[model_width + head_width : model_width + 2 * head_width]
-    norm_mid_grad = sums[model_width + 2 * head_width : 2 * model_width + 2 * head_width]
+    norm_mid_grad = sums[model_width : 2 * model_width]
+    query_gain_grad = sums[2 * model_width : 2 * model_width + head_width]
+    key_gain_grad = sums[2 * model_width + head_width : 2 * model_width + 2 * head_width]
     return (
         output,
         input_grad,

time: 859 us -> 733 us (0.85)
  waiting for transfers between devices: 82.1 us -> 8.45 us
  matrix products: 68.7 us -> 7.9 us
  Pallas kernels: 554 us -> 612 us
  other arithmetic: 79 us -> 45.6 us
  local copies, waits for them, and re-layouts: 44.5 us -> 29.3 us
    pallas_call x7 -> x1, Pallas kernels: 198 us -> 259 us  [attention_backward(): pl.pallas_call(attention_back_kernel, name='attention_backward', out_shap...]
    dot_general x18 -> x0, matrix products: 60.2 us -> none  [the longest x2 8.45 us: attend_back(): jnp.einsum('hqk,khd->qhd', score_low, key_low, preferred_element_type=jnp...]
    ppermute x3 -> x2, waiting for transfers between devices: 36.4 us -> 0.01 us  [exchange(): return own + lax.ppermute(sent, 'tensor', swap_line).astype(jnp.float32)]
    reduce_scatter x3 -> x1, waiting for transfers between devices: 26.7 us -> 0.01 us  [per_device(): lax.psum_scatter(y_all.reshape(expert_count * rows_own, model_width), 'ex...]
    convert_element_type x7 -> x0, other arithmetic: 22.8 us -> none  [the longest x3 12.6 us: exchange(): (pieces_near[1].astype(jnp.float32) + arrived[1].astype(jnp.float32)).ast...]
    psum x1, waiting for transfers between devices: 18.5 us -> 0.01 us  [per_device(): router_w_grad = lax.psum(router_part, ('expert', 'tensor'))]
    reshape x5 -> x0, local copies, waits for them, and re-layouts: 9.26 us -> none  [the longest x1 2.9 us: per_device(): key_heads = key_pre.reshape(heads_shape)]
    add x1 -> x2, other arithmetic: 5.51 us -> 14.1 us  [exchange(): summed = pieces_near.astype(jnp.float32) + arrived.astype(jnp.float32)]
  transfers between devices with their start and end apart: 11 -> 6, of which waited for: 3 -> 1; matrix products, arithmetic and copies ran while one was open for 12% -> 8% of each run, Pallas kernels for 26% -> 39%
where the time goes in v4:
time: 733 us; the launch traced here: 725 us
  Pallas kernels  612 us (83%)
  other arithmetic  45.6 us (6%)
  local copies, waits for them, and re-layouts  29.3 us (4%)
  between operations  16.4 us (2%)
  waiting for transfers between devices  8.45 us (1%)
  matrix products  7.9 us (1%)
    pallas_call x1, Pallas kernels, attention_backward(): pl.pallas_call(attention_back_kernel, name='attention_backward', out_shap...  259 us
    pallas_call x1, Pallas kernels, expert_pass(): pl.pallas_call(functools.partial(expert_kernel, experts_all), name='exper...  231 us
    pallas_call x1, Pallas kernels, attention_forward(): pl.pallas_call(attention_kernel, name='attention_forward', out_shape=(jax...  100 us
    pallas_call x1, Pallas kernels, sum_everywhere(): pl.pallas_call(sum_kernel, name='sum_everywhere', out_shape=jax.ShapeDtyp...  21.8 us
  transfers between devices with their start and end apart: 6, of which 1 were waited for; matrix products, arithmetic and copies ran while one was open for 8% of the time, Pallas kernels for 39%

profile of v4, /device:TPU:0, one launch (start us, length us, event | category | flops | bytes accessed | tf_op | source)
XLA Modules:
  0.0 725.1 jit_solution(3236453526544492073)
XLA Ops:
  8.0 0.0 copy-start
  8.0 0.0 copy-start.4
  8.0 0.0 copy-start.17
  8.1 0.0 reduce-scatter.2.cloned.1.call-start
  8.1 1.6 fusion.10
  9.7 0.0 copy-start.24
  9.7 2.0 fusion.24
  11.7 1.3 fusion.5.own
  13.0 1.3 pad_maximum_fusion
  14.3 100.0 %attention_forward.1 = (bf16[4,256,2048]{2,1,0:T(8,128)(2,1)}, bf16[1024,512]{1,0:T(8,128)(2,1)}, bf16[1024,512]{1,0:T(8,128)(2,1)}, bf16[1024,512]{1,0:T(8,128)...) custom-call(bf16[256,2048]{1,0:T(8,128)(2,1)} %fusion.5.own, ...), custom_call_target="tpu_custom_call" | custom-call | flops 8589934592 | bytes 67108864 | tf_op jit(solution)/shard_map/attention_forward/pallas_call | solution.py:1049
  114.3 0.0 copy-start.12
  114.3 2.0 multiply_reduce_fusion.2
  116.3 1.8 fusion.16
  118.2 0.0 copy-done.15
  118.2 0.0 copy-start.10
  118.3 0.0 copy-start.26
  118.4 0.1 copy.38
  118.5 0.4 copy-done.22
  118.8 0.0 copy-done.26
  118.9 0.7 copy.40
  119.6 0.1 copy.39
  119.7 0.2 fusion.17
  120.0 0.6 subtract_convert_fusion
  120.6 2.6 concatenate.14.own_rows
  123.2 231.5 %expert_pass.1 = (bf16[2048,2048]{1,0:T(8,128)(2,1)}, bf16[2,2048,2048]{2,1,0:T(8,128)(2,1)}, bf16[8,256,2048]{2,1,0:T(8,128)(2,1)}, f32[256,2176]{1,0:T(8,128)}...) custom-call(bf16[256,2176]{1,0:T(8,128)(2,1)} %concatenate.14.own_ro, ...), custom_call_target="tpu_custom_call" | custom-call | flops 154618822656 | bytes 67108864 | tf_op jit(solution)/shard_map/expert_pass/pallas_call | solution.py:665
  354.7 0.0 copy-start.23
  354.7 0.0 copy-start.27
  354.8 0.0 copy-start.13
  354.8 0.0 copy-start.20
  354.8 0.0 reduce-scatter.2.cloned.1.call-update
  354.8 0.0 all-reduce.2.cloned.1.call-start
  354.9 0.1 collective-permute-start
  355.0 0.5 collective-permute-start.2
  355.4 1.1 slice_add_fusion
  356.5 0.1 copy.41
  356.8 2.0 fusion.15
  358.8 0.0 all-reduce.2.cloned.1.call-update
  358.9 4.0 multiply_reduce_fusion
  362.9 1.3 copy-done.6
  364.2 1.8 fusion.27.branch
  366.0 8.4 %collective-permute-done.2 = bf16[2,2,256,2048]{3,2,1,0:T(8,128)(2,1)} collective-permute-done((bf16[2,2,256,2048]{3,2,1,0:T(8,128)(2,1)}, bf16[2,2,256,2048]{3,2,1,0:T(8,128)(2,1)}, u32[]{:S(2)}, u32[]{:S(2)}) %collective-permute-start.2) | collective-permute-done | bytes 4194336 | tf_op jit(solution)/shard_map/ppermute | solution.py:1571
  374.4 7.2 convert_add_fusion.1
  381.6 7.0 convert_add_fusion
  388.6 2.7 fusion.1
  391.3 3.1 collective-permute-start.1
  394.4 5.2 fusion.14
  399.6 1.9 collective-permute-start.3
  401.5 258.5 %attention_backward.1 = (f32[256,2048]{1,0:T(8,128)}, f32[256,512]{1,0:T(8,128)}, f32[256,512]{1,0:T(8,128)}, f32[256,512]{1,0:T(8,128)}, f32[256,512]{1,0:T(8,128)}, /*index=5*/f32[8,128]{1,0:T(8,128)}) custom-call(bf16[256,2048]{1,0:T(8,128)(2,1)} %fusion.27.branch, bf16[4,256,2048]{2,1,0:T(8,128)(2,1)} %get-tuple-element.40.gathered, ...), custom_call_target="tpu_custom_call" | custom-call | flops 17179869184 | bytes 67108864 | tf_op jit(solution)/shard_map/attention_backward/pallas_call | solution.py:1471
  660.1 2.1 fusion.13
  662.2 0.7 constant_dynamic-update-slice_fusion.2
  662.9 0.7 constant_dynamic-update-slice_fusion.1
  663.6 0.6 copy-done.21
  664.2 21.8 %sum_everywhere.1 = f32[6,40,128]{2,1,0:T(8,128)} custom-call(f32[40,128]{1,0:T(8,128)} %bitcast.42), custom_call_target="tpu_custom_call" | custom-call | flops 25600 | bytes 41943040 | tf_op jit(solution)/shard_map/sum_everywhere/pallas_call | solution.py:1552
  686.0 2.0 copy.43
  688.1 1.3 slice_bitcast_fusion.6
  689.3 1.3 slice_bitcast_fusion.4
  690.7 5.8 fusion.2
  696.4 5.6 fusion
  702.0 4.0 slice_bitcast_fusion.2
  706.1 5.9 fusion.9
  712.0 1.9 copy.53
  713.9 1.9 copy.54
  715.8 0.8 copy.55
  716.6 0.7 copy.56
  (64 shorter events, 0.4 us)
Async XLA Ops:
  8.0 108.3 %copy-start = (f32[2048,16]{0,1:T(8,128)S(1)}, f32[2048,16]{0,1:T(8,128)}, u32[]{:S(2)}) copy-start(f32[2048,16]{0,1:T(8,128)} %param.26) | copy-start | bytes 393220
  8.0 3.7 copy-start.4
  8.0 3.7 copy-start.17
  8.1 698.0 %reduce-scatter.2.cloned.1.call-start = ((), (), s32[]{:S(2)}) async-start(), calls=%async_computation.1 | async-start | bytes 9437184 | tf_op jit(solution)/shard_map/reduce_scatter | solution.py:1656
  9.7 4.6 copy-start.24
  114.3 2.0 copy-start.12
  116.3 3.7 copy-start.1
  116.3 1.9 copy-start.15
  116.3 3.6 copy-start.19
  118.2 1.4 copy-start.10
  118.3 0.6 copy-start.22
  118.3 0.6 copy-start.26
  354.7 1.9 copy-start.16
  354.7 1.9 copy-start.11
  354.7 1.9 copy-start.23
  354.7 1.9 copy-start.27
  354.8 2.0 copy-start.2
  354.8 2.0 copy-start.13
  354.8 2.0 copy-start.20
  354.8 357.1 %all-reduce.2.cloned.1.call-start = ((), (), s32[]{:S(2)}) async-start(), calls=%async_computation.2 | async-start | bytes 262144 | tf_op jit(solution)/shard_map/psum | solution.py:1668
  354.9 26.7 %collective-permute-start = (bf16[2,2,2,2048,256]{4,3,2,1,0:T(8,128)(2,1)}, bf16[2,2,2,2048,256]{4,3,2,1,0:T(8,128)(2,1)}, u32[]{:S(2)}, u32[]{:S(2)}) collective-permute-start(bf16[2,2,2,2048,256]{4,3,2,1,0:T(8,128)(2,1)} %get-tuple-element.55), channel_id=1, source_target_pairs={{0,1},{1,0},{2,3},{3,2},{4,5},{5,4},{6,7},{7,6},{8,9},{9,8},{10,11... | collective-permute-start | bytes 25165832 | tf_op jit(solution)/shard_map/ppermute | solution.py:1571
  355.0 19.5 %collective-permute-start.2 = (bf16[2,2,256,2048]{3,2,1,0:T(8,128)(2,1)}, bf16[2,2,256,2048]{3,2,1,0:T(8,128)(2,1)}, u32[]{:S(2)}, u32[]{:S(2)}) collective-permute-start(bf16[2,2,256,2048]{3,2,1,0:T(8,128)(2,1)} %get-tuple-element.57), channel_id=1, source_target_pairs={{0,1},{1,0},{2,3},{3,2},{4,5},{5,4},{6,7},{7,6},{8,9},{9,8},{10,11... | collective-permute-start | bytes 12582920 | tf_op jit(solution)/shard_map/ppermute | solution.py:1571
  358.8 5.4 copy-start.7
  362.9 1.3 copy-start.6
  364.2 10.2 %copy-start.8 = (bf16[2,2,256,2048]{3,2,1,0:T(8,128)(2,1)S(1)}, bf16[2,2,256,2048]{3,2,1,0:T(8,128)(2,1)}, u32[]{:S(2)}) copy-start(bf16[2,2,256,2048]{3,2,1,0:T(8,128)(2,1)} %get-tuple-element.56) | copy-start | bytes 12582916
  388.6 11.0 %copy-start.3 = (f32[2,2,2,2048,256]{4,3,2,1,0:T(8,128)}, f32[2,2,2,2048,256]{4,3,2,1,0:T(8,128)S(1)}, u32[]{:S(2)}) copy-start(f32[2,2,2,2048,256]{4,3,2,1,0:T(8,128)S(1)} %convert_add_fusion) | copy-start | bytes 50331652
  391.3 305.1 %collective-permute-start.1 = (bf16[2,2,2048,256]{3,2,1,0:T(8,128)(2,1)}, bf16[2,2,2048,256]{3,2,1,0:T(8,128)(2,1)}, u32[]{:S(2)}, u32[]{:S(2)}) collective-permute-start(bf16[2,2,2048,256]{3,2,1,0:T(8,128)(2,1)} %fusion.1), channel_id=1, source_target_pairs={{0,2},{1,3},{2,0},{3,1},{4,6},{5,7},{6,4},{7,5},{8,10},{9,11},{10,... | collective-permute-start | bytes 12582920 | tf_op jit(solution)/shard_map/ppermute | solution.py:1575
  399.6 291.1 %collective-permute-start.3 = (bf16[2,256,2048]{2,1,0:T(8,128)(2,1)}, bf16[2,256,2048]{2,1,0:T(8,128)(2,1)}, u32[]{:S(2)}, u32[]{:S(2)}) collective-permute-start(bf16[2,256,2048]{2,1,0:T(8,128)(2,1)} %fusion.14), channel_id=1, source_target_pairs={{0,2},{1,3},{2,0},{3,1},{4,6},{5,7},{6,4},{7,5},{8,10},{9,11},{10,... | collective-permute-start | bytes 6291464 | tf_op jit(solution)/shard_map/ppermute | solution.py:1575
  401.5 258.6 %copy-start.5 = (bf16[256,2048]{1,0:T(8,128)(2,1)S(1)}, bf16[256,2048]{1,0:T(8,128)(2,1)}, u32[]{:S(2)}) copy-start(bf16[256,2048]{1,0:T(8,128)(2,1)} %param.15) | copy-start | bytes 3145732
  401.5 258.6 %copy-start.18 = (f32[2048]{0:T(1024)S(1)}, f32[2048]{0:T(1024)}, u32[]{:S(2)}) copy-start(f32[2048]{0:T(1024)} %param.18) | copy-start | bytes 24580
  401.5 258.6 %copy-start.25 = (f32[256]{0:T(256)S(1)}, f32[256]{0:T(256)}, u32[]{:S(2)}) copy-start(f32[256]{0:T(256)} %copy-done.24) | copy-start | bytes 3076
  663.6 0.6 copy-start.21
  711.9 3.8 copy-start.9
  712.0 4.6 copy-start.14
Sparse Core Ops, SparseCore 0:
  354.9 159.5 reduce-scatter.1
Sparse Core Ops, SparseCore 1:
  362.3 201.7 all-reduce.1

commit v5 on v4

--- a/solution.py
+++ b/solution.py
@@ -89,9 +89,9 @@
     grads_all,
     y_all,
     total,
-    far_input,
+    core_input,
     near_input,
-    far_output,
+    core_output,
     near_output,
     gate_v,
     up_v,
@@ -113,6 +113,7 @@
     out_sem,
     item_in,
     item_out,
+    core_recv,
     gather_recv,
     gather_send,
     side_recv,
@@ -163,6 +164,8 @@
 
     barrier = pltpu.get_barrier_semaphore()
     pl.semaphore_signal(barrier, inc=1, device_id=device(z, 1 - x), device_id_type=pl.DeviceIdType.MESH)
+    core_peer = (position, y * 2 + 1 - core)
+    pl.semaphore_signal(barrier, inc=1, device_id=core_peer, device_id_type=pl.DeviceIdType.MESH)
 
     @pl.when(z < 3)
     def _():
@@ -172,7 +175,7 @@
     def _():
         pl.semaphore_signal(barrier, inc=1, device_id=device(z - 1, x), device_id_type=pl.DeviceIdType.MESH)
 
-    pl.semaphore_wait(barrier, 2 + middle.astype(jnp.int32))
+    pl.semaphore_wait(barrier, 3 + middle.astype(jnp.int32))
 
     def gather_copy(source, block, index, zz, xx):
         return pltpu.make_async_remote_copy(
@@ -483,16 +486,13 @@
         return column_y * 2 + column_core
 
     def item_source(i):
-        pair = i // 6
-        kind = (i % 6) // 2
-        e = i % 2
-        return pair, kind, e
+        return i // 6, (i % 6) // 2, i % 2
 
     def item_loads(i, act):
-        pair, kind, e = item_source(i)
+        pair_of, kind, e = item_source(i)
         slot = i % 2
         for q in range(2):
-            start = pl.multiple_of(e * hidden + columns_of(pair, q) * part, part)
+            start = pl.multiple_of(e * hidden + columns_of(pair_of, q) * part, part)
             place = gate_v.at[0, :, pl.ds(pl.multiple_of(slot * 2 * part + q * part, part), part)]
             sem = item_in.at[slot, q]
 
@@ -508,27 +508,51 @@
             def _(start=start, place=place, sem=sem):
                 act(pltpu.make_async_copy(hidden_all.at[:, pl.ds(start, part)], place, sem))
 
-    def item_stores(i, act):
-        pair, kind, e = item_source(i)
+    def core_copy(source, target, slot, number, q):
+        return pltpu.make_async_remote_copy(
+            src_ref=source,
+            dst_ref=target,
+            send_sem=item_out.at[slot, q],
+            recv_sem=core_recv.at[number, q],
+            device_id=core_peer,
+            device_id_type=pl.DeviceIdType.MESH,
+        )
+
+    def item_stores(i, starting):
+        pair_of, kind, e = item_source(i)
         slot = i % 2
+        number = i % 6
+        wide_kind = jnp.minimum(kind, 1)
         for q in range(2):
             wide_place = gate_v.at[1, :, pl.ds(pl.multiple_of(slot * 2 * part + q * part, part), part)]
             tall_place = down_v.at[slot, pl.ds(q * part, part)]
-            sem = item_out.at[slot, q]
-            for which, wide_out, tall_out in (
-                (0, far_input, far_output),
-                (1, near_input, near_output),
+
+            def far(source, target, q=q):
+                copy = core_copy(source, target, slot, number, q)
+                if starting:
+                    copy.start()
+                else:
+                    copy.wait_send()
+
+            def own(source, target, q=q):
+                copy = pltpu.make_async_copy(source, target, item_out.at[slot, q])
+                if starting:
+                    copy.start()
+                else:
+                    copy.wait()
+
+            for which, move, wide_out, tall_out in (
+                (0, far, core_input, core_output),
+                (1, own, near_input, near_output),
             ):
 
-                @pl.when((pair == which) & (kind < 2))
-                def _(wide_place=wide_place, sem=sem, wide_out=wide_out, q=q):
-                    act(
-                        pltpu.make_async_copy(wide_place, wide_out.at[jnp.minimum(kind, 1), q, e], sem)
-                    )
-
-                @pl.when((pair == which) & (kind == 2))
-                def _(tall_place=tall_place, sem=sem, tall_out=tall_out, q=q):
-                    act(pltpu.make_async_copy(tall_place, tall_out.at[q, e], sem))
+                @pl.when((pair_of == which) & (kind < 2))
+                def _(move=move, wide_place=wide_place, wide_out=wide_out, q=q):
+                    move(wide_place, wide_out.at[q, wide_kind, e])
+
+                @pl.when((pair_of == which) & (kind == 2))
+                def _(move=move, tall_place=tall_place, tall_out=tall_out, q=q):
+                    move(tall_place, tall_out.at[q, e])
 
     item_loads(0, lambda copy: copy.start())
     for copy in whole_cot:
@@ -553,7 +577,7 @@
 
             @pl.when(i > 1)
             def _():
-                item_stores(i - 2, lambda copy: copy.wait())
+                item_stores(i - 2, False)
 
         columns = pl.ds(pl.multiple_of(slot * 2 * part, 2 * part), 2 * part)
         span = pl.ds(pl.multiple_of(d * (width // 4), width // 4), width // 4)
@@ -576,7 +600,7 @@
 
         @pl.when(d == 3)
         def _():
-            item_stores(i, lambda copy: copy.start())
+            item_stores(i, True)
 
         @pl.when(at(index, 1, 1))
         def _():
@@ -602,7 +626,21 @@
 
     lax.fori_loop(0, 48, item, 0)
     for last in (10, 11):
-        item_stores(last, lambda copy: copy.wait())
+        item_stores(last, False)
+    for number in range(6):
+        for q in range(2):
+            if number < 4:
+                core_copy(
+                    gate_v.at[1, :, pl.ds(0, part)],
+                    core_input.at[q, number // 2, number % 2],
+                    0,
+                    number,
+                    q,
+                ).wait_recv()
+            else:
+                core_copy(
+                    down_v.at[0, pl.ds(0, part)], core_output.at[q, number % 2], 0, number, q
+                ).wait_recv()
 
     def finish(c, carry):
         area = pl.ds(c * chunk, chunk)
@@ -696,6 +734,7 @@
             dma((4,)),
             dma((2, 2)),
             dma((2, 2)),
+            dma((6, 2)),
             dma((8,)),
             dma((10,)),
             dma((3, chunks)),
@@ -1112,7 +1151,17 @@
     key_gain,
     cosine,
     sine,
+    sent_input,
+    sent_output,
+    y_all,
     rows_grad,
+    arrived_input,
+    arrived_output,
+    y_total,
+    y_side,
+    y_cross,
+    y_line,
+    y_sums,
     out_total,
     value_total,
     key_total,
@@ -1134,6 +1183,7 @@
     own_part,
     core_in,
     across_in,
+    y_v,
     load_sem,
     store_sem,
     branch_recv,
@@ -1144,6 +1194,15 @@
     side_send,
     line_recv,
     line_send,
+    swap_recv,
+    swap_send,
+    y_load,
+    y_store,
+    y_side_recv,
+    y_side_send,
+    y_cross_sems,
+    y_line_recv,
+    y_line_send,
 ):
     position = lax.axis_index("expert")
     t = lax.axis_index("tensor")
@@ -1211,6 +1270,20 @@
     to_across.start()
     to_near.start()
 
+    swaps = [
+        pltpu.make_async_remote_copy(
+            src_ref=sent,
+            dst_ref=arrived,
+            send_sem=swap_send.at[i],
+            recv_sem=swap_recv.at[i],
+            device_id=(position, across),
+            device_id_type=mesh_ids,
+        )
+        for i, (sent, arrived) in enumerate(
+            ((sent_input, arrived_input), (sent_output, arrived_output))
+        )
+    ]
+
     def side_copy(k, c):
         return pltpu.make_async_remote_copy(
             src_ref=scattered.at[c, pick(k, slots) * 2 + 1 - x],
@@ -1248,6 +1321,113 @@
 
     def send_order(i):
         return jnp.where(middle, pick(i, [3, 1, 2, 0]), pick(i, [3, 2, 1, 0]))
+
+    pair = z + 1 - 2 * (z % 2)
+    ends = (z == 0) | (z == 3)
+
+    def y_remote(source, target, send_sem, recv_sem, zz, xx):
+        return pltpu.make_async_remote_copy(
+            src_ref=source,
+            dst_ref=target,
+            send_sem=send_sem,
+            recv_sem=recv_sem,
+            device_id=(zz * 2 + xx, t),
+            device_id_type=mesh_ids,
+        )
+
+    def y_block(k, xx):
+        return y_all.at[slots[k] * 2 + xx]
+
+    def y_side_copy(k):
+        slot = max(k - 1, 0)
+        source = y_sums.at[0] if k == 0 else y_block(k, 1 - x)
+        return y_remote(
+            source, y_side.at[slot], y_side_send.at[slot], y_side_recv.at[slot], z, 1 - x
+        )
+
+    def y_cross_copy():
+        return y_remote(
+            y_block(1, 1 - x), y_cross, y_cross_sems.at[0], y_cross_sems.at[1], pair, x
+        )
+
+    def y_line_copy(k, source):
+        target = jnp.where(slots[k] < z, z - 1, z + 1)
+        return y_remote(
+            source,
+            y_line.at[line_slot(k)],
+            y_line_send.at[k - 1],
+            y_line_recv.at[line_slot(k)],
+            jnp.clip(target, 0, 3),
+            x,
+        )
+
+    def y_line_wait(slot):
+        y_remote(
+            y_all.at[0], y_line.at[slot], y_line_send.at[0], y_line_recv.at[slot], z, 1 - x
+        ).wait_recv()
+
+    def y_add(target, sources):
+        half = rows // 2
+        for part in range(2):
+            area = pl.ds(part * half, half)
+
+            def load(i, source, area=area):
+                return pltpu.make_async_copy(source.at[area], y_v.at[i], y_load.at[i])
+
+            for i, (source, needed) in enumerate(sources):
+                if needed is None:
+                    load(i, source).start()
+                else:
+
+                    @pl.when(needed)
+                    def _(i=i, source=source, load=load):
+                        load(i, source).start()
+
+            for i, (source, needed) in enumerate(sources):
+                if needed is None:
+                    load(i, source).wait()
+                else:
+
+                    @pl.when(needed)
+                    def _(i=i, source=source, load=load):
+                        load(i, source).wait()
+
+            for i, (source, needed) in enumerate(sources[1:], 1):
+
+                def add(i=i):
+                    y_v[0] = (y_v[0].astype(jnp.float32) + y_v[i].astype(jnp.float32)).astype(
+                        jnp.bfloat16
+                    )
+
+                if needed is None:
+                    add()
+                else:
+                    pl.when(needed)(add)
+            store = pltpu.make_async_copy(y_v.at[0], target.at[area], y_store)
+            store.start()
+            store.wait()
+
+    def y_relay(k):
+        if k > 1:
+            y_side_copy(k).wait_recv()
+        sources = [(y_block(k, x), None)]
+        if k > 1:
+            sources.append((y_side.at[k - 1], None))
+
+        @pl.when(middle)
+        def _():
+            y_line_wait(line_slot(k))
+
+        y_add(y_sums.at[k], [*sources, (y_line.at[line_slot(k)], middle)])
+        y_line_copy(k, y_sums.at[k]).start()
+
+    y_side_copy(3).start()
+    y_cross_copy().start()
+    y_side_copy(2).start()
+
+    @pl.when(ends)
+    def _():
+        y_line_copy(1, y_block(1, x)).start()
 
     def start_side(c):
         def one(i, carry):
@@ -1297,6 +1477,13 @@
         def _():
             to_across.wait_recv()
             forward.start()
+            to_across.wait_send()
+            for swap in swaps:
+                swap.start()
+
+            @pl.when(ends)
+            def _():
+                y_relay(3)
 
         @pl.when(i == 3)
         def _():
@@ -1338,6 +1525,15 @@
     lax.fori_loop(0, 4, attend, 0)
     for load in loads[9:]:
         load.wait()
+
+    @pl.when(ends)
+    def _():
+        y_relay(2)
+
+    @pl.when(middle)
+    def _():
+        y_relay(3)
+
     grads_v[2] = value_acc[...].astype(jnp.bfloat16)
     weight_part(1, rows_v, grads_v.at[2])
     start_side(1)
@@ -1353,6 +1549,10 @@
     start_side(2)
     weight_part(3, rows_v, grads_v.at[0])
     start_side(3)
+
+    y_cross_copy().wait_recv()
+    y_add(y_sums.at[0], [(y_block(0, 1 - x), None), (y_cross, None)])
+    y_side_copy(0).start()
 
     def part_copy(source, target, index, to):
         return pltpu.make_async_remote_copy(
@@ -1364,7 +1564,7 @@
             device_id_type=mesh_ids,
         )
 
-    for copy in (to_across, to_near, forward):
+    for copy in (to_near, forward):
         copy.wait_send()
     core_first = part_copy(branch_v.at[0], core_in.at[0], 0, near)
     across_copy = part_copy(branch_v.at[1], across_in, 1, across)
@@ -1428,6 +1628,12 @@
 
     lax.fori_loop(0, 4, rows_part, 0)
     relays(0)
+
+    @pl.when(middle)
+    def _():
+        y_relay(1)
+        y_relay(2)
+
     relays(1)
     core_second.wait_recv()
     own_part[...] += core_in[1].astype(jnp.float32)
@@ -1436,6 +1642,25 @@
     last = pltpu.make_async_copy(own_part, rows_grad, store_sem)
     last.start()
     relays(2)
+    y_side_copy(0).wait_recv()
+
+    @pl.when(z < 3)
+    def _():
+        y_line_wait(z)
+
+    @pl.when(z > 0)
+    def _():
+        y_line_wait(z + 1)
+
+    y_add(
+        y_total,
+        [
+            (y_all.at[position], None),
+            (y_side.at[0], None),
+            (y_line.at[z], z < 3),
+            (y_line.at[z + 1], z > 0),
+        ],
+    )
     relays(3)
     for c, total in enumerate((out_total, value_total, key_total, query_total)):
         side_copy(0, c).wait_recv()
@@ -1458,9 +1683,16 @@
     for copy in (core_first, across_copy, core_second):
         copy.wait_send()
     last.wait()
-
-
-def attention_backward(branch, saved, weights, out_w, gains, tables, collective):
+    for swap in swaps:
+        swap.wait()
+    for k in (0, 2, 3):
+        y_side_copy(k).wait_send()
+    y_cross_copy().wait_send()
+    for k in (1, 2, 3):
+        y_line_copy(k, y_sums.at[k]).wait_send()
+
+
+def attention_backward(branch, saved, weights, out_w, gains, tables, sent, y_all, collective):
     rows, width = branch.shape
     local = out_w.shape[0]
     length = 4 * rows
@@ -1472,10 +1704,18 @@
         attention_back_kernel,
         name="attention_backward",
         out_shape=(jax.ShapeDtypeStruct((rows, width), full),)
+        + tuple(jax.ShapeDtypeStruct(array.shape, array.dtype) for array in sent)
+        + (
+            jax.ShapeDtypeStruct((rows, width), low),
+            jax.ShapeDtypeStruct((3, rows, width), low),
+            jax.ShapeDtypeStruct((rows, width), low),
+            jax.ShapeDtypeStruct((5, rows, width), low),
+            jax.ShapeDtypeStruct((4, rows, width), low),
+        )
         + (jax.ShapeDtypeStruct((width // 8, local), full),) * 4
         + (jax.ShapeDtypeStruct((8, 128), full),),
-        in_specs=[any_space] * 13 + [vector] * 4,
-        out_specs=(any_space,) + (vector,) * 5,
+        in_specs=[any_space] * 13 + [vector] * 4 + [any_space] * 3,
+        out_specs=(any_space,) * 8 + (vector,) * 5,
         scratch_shapes=[
             pltpu.VMEM((4, rows, width), low),
             pltpu.VMEM((4, rows, width), low),
@@ -1493,6 +1733,7 @@
             pltpu.VMEM((rows, width), full),
             pltpu.VMEM((2, rows, width), low),
             pltpu.VMEM((rows, width), low),
+            pltpu.VMEM((4, rows // 2, width), low),
             dma((13,)),
             dma,
             dma((3,)),
@@ -1503,6 +1744,15 @@
             dma((4, 4)),
             dma((4, 5)),
             dma((4, 3)),
+            dma((2,)),
+            dma((2,)),
+            dma((4,)),
+            dma,
+            dma((3,)),
+            dma((3,)),
+            dma((2,)),
+            dma((5,)),
+            dma((3,)),
         ],
         compiler_params=pltpu.CompilerParams(
             collective_id=collective, has_side_effects=True, vmem_limit_bytes=60 << 20
@@ -1510,7 +1760,7 @@
         cost_estimate=pl.CostEstimate(
             flops=16 * length * width * local, bytes_accessed=64 << 20, transcendentals=length * length * 4
         ),
-    )(branch, *saved, *weights, out_w, *gains, *tables)
+    )(branch, *saved, *weights, out_w, *gains, *tables, *sent, y_all)
 
 
 def sum_kernel(own, total, incoming, recv, send):
@@ -1565,14 +1815,8 @@
     )(own)[steps]
 
 
-def exchange(pieces_far, pieces_near, axis):
-    swap_core = [(0, 1), (1, 0), (2, 3), (3, 2)]
-    swap_line = [(0, 2), (1, 3), (2, 0), (3, 1)]
-    arrived = lax.ppermute(pieces_far, "tensor", swap_core)
-    summed = pieces_near.astype(jnp.float32) + arrived.astype(jnp.float32)
-    own = lax.index_in_dim(summed, 0, axis, keepdims=False)
-    sent = lax.index_in_dim(summed, 1, axis, keepdims=False).astype(jnp.bfloat16)
-    return own + lax.ppermute(sent, "tensor", swap_line).astype(jnp.float32)
+def add_three(first, second, third):
+    return first.astype(jnp.float32) + second.astype(jnp.float32) + third.astype(jnp.float32)
 
 
 def per_device(
@@ -1594,7 +1838,6 @@
 ):
     rows_own = tokens.shape[0]
     model_width = tokens.shape[1]
-    expert_count = lax.axis_size("expert")
     head_width = query_gain.shape[0]
     experts_all = router_w.shape[1]
     source = tokens.astype(jnp.float32)
@@ -1623,7 +1866,7 @@
     gates_low = (gates - gates_high.astype(jnp.float32)).astype(jnp.bfloat16)
     spare = jnp.zeros((rows_own, 128 - 2 * experts_all), jnp.bfloat16)
     own_rows = jnp.concatenate([mid_low, gates_high, gates_low, spare], axis=1)
-    _, _, y_all, row_total, far_input, near_input, far_output, near_output = expert_pass(
+    _, _, y_all, row_total, core_input, near_input, core_output, near_output = expert_pass(
         own_rows, cot_all.reshape(-1, model_width), gate_w, up_w, down_w, experts_all, 2
     )
     expert_input_grad = row_total[:, :model_width]
@@ -1642,8 +1885,26 @@
     upstream = cotangent.astype(jnp.float32)
     middle_grad = upstream + norm_backward(normed_mid_grad, middle, scale_mid, norm_mid)
     branch_low = middle_grad.astype(jnp.bfloat16)
-    rows_grad, out_w_turned, value_w_grad, key_w_grad, query_w_grad, gain_sums = attention_backward(
-        branch_low, saved, (query_w, key_w, value_w), out_w, gains, tables, 3
+    sent = (
+        (near_input[1].astype(jnp.float32) + core_input[1].astype(jnp.float32)).astype(jnp.bfloat16),
+        (near_output[1].astype(jnp.float32) + core_output[1].astype(jnp.float32)).astype(jnp.bfloat16),
+    )
+    (
+        rows_grad,
+        line_input,
+        line_output,
+        y_sum,
+        _,
+        _,
+        _,
+        _,
+        out_w_turned,
+        value_w_grad,
+        key_w_grad,
+        query_w_grad,
+        gain_sums,
+    ) = attention_backward(
+        branch_low, saved, (query_w, key_w, value_w), out_w, gains, tables, sent, y_all, 3
     )
     out_w_grad = out_w_turned.T
     router_part = lax.dot_general(
@@ -1653,16 +1914,10 @@
         precision=highest,
         preferred_element_type=jnp.float32,
     )
-    y_sum = lax.psum_scatter(
-        y_all.reshape(expert_count * rows_own, model_width),
-        "expert",
-        scatter_dimension=0,
-        tiled=True,
-    )
     output = (middle + y_sum.astype(jnp.float32)).astype(jnp.bfloat16)
-    input_parts = exchange(far_input, near_input, 1)
-    gate_w_grad, up_w_grad = input_parts[0], input_parts[1]
-    down_w_grad = exchange(far_output, near_output, 0)
+    gate_w_grad = add_three(near_input[0, 0], core_input[0, 0], line_input[0])
+    up_w_grad = add_three(near_input[0, 1], core_input[0, 1], line_input[1])
+    down_w_grad = add_three(near_output[0], core_output[0], line_output)
     norm_in_part = jnp.sum(rows_grad * source * scale_in, axis=0)
     input_grad = middle_grad + norm_backward(rows_grad, source, scale_in, norm_in)
     router_w_grad = lax.psum(router_part, ("expert", "tensor"))

time: 733 us -> 669 us (0.913)
  Pallas kernels: 612 us -> 583 us
  local copies, waits for them, and re-layouts: 29.3 us -> 15.6 us
  waiting for transfers between devices: 8.45 us -> 0.02 us
    pallas_call x1, Pallas kernels: 259 us -> 232 us  [attention_backward(): pl.pallas_call(attention_back_kernel, name='attention_backward', out_shap...]
    add x4 -> x2, other arithmetic: 25.5 us -> 13 us  [add_three(): first.astype(jnp.float32) + second.astype(jnp.float32)]
    ppermute x4 -> x0, waiting for transfers between devices: 8.41 us -> none  [the longest x2 8.4 us: exchange(): arrived = lax.ppermute(pieces_far, 'tensor', swap_core)]
    pallas_call x1, Pallas kernels: 21.8 us -> 13.8 us  [sum_everywhere(): pl.pallas_call(sum_kernel, name='sum_everywhere', out_shape=jax.ShapeDtyp...]
    convert_element_type x2 -> x0, local copies, waits for them, and re-layouts: 7.89 us -> none  [exchange(): lax.index_in_dim(summed, 1, axis, keepdims=False).astype(jnp.bfloat16)]
    convert_element_type x0 -> x2, other arithmetic: none -> 7.79 us  [the longest x1 5.24 us: per_device(): (near_output[1].astype(jnp.float32) + core_output[1].astype(jnp.float32))...]
  transfers between devices with their start and end apart: 6 -> 1, of which waited for: 1 -> 0; matrix products, arithmetic and copies ran while one was open for 8% -> 6% of each run, Pallas kernels for 39% -> 37%
where the time goes in v5:
time: 669 us; the launch traced here: 661 us
  Pallas kernels  583 us (87%)
  other arithmetic  39.4 us (6%)
  local copies, waits for them, and re-layouts  15.6 us (2%)
  between operations  15 us (2%)
  matrix products  7.94 us (1%)
    pallas_call x1, Pallas kernels, expert_pass(): pl.pallas_call(functools.partial(expert_kernel, experts_all), name='exper...  237 us
    pallas_call x1, Pallas kernels, attention_backward(): pl.pallas_call(attention_back_kernel, name='attention_backward', out_shap...  232 us
    pallas_call x1, Pallas kernels, attention_forward(): pl.pallas_call(attention_kernel, name='attention_forward', out_shape=(jax...  100 us
    pallas_call x1, Pallas kernels, sum_everywhere(): pl.pallas_call(sum_kernel, name='sum_everywhere', out_shape=jax.ShapeDtyp...  13.8 us
  transfers between devices with their start and end apart: 1, of which 0 were waited for; matrix products, arithmetic and copies ran while one was open for 6% of the time, Pallas kernels for 37%

profile of v5, /device:TPU:0, one launch (start us, length us, event | category | flops | bytes accessed | tf_op | source)
XLA Modules:
  0.0 660.8 jit_solution(4361133232342633788)
XLA Ops:
  7.2 0.0 copy-start
  7.2 0.0 copy-start.3
  7.2 0.0 copy-start.19
  7.2 0.0 all-reduce.2.cloned.1.call-start
  7.3 1.6 fusion.8
  8.9 2.0 fusion.22
  10.9 1.3 fusion.3.own
  12.2 1.3 pad_maximum_fusion
  13.5 100.0 %attention_forward.1 = (bf16[4,256,2048]{2,1,0:T(8,128)(2,1)}, bf16[1024,512]{1,0:T(8,128)(2,1)}, bf16[1024,512]{1,0:T(8,128)(2,1)}, bf16[1024,512]{1,0:T(8,128)...) custom-call(bf16[256,2048]{1,0:T(8,128)(2,1)} %fusion.3.own, ...), custom_call_target="tpu_custom_call" | custom-call | flops 8589934592 | bytes 67108864 | tf_op jit(solution)/shard_map/attention_forward/pallas_call | solution.py:1088
  113.5 0.0 copy-start.14
  113.5 2.0 multiply_reduce_fusion.2
  115.5 0.0 copy-start.17
  115.5 0.0 copy-start.21
  115.5 1.8 fusion.14
  117.3 0.0 copy-done.17
  117.4 0.0 copy-start.12
  117.5 0.0 copy-start.28
  117.5 0.1 copy.36
  117.6 0.4 copy-done.24
  118.0 0.0 copy-done.28
  118.0 0.7 copy.38
  118.8 0.1 copy.37
  118.9 0.2 fusion.15
  119.1 0.0 copy-done.1
  119.1 0.0 copy-done.21
  119.1 0.6 subtract_convert_fusion
  119.8 2.6 concatenate.14.own_rows
  122.4 0.0 copy-start.29
  122.4 0.0 copy-start.2
  122.4 0.0 copy-start.15
  122.4 0.0 copy-start.22
  122.4 237.1 %expert_pass.1 = (bf16[2048,2048]{1,0:T(8,128)(2,1)}, bf16[2,2048,2048]{2,1,0:T(8,128)(2,1)}, bf16[8,256,2048]{2,1,0:T(8,128)(2,1)}, f32[256,2176]{1,0:T(8,128)}...) custom-call(bf16[256,2176]{1,0:T(8,128)(2,1)} %concatenate.14.own_ro, ...), custom_call_target="tpu_custom_call" | custom-call | flops 154618822656 | bytes 67108864 | tf_op jit(solution)/shard_map/expert_pass/pallas_call | solution.py:703
  359.5 1.1 slice_add_fusion
  360.6 0.1 copy.39
  360.8 2.0 fusion.13
  362.9 0.0 all-reduce.2.cloned.1.call-update
  362.9 0.0 copy-start.9
  362.9 0.0 slice-start
  362.9 4.1 multiply_reduce_fusion
  367.0 0.0 copy-done.9
  367.0 0.0 slice-start.1
  367.1 1.8 fusion.25.branch
  368.9 5.2 fusion.12.sent_output
  374.1 0.7 copy-done.6
  374.8 2.5 fusion.sent_input
  377.3 231.9 %attention_backward.1 = (f32[256,2048]{1,0:T(8,128)}, bf16[2,2,2048,256]{3,2,1,0:T(8,128)(2,1)}, bf16[2,256,2048]{2,1,0:T(8,128)(2,1)}, bf16[256,2048]{1,0:T(8,1...) custom-call(bf16[256,2048]{1,0:T(8,128)(2,1)} %fusion.25.branch, ...), custom_call_target="tpu_custom_call" | custom-call | flops 17179869184 | bytes 67108864 | tf_op jit(solution)/shard_map/attention_backward/pallas_call | solution.py:1703
  609.3 6.2 bitcast_add_fusion
  615.5 0.0 copy-start.27
  615.5 6.7 %convert_add_fusion = (f32[2,2048,256]{2,1,0:T(8,128)}, f32[2,2048,256]{2,1,0:T(8,128)}) fusion(bf16[2,2,2048,256]{3,2,1,0:T(8,128)(2,1)S(1)} %copy-done.8, bf16[2,2,2,2048,256]{4,3,2,1,0:T(8,128)(2,1)} %get-tuple-element.51, bf16[2,2,2,2048,256]{4,3,2,1,0:T(8,128)(2,1)} %get-tuple-element.50), kind=kLoop, calls=%fused_computation.2 | loop fusion | flops 10485760 | bytes 20971520 | tf_op jit(solution)/shard_map/add | solution.py:1819
  622.3 0.6 fusion.11
  623.0 0.7 constant_dynamic-update-slice_fusion.2
  623.7 0.7 constant_dynamic-update-slice_fusion.1
  624.4 0.0 copy-start.23
  624.4 0.6 copy-done.23
  625.0 13.8 %sum_everywhere.1 = f32[6,40,128]{2,1,0:T(8,128)} custom-call(f32[40,128]{1,0:T(8,128)} %bitcast.40), custom_call_target="tpu_custom_call" | custom-call | flops 25600 | bytes 41943040 | tf_op jit(solution)/shard_map/sum_everywhere/pallas_call | solution.py:1802
  638.8 1.3 slice_bitcast_fusion
  640.1 5.9 fusion.7
  646.0 1.3 slice_bitcast_fusion.2
  647.3 2.0 copy.40
  649.3 1.9 copy.49
  651.3 0.8 copy.50
  652.0 0.0 copy-done.10
  652.0 0.8 copy.51
  652.8 0.7 copy.52
  (59 shorter events, 0.3 us)
Async XLA Ops:
  7.2 108.3 %copy-start = (f32[2048,16]{0,1:T(8,128)S(1)}, f32[2048,16]{0,1:T(8,128)}, u32[]{:S(2)}) copy-start(f32[2048,16]{0,1:T(8,128)} %param.26) | copy-start | bytes 393220
  7.2 3.7 copy-start.3
  7.2 3.7 copy-start.19
  7.2 642.1 %all-reduce.2.cloned.1.call-start = ((), (), s32[]{:S(2)}) async-start(), calls=%async_computation | async-start | bytes 262144 | tf_op jit(solution)/shard_map/psum | solution.py:1923
  8.9 4.6 copy-start.26
  113.5 2.0 copy-start.14
  115.4 3.7 copy-start.1
  115.5 1.9 copy-start.17
  115.5 3.6 copy-start.21
  117.4 1.4 copy-start.12
  117.4 0.6 copy-start.24
  117.5 0.6 copy-start.28
  122.4 238.3 %copy-start.18 = (s32[256,8]{0,1:T(8,128)S(1)}, s32[256,8]{0,1:T(8,128)}, u32[]{:S(2)}) copy-start(s32[256,8]{0,1:T(8,128)} %param.17) | copy-start | bytes 24580
  122.4 238.3 %copy-start.13 = (f32[256,8]{0,1:T(8,128)S(1)}, f32[256,8]{0,1:T(8,128)}, u32[]{:S(2)}) copy-start(f32[256,8]{0,1:T(8,128)} %copy-done.12) | copy-start | bytes 24580
  122.4 238.3 %copy-start.25 = (f32[256]{0:T(256)S(1)}, f32[256]{0:T(256)}, u32[]{:S(2)}) copy-start(f32[256]{0:T(256)} %copy-done.24) | copy-start | bytes 3076
  122.4 238.3 %copy-start.29 = (f32[256]{0:T(256)S(1)}, f32[256]{0:T(256)}, u32[]{:S(2)}) copy-start(f32[256]{0:T(256)} %copy-done.28) | copy-start | bytes 3076
  122.4 238.4 %copy-start.2 = (f32[256,2048]{1,0:T(8,128)S(1)}, f32[256,2048]{1,0:T(8,128)}, u32[]{:S(2)}) copy-start(f32[256,2048]{1,0:T(8,128)} %copy-done.1) | copy-start | bytes 6291460
  122.4 238.4 %copy-start.15 = (f32[2048]{0:T(1024)S(1)}, f32[2048]{0:T(1024)}, u32[]{:S(2)}) copy-start(f32[2048]{0:T(1024)} %param.25) | copy-start | bytes 24580
  122.4 238.4 %copy-start.22 = (f32[256]{0:T(256)S(1)}, f32[256]{0:T(256)}, u32[]{:S(2)}) copy-start(f32[256]{0:T(256)} %copy-done.21) | copy-start | bytes 3076
  362.9 4.1 copy-start.9
  362.9 11.2 %slice-start = ((s8[8388608]{0:T(1024)(128)(4,1)}), s8[4194304]{0:T(1024)(128)(4,1)S(1)}, s32[]{:S(2)}) async-start(s8[8388608]{0:T(1024)(128)(4,1)} %bitcast.37), calls=%async_computation.1 | async-start | bytes 8388608
  367.0 1.8 copy-start.5
  367.0 7.1 %slice-start.1 = ((s8[8388608]{0:T(1024)(128)(4,1)}), s8[4194304]{0:T(1024)(128)(4,1)S(1)}, s32[]{:S(2)}) async-start(s8[8388608]{0:T(1024)(128)(4,1)} %bitcast.37), calls=%async_computation.2 | async-start | bytes 8388608
  367.0 7.7 %copy-start.6 = (bf16[2,2,2,2048,256]{4,3,2,1,0:T(8,128)(2,1)S(1)}, bf16[2,2,2,2048,256]{4,3,2,1,0:T(8,128)(2,1)}, u32[]{:S(2)}) copy-start(bf16[2,2,2,2048,256]{4,3,2,1,0:T(8,128)(2,1)} %get-tuple-element.50) | copy-start | bytes 25165828
  609.3 6.3 copy-start.8
  615.5 6.8 %copy-start.4 = (bf16[256,2048]{1,0:T(8,128)(2,1)S(1)}, bf16[256,2048]{1,0:T(8,128)(2,1)}, u32[]{:S(2)}) copy-start(bf16[256,2048]{1,0:T(8,128)(2,1)} %param.15) | copy-start | bytes 3145732
  615.5 6.8 %copy-start.7 = (f32[256,2048]{1,0:T(8,128)S(1)}, f32[256,2048]{1,0:T(8,128)}, u32[]{:S(2)}) copy-start(f32[256,2048]{1,0:T(8,128)} %get-tuple-element.56) | copy-start | bytes 6291460
  615.5 6.8 %copy-start.20 = (f32[2048]{0:T(1024)S(1)}, f32[2048]{0:T(1024)}, u32[]{:S(2)}) copy-start(f32[2048]{0:T(1024)} %param.18) | copy-start | bytes 24580
  615.5 6.8 %copy-start.27 = (f32[256]{0:T(256)S(1)}, f32[256]{0:T(256)}, u32[]{:S(2)}) copy-start(f32[256]{0:T(256)} %copy-done.26) | copy-start | bytes 3076
  624.4 0.6 copy-start.23
  646.0 5.2 copy-start.11
  646.0 6.0 copy-start.10
  649.3 3.5 copy-start.16
Sparse Core Ops, SparseCore 0:
  363.0 132.8 all-reduce.1

commit v6 on v5

--- a/solution.py
+++ b/solution.py
@@ -93,6 +93,7 @@
     near_input,
     core_output,
     near_output,
+    cot_late,
     gate_v,
     up_v,
     down_v,
@@ -122,6 +123,8 @@
     cross_send,
     line_recv,
     line_send,
+    late_recv,
+    late_send,
 ):
     position = lax.axis_index("expert")
     peer = lax.axis_index("tensor")
@@ -315,6 +318,16 @@
     def cot_copy(step):
         return pltpu.make_async_copy(cot_all.at[block_rows(block_of(step)[2])], cot_v, cot_sem)
 
+    def late_copy():
+        return pltpu.make_async_remote_copy(
+            src_ref=cot_all.at[block_rows(slot_z(3) * 2 + x)],
+            dst_ref=cot_late,
+            send_sem=late_send,
+            recv_sem=late_recv,
+            device_id=device(z, 1 - x),
+            device_id_type=pl.DeviceIdType.MESH,
+        )
+
     def y_copy(block):
         return pltpu.make_async_copy(y_v, y_all.at[block], out_sem.at[3])
 
@@ -358,6 +371,15 @@
                 arrive(3)
 
             arrived(slot_z(1) * 2 + 1 - x)
+
+        @pl.when(step == 4)
+        def _():
+            late_copy().start()
+
+        @pl.when(step == 6)
+        def _():
+            late_copy().wait_recv()
+            pltpu.make_async_copy(cot_late, cot_v, cot_sem).start()
 
         @pl.when(step == 5)
         def _():
@@ -410,7 +432,7 @@
             ext = jnp.where(high, grad_high, ext)
             ext = jnp.where(low, gate_grad - grad_high, ext)
 
-        @pl.when(step < 7)
+        @pl.when((step < 7) & (step != 5))
         def _():
             cot_copy(step + 1).start()
 
@@ -557,6 +579,18 @@
     item_loads(0, lambda copy: copy.start())
     for copy in whole_cot:
         copy.wait()
+    late_rows = block_rows(slot_z(3) * 2 + 1 - x)
+    late_parts = [
+        pltpu.make_async_copy(
+            cot_late.at[:, pl.ds(h * hidden, hidden)], up_v.at[h, late_rows], weight_sem.at[h]
+        )
+        for h in range(2)
+    ]
+    for copy in late_parts:
+        copy.start()
+    for copy in late_parts:
+        copy.wait()
+    late_copy().wait_send()
 
     def at(index, first, gap):
         return (index >= first) & (index < first + gap * chunks) & ((index - first) % gap == 0)
@@ -710,9 +744,10 @@
             jax.ShapeDtypeStruct((rows, wide), jnp.float32),
             *(jax.ShapeDtypeStruct((2, 2, experts_local, width, hidden // 4), low),) * 2,
             *(jax.ShapeDtypeStruct((2, experts_local, hidden // 4, width), low),) * 2,
+            jax.ShapeDtypeStruct((rows, width), low),
         ),
         in_specs=[any_space] * 5,
-        out_specs=(any_space,) * 8,
+        out_specs=(any_space,) * 9,
         scratch_shapes=[
             pltpu.VMEM((experts_local, width, hidden), low),
             pltpu.VMEM((experts_local, width, hidden), low),
@@ -743,6 +778,8 @@
             dma((chunks,)),
             dma((5, chunks)),
             dma((3, chunks)),
+            dma,
+            dma,
         ],
         compiler_params=pltpu.CompilerParams(
             collective_id=collective, has_side_effects=True, vmem_limit_bytes=60 << 20
@@ -805,7 +842,8 @@
 
     def arrive(k):
         wait_block(slots[k] * 2 + x)
-        side(k).start()
+        if k < 3:
+            side(k).start()
 
         @pl.when(middle)
         def _():
@@ -826,7 +864,8 @@
             own_down().wait_send()
 
         for k in range(1, 4):
-            side(k).wait_send()
+            if k < 3:
+                side(k).wait_send()
 
             @pl.when(middle)
             def _(k=k):
@@ -1068,7 +1107,7 @@
     def _():
         gather_arrive(3)
 
-    for k in range(4):
+    for k in range(3):
         gather_side(k)
     gather_drain()
     for copy in (to_across, to_near, forward, core_first, line_copy, core_second):
@@ -1635,12 +1674,6 @@
         y_relay(2)
 
     relays(1)
-    core_second.wait_recv()
-    own_part[...] += core_in[1].astype(jnp.float32)
-    across_copy.wait_recv()
-    own_part[...] += across_in[...].astype(jnp.float32)
-    last = pltpu.make_async_copy(own_part, rows_grad, store_sem)
-    last.start()
     relays(2)
     y_side_copy(0).wait_recv()
 
@@ -1680,6 +1713,12 @@
             side_copy(k, c).wait_send()
         for k in range(1, 4):
             line_copy(k, c).wait_send()
+    core_second.wait_recv()
+    own_part[...] += core_in[1].astype(jnp.float32)
+    across_copy.wait_recv()
+    own_part[...] += across_in[...].astype(jnp.float32)
+    last = pltpu.make_async_copy(own_part, rows_grad, store_sem)
+    last.start()
     for copy in (core_first, across_copy, core_second):
         copy.wait_send()
     last.wait()
@@ -1866,7 +1905,7 @@
     gates_low = (gates - gates_high.astype(jnp.float32)).astype(jnp.bfloat16)
     spare = jnp.zeros((rows_own, 128 - 2 * experts_all), jnp.bfloat16)
     own_rows = jnp.concatenate([mid_low, gates_high, gates_low, spare], axis=1)
-    _, _, y_all, row_total, core_input, near_input, core_output, near_output = expert_pass(
+    _, _, y_all, row_total, core_input, near_input, core_output, near_output, _ = expert_pass(
         own_rows, cot_all.reshape(-1, model_width), gate_w, up_w, down_w, experts_all, 2
     )
     expert_input_grad = row_total[:, :model_width]

time: 669 us -> 619 us (0.925)
  Pallas kernels: 583 us -> 533 us
    pallas_call x1, Pallas kernels: 232 us -> 197 us  [attention_backward(): pl.pallas_call(attention_back_kernel, name='attention_backward', out_shap...]
    pallas_call x1, Pallas kernels: 100 us -> 77.2 us  [attention_forward(): pl.pallas_call(attention_kernel, name='attention_forward', out_shape=(jax...]
    pallas_call x1, Pallas kernels: 13.8 us -> 21.5 us  [sum_everywhere(): pl.pallas_call(sum_kernel, name='sum_everywhere', out_shape=jax.ShapeDtyp...]
  transfers between devices with their start and end apart: 1 -> 1, of which waited for: 0 -> 0; matrix products, arithmetic and copies ran while one was open for 6% -> 6% of each run, Pallas kernels for 37% -> 36%
where the time goes in v6:
time: 619 us; the launch traced here: 611 us
  Pallas kernels  533 us (86%)
  other arithmetic  39.4 us (6%)
  local copies, waits for them, and re-layouts  15.6 us (3%)
  between operations  15 us (2%)
  matrix products  7.94 us (1%)
    pallas_call x1, Pallas kernels, expert_pass(): pl.pallas_call(functools.partial(expert_kernel, experts_all), name='exper...  237 us
    pallas_call x1, Pallas kernels, attention_backward(): pl.pallas_call(attention_back_kernel, name='attention_backward', out_shap...  197 us
    pallas_call x1, Pallas kernels, attention_forward(): pl.pallas_call(attention_kernel, name='attention_forward', out_shape=(jax...  77.2 us
    pallas_call x1, Pallas kernels, sum_everywhere(): pl.pallas_call(sum_kernel, name='sum_everywhere', out_shape=jax.ShapeDtyp...  21.5 us
    add x2, other arithmetic, add_three(): first.astype(jnp.float32) + second.astype(jnp.float32)  13 us
  transfers between devices with their start and end apart: 1, of which 0 were waited for; matrix products, arithmetic and copies ran while one was open for 6% of the time, Pallas kernels for 36%

profile of v6, /device:TPU:0, one launch (start us, length us, event | category | flops | bytes accessed | tf_op | source)
XLA Modules:
  0.0 610.5 jit_solution(4282938949567625359)
XLA Ops:
  7.2 0.0 copy-start
  7.2 0.0 copy-start.3
  7.2 0.0 copy-start.19
  7.2 0.0 all-reduce.2.cloned.1.call-start
  7.3 1.6 fusion.8
  8.9 2.0 fusion.22
  10.9 1.3 fusion.3.own
  12.2 1.3 pad_maximum_fusion
  13.5 77.2 %attention_forward.1 = (bf16[4,256,2048]{2,1,0:T(8,128)(2,1)}, bf16[1024,512]{1,0:T(8,128)(2,1)}, bf16[1024,512]{1,0:T(8,128)(2,1)}, bf16[1024,512]{1,0:T(8,128)...) custom-call(bf16[256,2048]{1,0:T(8,128)(2,1)} %fusion.3.own, ...), custom_call_target="tpu_custom_call" | custom-call | flops 8589934592 | bytes 67108864 | tf_op jit(solution)/shard_map/attention_forward/pallas_call | solution.py:1127
  90.6 0.0 copy-start.14
  90.7 2.0 multiply_reduce_fusion.2
  92.6 0.0 copy-start.17
  92.6 0.0 copy-start.21
  92.7 0.0 copy-done
  92.7 0.0 copy-done.14
  92.7 1.8 fusion.14
  94.5 0.0 copy-done.17
  94.6 0.0 copy-start.12
  94.6 0.0 copy-start.28
  94.7 0.1 copy.36
  94.8 0.4 copy-done.24
  95.1 0.0 copy-done.28
  95.2 0.7 copy.38
  95.9 0.1 copy.37
  96.0 0.2 fusion.15
  96.3 0.6 subtract_convert_fusion
  96.9 2.6 concatenate.14.own_rows
  99.6 0.0 copy-start.29
  99.6 0.0 copy-start.2
  99.6 0.0 copy-start.15
  99.6 0.0 copy-start.22
  99.6 237.3 %expert_pass.1 = (bf16[2048,2048]{1,0:T(8,128)(2,1)}, bf16[2,2048,2048]{2,1,0:T(8,128)(2,1)}, bf16[8,256,2048]{2,1,0:T(8,128)(2,1)}, f32[256,2176]{1,0:T(8,128)}...) custom-call(bf16[256,2176]{1,0:T(8,128)(2,1)} %concatenate.14.own_ro, ...), custom_call_target="tpu_custom_call" | custom-call | flops 154618822656 | bytes 67108864 | tf_op jit(solution)/shard_map/expert_pass/pallas_call | solution.py:737
  336.9 1.1 slice_add_fusion
  338.0 0.1 copy.39
  338.0 0.0 copy-done.18
  338.2 2.0 fusion.13
  340.3 0.0 all-reduce.2.cloned.1.call-update
  340.3 0.0 copy-start.9
  340.3 0.0 slice-start
  340.3 4.1 multiply_reduce_fusion
  344.4 0.0 slice-start.1
  344.4 0.0 copy-start.6
  344.5 1.8 fusion.25.branch
  346.3 5.2 fusion.12.sent_output
  351.5 0.0 slice-done.1
  351.5 0.7 copy-done.6
  352.2 2.5 fusion.sent_input
  354.7 196.6 %attention_backward.1 = (f32[256,2048]{1,0:T(8,128)}, bf16[2,2,2048,256]{3,2,1,0:T(8,128)(2,1)}, bf16[2,256,2048]{2,1,0:T(8,128)(2,1)}, bf16[256,2048]{1,0:T(8,1...) custom-call(bf16[256,2048]{1,0:T(8,128)(2,1)} %fusion.25.branch, ...), custom_call_target="tpu_custom_call" | custom-call | flops 17179869184 | bytes 67108864 | tf_op jit(solution)/shard_map/attention_backward/pallas_call | solution.py:1742
  551.3 6.2 %bitcast_add_fusion = f32[2,256,2048]{2,1,0:T(8,128)} fusion(bf16[2,256,2048]{2,1,0:T(8,128)(2,1)} %get-tuple-element.63, bf16[2,2,256,2048]{3,2,1,0:T(8,128)(2,1)} %get-tuple-element.53, bf16[2,2,256,2048]{3,2,1,0:T(8,128)(2,1)} %get-tuple-element.52), kind=kLoop, calls=%fused_computation.4 | loop fusion | flops 5242880 | bytes 10485760 | tf_op jit(solution)/shard_map/add | solution.py:1858
  557.6 6.7 %convert_add_fusion = (f32[2,2048,256]{2,1,0:T(8,128)}, f32[2,2048,256]{2,1,0:T(8,128)}) fusion(bf16[2,2,2048,256]{3,2,1,0:T(8,128)(2,1)S(1)} %copy-done.8, bf16[2,2,2,2048,256]{4,3,2,1,0:T(8,128)(2,1)} %get-tuple-element.51, bf16[2,2,2,2048,256]{4,3,2,1,0:T(8,128)(2,1)} %get-tuple-element.50), kind=kLoop, calls=%fused_computation.2 | loop fusion | flops 10485760 | bytes 20971520 | tf_op jit(solution)/shard_map/add | solution.py:1858
  564.3 0.6 fusion.11
  565.0 0.7 constant_dynamic-update-slice_fusion.2
  565.7 0.7 constant_dynamic-update-slice_fusion.1
  566.4 0.0 copy-start.23
  566.4 0.6 copy-done.23
  567.0 21.5 %sum_everywhere.1 = f32[6,40,128]{2,1,0:T(8,128)} custom-call(f32[40,128]{1,0:T(8,128)} %bitcast.40), custom_call_target="tpu_custom_call" | custom-call | flops 25600 | bytes 41943040 | tf_op jit(solution)/shard_map/sum_everywhere/pallas_call | solution.py:1841
  588.6 1.3 slice_bitcast_fusion
  589.9 5.9 fusion.7
  595.8 1.3 slice_bitcast_fusion.2
  597.1 2.0 copy.40
  599.1 1.9 copy.49
  601.0 0.8 copy.50
  601.8 0.8 copy.51
  602.6 0.7 copy.52
  (59 shorter events, 0.3 us)
Async XLA Ops:
  7.2 85.5 %copy-start = (f32[2048,16]{0,1:T(8,128)S(1)}, f32[2048,16]{0,1:T(8,128)}, u32[]{:S(2)}) copy-start(f32[2048,16]{0,1:T(8,128)} %param.26) | copy-start | bytes 393220
  7.2 3.7 copy-start.3
  7.2 3.7 copy-start.19
  7.2 591.9 %all-reduce.2.cloned.1.call-start = ((), (), s32[]{:S(2)}) async-start(), calls=%async_computation | async-start | bytes 262144 | tf_op jit(solution)/shard_map/psum | solution.py:1962
  8.9 4.6 copy-start.26
  90.6 2.0 copy-start.14
  92.6 3.7 copy-start.1
  92.6 1.9 copy-start.17
  92.6 3.6 copy-start.21
  94.6 1.4 copy-start.12
  94.6 0.6 copy-start.24
  94.6 0.6 copy-start.28
  99.5 238.5 %copy-start.18 = (s32[256,8]{0,1:T(8,128)S(1)}, s32[256,8]{0,1:T(8,128)}, u32[]{:S(2)}) copy-start(s32[256,8]{0,1:T(8,128)} %param.17) | copy-start | bytes 24580
  99.5 238.6 %copy-start.13 = (f32[256,8]{0,1:T(8,128)S(1)}, f32[256,8]{0,1:T(8,128)}, u32[]{:S(2)}) copy-start(f32[256,8]{0,1:T(8,128)} %copy-done.12) | copy-start | bytes 24580
  99.6 238.6 %copy-start.25 = (f32[256]{0:T(256)S(1)}, f32[256]{0:T(256)}, u32[]{:S(2)}) copy-start(f32[256]{0:T(256)} %copy-done.24) | copy-start | bytes 3076
  99.6 238.6 %copy-start.29 = (f32[256]{0:T(256)S(1)}, f32[256]{0:T(256)}, u32[]{:S(2)}) copy-start(f32[256]{0:T(256)} %copy-done.28) | copy-start | bytes 3076
  99.6 238.6 %copy-start.2 = (f32[256,2048]{1,0:T(8,128)S(1)}, f32[256,2048]{1,0:T(8,128)}, u32[]{:S(2)}) copy-start(f32[256,2048]{1,0:T(8,128)} %copy-done.1) | copy-start | bytes 6291460
  99.6 238.6 %copy-start.15 = (f32[2048]{0:T(1024)S(1)}, f32[2048]{0:T(1024)}, u32[]{:S(2)}) copy-start(f32[2048]{0:T(1024)} %param.25) | copy-start | bytes 24580
  99.6 238.6 %copy-start.22 = (f32[256]{0:T(256)S(1)}, f32[256]{0:T(256)}, u32[]{:S(2)}) copy-start(f32[256]{0:T(256)} %copy-done.21) | copy-start | bytes 3076
  340.3 4.1 copy-start.9
  340.3 11.2 %slice-start = ((s8[8388608]{0:T(1024)(128)(4,1)}), s8[4194304]{0:T(1024)(128)(4,1)S(1)}, s32[]{:S(2)}) async-start(s8[8388608]{0:T(1024)(128)(4,1)} %bitcast.37), calls=%async_computation.1 | async-start | bytes 8388608
  344.4 1.8 copy-start.5
  344.4 7.1 %slice-start.1 = ((s8[8388608]{0:T(1024)(128)(4,1)}), s8[4194304]{0:T(1024)(128)(4,1)S(1)}, s32[]{:S(2)}) async-start(s8[8388608]{0:T(1024)(128)(4,1)} %bitcast.37), calls=%async_computation.2 | async-start | bytes 8388608
  344.4 7.7 %copy-start.6 = (bf16[2,2,2,2048,256]{4,3,2,1,0:T(8,128)(2,1)S(1)}, bf16[2,2,2,2048,256]{4,3,2,1,0:T(8,128)(2,1)}, u32[]{:S(2)}) copy-start(bf16[2,2,2,2048,256]{4,3,2,1,0:T(8,128)(2,1)} %get-tuple-element.50) | copy-start | bytes 25165828
  551.3 6.3 %copy-start.8 = (bf16[2,2,2048,256]{3,2,1,0:T(8,128)(2,1)S(1)}, bf16[2,2,2048,256]{3,2,1,0:T(8,128)(2,1)}, u32[]{:S(2)}) copy-start(bf16[2,2,2048,256]{3,2,1,0:T(8,128)(2,1)} %get-tuple-element.62) | copy-start | bytes 12582916
  557.6 6.8 %copy-start.4 = (bf16[256,2048]{1,0:T(8,128)(2,1)S(1)}, bf16[256,2048]{1,0:T(8,128)(2,1)}, u32[]{:S(2)}) copy-start(bf16[256,2048]{1,0:T(8,128)(2,1)} %param.15) | copy-start | bytes 3145732
  557.6 6.8 %copy-start.7 = (f32[256,2048]{1,0:T(8,128)S(1)}, f32[256,2048]{1,0:T(8,128)}, u32[]{:S(2)}) copy-start(f32[256,2048]{1,0:T(8,128)} %get-tuple-element.56) | copy-start | bytes 6291460
  557.6 6.8 %copy-start.20 = (f32[2048]{0:T(1024)S(1)}, f32[2048]{0:T(1024)}, u32[]{:S(2)}) copy-start(f32[2048]{0:T(1024)} %param.18) | copy-start | bytes 24580
  557.6 6.8 %copy-start.27 = (f32[256]{0:T(256)S(1)}, f32[256]{0:T(256)}, u32[]{:S(2)}) copy-start(f32[256]{0:T(256)} %copy-done.26) | copy-start | bytes 3076
  566.4 0.6 copy-start.23
  595.8 5.2 copy-start.11
  595.8 6.0 copy-start.10
  599.1 3.5 copy-start.16
Sparse Core Ops, SparseCore 0:
  340.4 134.2 all-reduce.1

commit v7 on v6

--- a/solution.py
+++ b/solution.py
@@ -1193,6 +1193,7 @@
     sent_input,
     sent_output,
     y_all,
+    norm_mid_part,
     rows_grad,
     arrived_input,
     arrived_output,
@@ -1205,7 +1206,7 @@
     value_total,
     key_total,
     query_total,
-    gain_sums,
+    sums,
     branch_v,
     rows_v,
     weights_v,
@@ -1223,6 +1224,8 @@
     core_in,
     across_in,
     y_v,
+    gain_sums,
+    sums_in,
     load_sem,
     store_sem,
     branch_recv,
@@ -1242,6 +1245,8 @@
     y_cross_sems,
     y_line_recv,
     y_line_send,
+    sums_recv,
+    sums_send,
 ):
     position = lax.axis_index("expert")
     t = lax.axis_index("tensor")
@@ -1291,7 +1296,9 @@
     def _():
         pl.semaphore_signal(barrier, inc=1, device_id=(position - 2, t), device_id_type=mesh_ids)
 
-    pl.semaphore_wait(barrier, 4 + middle.astype(jnp.int32))
+    distant = ((z + 2) % 4) * 2 + x
+    pl.semaphore_signal(barrier, inc=1, device_id=(distant, t), device_id_type=mesh_ids)
+    pl.semaphore_wait(barrier, 5 + middle.astype(jnp.int32))
 
     def branch_copy(source, block, index, to):
         return pltpu.make_async_remote_copy(
@@ -1490,6 +1497,8 @@
             scattered[c, 2 * d + 1] = product[256:].astype(jnp.bfloat16)
 
     gain_sums[...] = jnp.zeros_like(gain_sums)
+    sums[0] = jnp.zeros(sums.shape[1:], jnp.float32)
+    sums[0, 1:2] = norm_mid_part[...]
     for load in loads[:9]:
         load.wait()
 
@@ -1646,6 +1655,9 @@
                     preferred_element_type=jnp.float32,
                 )
             own_part[:, span] = product
+            sums[0, 0:1, span] += jnp.sum(
+                product * rows_v[block, :, span].astype(jnp.float32), axis=0, keepdims=True
+            )
 
         @pl.when(i == 0)
         def _():
@@ -1713,12 +1725,33 @@
             side_copy(k, c).wait_send()
         for k in range(1, 4):
             line_copy(k, c).wait_send()
+    sums[0, 2:3, :128] = gain_sums[0:1]
+    sums[0, 2:3, 128:256] = gain_sums[1:2]
+
+    def sums_round(i, to):
+        copy = pltpu.make_async_remote_copy(
+            src_ref=sums.at[i],
+            dst_ref=sums_in.at[i],
+            send_sem=sums_send.at[i],
+            recv_sem=sums_recv.at[i],
+            device_id=to,
+            device_id_type=mesh_ids,
+        )
+        copy.start()
+        copy.wait()
+        sums[i + 1] = sums[i] + sums_in[i]
+
+    sums_round(0, (position, near))
+    sums_round(1, (z * 2 + 1 - x, t))
+    sums_round(2, (pair * 2 + x, t))
+    sums_round(3, (distant, t))
     core_second.wait_recv()
     own_part[...] += core_in[1].astype(jnp.float32)
     across_copy.wait_recv()
     own_part[...] += across_in[...].astype(jnp.float32)
     last = pltpu.make_async_copy(own_part, rows_grad, store_sem)
     last.start()
+    sums_round(4, (position, across))
     for copy in (core_first, across_copy, core_second):
         copy.wait_send()
     last.wait()
@@ -1731,7 +1764,7 @@
         y_line_copy(k, y_sums.at[k]).wait_send()
 
 
-def attention_backward(branch, saved, weights, out_w, gains, tables, sent, y_all, collective):
+def attention_backward(branch, saved, weights, out_w, gains, tables, sent, y_all, norm_mid_part, collective):
     rows, width = branch.shape
     local = out_w.shape[0]
     length = 4 * rows
@@ -1752,8 +1785,8 @@
             jax.ShapeDtypeStruct((4, rows, width), low),
         )
         + (jax.ShapeDtypeStruct((width // 8, local), full),) * 4
-        + (jax.ShapeDtypeStruct((8, 128), full),),
-        in_specs=[any_space] * 13 + [vector] * 4 + [any_space] * 3,
+        + (jax.ShapeDtypeStruct((6, 8, width), full),),
+        in_specs=[any_space] * 13 + [vector] * 4 + [any_space] * 3 + [vector],
         out_specs=(any_space,) * 8 + (vector,) * 5,
         scratch_shapes=[
             pltpu.VMEM((4, rows, width), low),
@@ -1773,6 +1806,8 @@
             pltpu.VMEM((2, rows, width), low),
             pltpu.VMEM((rows, width), low),
             pltpu.VMEM((4, rows // 2, width), low),
+            pltpu.VMEM((8, 128), full),
+            pltpu.VMEM((5, 8, width), full),
             dma((13,)),
             dma,
             dma((3,)),
@@ -1792,6 +1827,8 @@
             dma((2,)),
             dma((5,)),
             dma((3,)),
+            dma((5,)),
+            dma((5,)),
         ],
         compiler_params=pltpu.CompilerParams(
             collective_id=collective, has_side_effects=True, vmem_limit_bytes=60 << 20
@@ -1799,59 +1836,7 @@
         cost_estimate=pl.CostEstimate(
             flops=16 * length * width * local, bytes_accessed=64 << 20, transcendentals=length * length * 4
         ),
-    )(branch, *saved, *weights, out_w, *gains, *tables, *sent, y_all)
-
-
-def sum_kernel(own, total, incoming, recv, send):
-    position = lax.axis_index("expert")
-    peer = lax.axis_index("tensor")
-    mesh_ids = pl.DeviceIdType.MESH
-
-    def flip(index, bit):
-        return index + bit - 2 * bit * ((index // bit) % 2)
-
-    partners = [
-        (position, flip(peer, 1)),
-        (position, flip(peer, 2)),
-        (flip(position, 1), peer),
-        (flip(position, 2), peer),
-        (flip(position, 4), peer),
-    ]
-    barrier = pltpu.get_barrier_semaphore()
-    for partner in partners:
-        pl.semaphore_signal(barrier, inc=1, device_id=partner, device_id_type=mesh_ids)
-    pl.semaphore_wait(barrier, len(partners))
-    total[0] = own[...]
-    for i, partner in enumerate(partners):
-        copy = pltpu.make_async_remote_copy(
-            src_ref=total.at[i],
-            dst_ref=incoming.at[i],
-            send_sem=send.at[i],
-            recv_sem=recv.at[i],
-            device_id=partner,
-            device_id_type=mesh_ids,
-        )
-        copy.start()
-        copy.wait()
-        total[i + 1] = total[i] + incoming[i]
-
-
-def sum_everywhere(own, collective):
-    steps = 5
-    return pl.pallas_call(
-        sum_kernel,
-        name="sum_everywhere",
-        out_shape=jax.ShapeDtypeStruct((steps + 1,) + own.shape, jnp.float32),
-        in_specs=[pl.BlockSpec(memory_space=pltpu.VMEM)],
-        out_specs=pl.BlockSpec(memory_space=pltpu.VMEM),
-        scratch_shapes=[
-            pltpu.VMEM((steps,) + own.shape, jnp.float32),
-            pltpu.SemaphoreType.DMA((steps,)),
-            pltpu.SemaphoreType.DMA((steps,)),
-        ],
-        compiler_params=pltpu.CompilerParams(collective_id=collective, has_side_effects=True),
-        cost_estimate=pl.CostEstimate(flops=own.size * steps, bytes_accessed=40 << 20, transcendentals=0),
-    )(own)[steps]
+    )(branch, *saved, *weights, out_w, *gains, *tables, *sent, y_all, norm_mid_part)
 
 
 def add_three(first, second, third):
@@ -1941,9 +1926,9 @@
         value_w_grad,
         key_w_grad,
         query_w_grad,
-        gain_sums,
+        sums,
     ) = attention_backward(
-        branch_low, saved, (query_w, key_w, value_w), out_w, gains, tables, sent, y_all, 3
+        branch_low, saved, (query_w, key_w, value_w), out_w, gains, tables, sent, y_all, norm_mid_part[None], 3
     )
     out_w_grad = out_w_turned.T
     router_part = lax.dot_general(
@@ -1957,23 +1942,12 @@
     gate_w_grad = add_three(near_input[0, 0], core_input[0, 0], line_input[0])
     up_w_grad = add_three(near_input[0, 1], core_input[0, 1], line_input[1])
     down_w_grad = add_three(near_output[0], core_output[0], line_output)
-    norm_in_part = jnp.sum(rows_grad * source * scale_in, axis=0)
     input_grad = middle_grad + norm_backward(rows_grad, source, scale_in, norm_in)
     router_w_grad = lax.psum(router_part, ("expert", "tensor"))
-    small = jnp.concatenate(
-        [
-            norm_in_part,
-            norm_mid_part,
-            gain_sums[0],
-            gain_sums[1],
-            jnp.zeros((-(2 * model_width + 2 * head_width) % 1024,), jnp.float32),
-        ]
-    ).reshape(-1, 128)
-    sums = sum_everywhere(small, 4).reshape(-1)
-    norm_in_grad = sums[:model_width]
-    norm_mid_grad = sums[model_width : 2 * model_width]
-    query_gain_grad = sums[2 * model_width : 2 * model_width + head_width]
-    key_gain_grad = sums[2 * model_width + head_width : 2 * model_width + 2 * head_width]
+    norm_in_grad = sums[5, 0] / norm_in
+    norm_mid_grad = sums[5, 1]
+    query_gain_grad = sums[5, 2, :head_width]
+    key_gain_grad = sums[5, 2, head_width : 2 * head_width]
     return (
         output,
         input_grad,

time: 619 us -> 612 us (0.989)
    pallas_call x1 -> x0, Pallas kernels: 21.5 us -> none  [sum_everywhere(): pl.pallas_call(sum_kernel, name='sum_everywhere', out_shape=jax.ShapeDtyp...]
    pallas_call x1, Pallas kernels: 197 us -> 215 us  [attention_backward(): pl.pallas_call(attention_back_kernel, name='attention_backward', out_shap...]
where the time goes in v7:
time: 612 us; the launch traced here: 603 us
  Pallas kernels  529 us (86%)
  other arithmetic  36.9 us (6%)
  between operations  14.7 us (2%)
  local copies, waits for them, and re-layouts  14.1 us (2%)
  matrix products  8.54 us (1%)
    pallas_call x1, Pallas kernels, expert_pass(): pl.pallas_call(functools.partial(expert_kernel, experts_all), name='exper...  237 us
    pallas_call x1, Pallas kernels, attention_backward(): pl.pallas_call(attention_back_kernel, name='attention_backward', out_shap...  215 us
    pallas_call x1, Pallas kernels, attention_forward(): pl.pallas_call(attention_kernel, name='attention_forward', out_shape=(jax...  77.2 us
    add x2, other arithmetic, add_three(): first.astype(jnp.float32) + second.astype(jnp.float32)  12.9 us
  transfers between devices with their start and end apart: 1, of which 0 were waited for; matrix products, arithmetic and copies ran while one was open for 6% of the time, Pallas kernels for 36%

profile of v7, /device:TPU:0, one launch (start us, length us, event | category | flops | bytes accessed | tf_op | source)
XLA Modules:
  0.0 603.4 jit_solution(6720517611494636915)
XLA Ops:
  7.2 0.0 copy-start
  7.2 0.0 copy-start.3
  7.2 0.0 copy-start.21
  7.2 0.0 all-reduce.2.cloned.1.call-start
  7.3 1.6 fusion.8
  8.9 0.0 copy-start.29
  8.9 2.0 fusion.20
  10.9 0.0 copy-done.3
  10.9 0.0 copy-done.21
  10.9 1.3 fusion.3.own
  12.2 1.3 pad_maximum_fusion
  13.5 0.0 copy-done.29
  13.5 77.2 %attention_forward.1 = (bf16[4,256,2048]{2,1,0:T(8,128)(2,1)}, bf16[1024,512]{1,0:T(8,128)(2,1)}, bf16[1024,512]{1,0:T(8,128)(2,1)}, bf16[1024,512]{1,0:T(8,128)...) custom-call(bf16[256,2048]{1,0:T(8,128)(2,1)} %fusion.3.own, ...), custom_call_target="tpu_custom_call" | custom-call | flops 8589934592 | bytes 67108864 | tf_op jit(solution)/shard_map/attention_forward/pallas_call | solution.py:1127
  90.6 0.0 copy-start.16
  90.7 2.0 multiply_reduce_fusion.2
  92.6 0.0 copy-start.19
  92.6 0.0 copy-start.23
  92.7 0.0 copy-done
  92.7 1.8 fusion.12
  94.5 0.0 copy-done.19
  94.6 0.0 copy-start.14
  94.6 0.0 copy-start.27
  94.7 0.1 copy.36
  94.8 0.4 copy-done.25
  95.1 0.0 copy-done.27
  95.2 0.7 copy.38
  95.9 0.1 copy.37
  96.0 0.2 fusion.13
  96.3 0.6 subtract_convert_fusion
  96.9 2.6 concatenate.11.own_rows
  99.6 0.0 copy-start.28
  99.6 0.0 copy-start.2
  99.6 0.0 copy-start.17
  99.6 0.0 copy-start.24
  99.6 237.1 %expert_pass.1 = (bf16[2048,2048]{1,0:T(8,128)(2,1)}, bf16[2,2048,2048]{2,1,0:T(8,128)(2,1)}, bf16[8,256,2048]{2,1,0:T(8,128)(2,1)}, f32[256,2176]{1,0:T(8,128)}...) custom-call(bf16[256,2176]{1,0:T(8,128)(2,1)} %concatenate.11.own_ro, ...), custom_call_target="tpu_custom_call" | custom-call | flops 154618822656 | bytes 67108864 | tf_op jit(solution)/shard_map/expert_pass/pallas_call | solution.py:737
  336.8 1.1 slice_add_fusion
  337.8 0.1 copy.39
  338.1 2.0 fusion.11
  340.1 0.0 all-reduce.2.cloned.1.call-update
  340.2 0.0 copy-start.10
  340.2 0.0 slice-start
  340.2 4.7 multiply_reduce_fusion
  344.9 0.0 copy-start.7
  344.9 1.7 fusion.23.branch
  346.6 0.0 copy-done.5
  346.6 5.2 fusion.10.sent_output
  351.9 0.0 slice-done.1
  351.9 0.8 copy-done.7
  352.7 2.5 fusion.sent_input
  355.2 214.8 %attention_backward.1 = (f32[256,2048]{1,0:T(8,128)}, bf16[2,2,2048,256]{3,2,1,0:T(8,128)(2,1)}, bf16[2,256,2048]{2,1,0:T(8,128)(2,1)}, bf16[256,2048]{1,0:T(8,1...) custom-call(bf16[256,2048]{1,0:T(8,128)(2,1)} %fusion.23.branch, ...), custom_call_target="tpu_custom_call" | custom-call | flops 17179869184 | bytes 67108864 | tf_op jit(solution)/shard_map/attention_backward/pallas_call | solution.py:1775
  570.0 6.2 %bitcast_add_fusion = f32[2,256,2048]{2,1,0:T(8,128)} fusion(bf16[2,256,2048]{2,1,0:T(8,128)(2,1)} %get-tuple-element.63, bf16[2,2,256,2048]{3,2,1,0:T(8,128)(2,1)} %get-tuple-element.53, bf16[2,2,256,2048]{3,2,1,0:T(8,128)(2,1)} %get-tuple-element.52), kind=kLoop, calls=%fused_computation.4 | loop fusion | flops 5242880 | bytes 10485760 | tf_op jit(solution)/shard_map/add | solution.py:1843
  576.2 0.0 copy-done.9
  576.2 6.7 %convert_add_fusion = (f32[2,2048,256]{2,1,0:T(8,128)}, f32[2,2048,256]{2,1,0:T(8,128)}) fusion(bf16[2,2,2048,256]{3,2,1,0:T(8,128)(2,1)S(1)} %copy-done.9, bf16[2,2,2,2048,256]{4,3,2,1,0:T(8,128)(2,1)} %get-tuple-element.51, bf16[2,2,2,2048,256]{4,3,2,1,0:T(8,128)(2,1)} %get-tuple-element.50), kind=kLoop, calls=%fused_computation.2 | loop fusion | flops 10485760 | bytes 20971520 | tf_op jit(solution)/shard_map/add | solution.py:1843
  583.0 0.4 fusion.9
  583.3 1.7 fusion.24
  585.0 0.0 copy-done.30
  585.0 3.2 fusion.7
  588.2 1.3 slice_bitcast_fusion
  589.5 0.6 div.50
  590.1 2.0 copy.40
  592.2 1.9 copy.45
  594.1 0.8 copy.46
  594.9 0.8 copy.47
  595.7 0.7 copy.48
  (56 shorter events, 0.3 us)
Async XLA Ops:
  7.2 85.5 %copy-start = (f32[2048,16]{0,1:T(8,128)S(1)}, f32[2048,16]{0,1:T(8,128)}, u32[]{:S(2)}) copy-start(f32[2048,16]{0,1:T(8,128)} %param.26) | copy-start | bytes 393220
  7.2 3.7 copy-start.3
  7.2 3.7 copy-start.21
  7.2 585.0 %all-reduce.2.cloned.1.call-start = ((), (), s32[]{:S(2)}) async-start(), calls=%async_computation | async-start | bytes 262144 | tf_op jit(solution)/shard_map/psum | solution.py:1946
  8.9 4.6 copy-start.29
  90.6 2.0 copy-start.16
  92.6 3.7 copy-start.1
  92.6 1.9 copy-start.19
  92.6 3.6 copy-start.23
  94.6 1.4 copy-start.14
  94.6 0.6 copy-start.25
  94.6 0.6 copy-start.27
  99.5 238.4 %copy-start.20 = (s32[256,8]{0,1:T(8,128)S(1)}, s32[256,8]{0,1:T(8,128)}, u32[]{:S(2)}) copy-start(s32[256,8]{0,1:T(8,128)} %param.17) | copy-start | bytes 24580
  99.5 238.4 %copy-start.15 = (f32[256,8]{0,1:T(8,128)S(1)}, f32[256,8]{0,1:T(8,128)}, u32[]{:S(2)}) copy-start(f32[256,8]{0,1:T(8,128)} %copy-done.14) | copy-start | bytes 24580
  99.6 238.4 %copy-start.26 = (f32[256]{0:T(256)S(1)}, f32[256]{0:T(256)}, u32[]{:S(2)}) copy-start(f32[256]{0:T(256)} %copy-done.25) | copy-start | bytes 3076
  99.6 238.4 %copy-start.28 = (f32[256]{0:T(256)S(1)}, f32[256]{0:T(256)}, u32[]{:S(2)}) copy-start(f32[256]{0:T(256)} %copy-done.27) | copy-start | bytes 3076
  99.6 238.5 %copy-start.2 = (f32[256,2048]{1,0:T(8,128)S(1)}, f32[256,2048]{1,0:T(8,128)}, u32[]{:S(2)}) copy-start(f32[256,2048]{1,0:T(8,128)} %copy-done.1) | copy-start | bytes 6291460
  99.6 238.5 %copy-start.17 = (f32[2048]{0:T(1024)S(1)}, f32[2048]{0:T(1024)}, u32[]{:S(2)}) copy-start(f32[2048]{0:T(1024)} %param.25) | copy-start | bytes 24580
  99.6 238.5 %copy-start.24 = (f32[256]{0:T(256)S(1)}, f32[256]{0:T(256)}, u32[]{:S(2)}) copy-start(f32[256]{0:T(256)} %copy-done.23) | copy-start | bytes 3076
  340.2 4.7 copy-start.10
  340.2 11.7 %slice-start = ((s8[8388608]{0:T(1024)(128)(4,1)}), s8[4194304]{0:T(1024)(128)(4,1)S(1)}, s32[]{:S(2)}) async-start(s8[8388608]{0:T(1024)(128)(4,1)} %bitcast.31), calls=%async_computation.1 | async-start | bytes 8388608
  344.9 1.8 copy-start.5
  344.9 7.0 %slice-start.1 = ((s8[8388608]{0:T(1024)(128)(4,1)}), s8[4194304]{0:T(1024)(128)(4,1)S(1)}, s32[]{:S(2)}) async-start(s8[8388608]{0:T(1024)(128)(4,1)} %bitcast.31), calls=%async_computation.2 | async-start | bytes 8388608
  344.9 7.8 %copy-start.7 = (bf16[2,2,2,2048,256]{4,3,2,1,0:T(8,128)(2,1)S(1)}, bf16[2,2,2,2048,256]{4,3,2,1,0:T(8,128)(2,1)}, u32[]{:S(2)}) copy-start(bf16[2,2,2,2048,256]{4,3,2,1,0:T(8,128)(2,1)} %get-tuple-element.50) | copy-start | bytes 25165828
  570.0 6.3 %copy-start.9 = (bf16[2,2,2048,256]{3,2,1,0:T(8,128)(2,1)S(1)}, bf16[2,2,2048,256]{3,2,1,0:T(8,128)(2,1)}, u32[]{:S(2)}) copy-start(bf16[2,2,2048,256]{3,2,1,0:T(8,128)(2,1)} %get-tuple-element.62) | copy-start | bytes 12582916
  576.2 6.7 %copy-start.4 = (bf16[256,2048]{1,0:T(8,128)(2,1)S(1)}, bf16[256,2048]{1,0:T(8,128)(2,1)}, u32[]{:S(2)}) copy-start(bf16[256,2048]{1,0:T(8,128)(2,1)} %param.15) | copy-start | bytes 3145732
  576.2 6.7 %copy-start.8 = (f32[256,2048]{1,0:T(8,128)S(1)}, f32[256,2048]{1,0:T(8,128)}, u32[]{:S(2)}) copy-start(f32[256,2048]{1,0:T(8,128)} %get-tuple-element.56) | copy-start | bytes 6291460
  576.2 6.7 %copy-start.22 = (f32[2048]{0:T(1024)S(1)}, f32[2048]{0:T(1024)}, u32[]{:S(2)}) copy-start(f32[2048]{0:T(1024)} %param.18) | copy-start | bytes 24580
  582.9 2.1 copy-start.6
  582.9 2.1 copy-start.11
  582.9 2.1 copy-start.30
  588.2 5.8 copy-start.13
  588.2 6.6 %copy-start.12 = (f32[256,512]{1,0:T(8,128)S(1)}, f32[256,512]{1,0:T(8,128)}, u32[]{:S(2)}) copy-start(f32[256,512]{1,0:T(8,128)} %get-tuple-element.143) | copy-start | bytes 1572868
  592.2 3.5 copy-start.18
Sparse Core Ops, SparseCore 0:
  340.3 134.2 all-reduce.1

commit v8 on v7

--- a/solution.py
+++ b/solution.py
@@ -1678,6 +1678,23 @@
         return carry
 
     lax.fori_loop(0, 4, rows_part, 0)
+    sums[0, 2:3, :128] = gain_sums[0:1]
+    sums[0, 2:3, 128:256] = gain_sums[1:2]
+
+    def sums_round(i, to):
+        copy = pltpu.make_async_remote_copy(
+            src_ref=sums.at[i],
+            dst_ref=sums_in.at[i],
+            send_sem=sums_send.at[i],
+            recv_sem=sums_recv.at[i],
+            device_id=to,
+            device_id_type=mesh_ids,
+        )
+        copy.start()
+        copy.wait()
+        sums[i + 1] = sums[i] + sums_in[i]
+
+    sums_round(0, (position, near))
     relays(0)
 
     @pl.when(middle)
@@ -1725,23 +1742,6 @@
             side_copy(k, c).wait_send()
         for k in range(1, 4):
             line_copy(k, c).wait_send()
-    sums[0, 2:3, :128] = gain_sums[0:1]
-    sums[0, 2:3, 128:256] = gain_sums[1:2]
-
-    def sums_round(i, to):
-        copy = pltpu.make_async_remote_copy(
-            src_ref=sums.at[i],
-            dst_ref=sums_in.at[i],
-            send_sem=sums_send.at[i],
-            recv_sem=sums_recv.at[i],
-            device_id=to,
-            device_id_type=mesh_ids,
-        )
-        copy.start()
-        copy.wait()
-        sums[i + 1] = sums[i] + sums_in[i]
-
-    sums_round(0, (position, near))
     sums_round(1, (z * 2 + 1 - x, t))
     sums_round(2, (pair * 2 + x, t))
     sums_round(3, (distant, t))

time: 612 us -> 614 us (level)
  no operation moved by 1% of the time
where the time goes in v8:
time: 614 us; the launch traced here: 605 us
  Pallas kernels  531 us (86%)
  other arithmetic  36.9 us (6%)
  between operations  14.7 us (2%)
  local copies, waits for them, and re-layouts  14.1 us (2%)
  matrix products  8.54 us (1%)
    pallas_call x1, Pallas kernels, expert_pass(): pl.pallas_call(functools.partial(expert_kernel, experts_all), name='exper...  237 us
    pallas_call x1, Pallas kernels, attention_backward(): pl.pallas_call(attention_back_kernel, name='attention_backward', out_shap...  217 us
    pallas_call x1, Pallas kernels, attention_forward(): pl.pallas_call(attention_kernel, name='attention_forward', out_shape=(jax...  77.2 us
    add x2, other arithmetic, add_three(): first.astype(jnp.float32) + second.astype(jnp.float32)  12.9 us
  transfers between devices with their start and end apart: 1, of which 0 were waited for; matrix products, arithmetic and copies ran while one was open for 6% of the time, Pallas kernels for 36%

profile of v8, /device:TPU:0, one launch (start us, length us, event | category | flops | bytes accessed | tf_op | source)
XLA Modules:
  0.0 605.3 jit_solution(11833976464409133401)
XLA Ops:
  7.2 0.0 copy-start
  7.2 0.0 copy-start.3
  7.2 0.0 copy-start.21
  7.2 0.0 all-reduce.2.cloned.1.call-start
  7.3 1.6 fusion.8
  8.9 0.0 copy-start.29
  8.9 2.0 fusion.20
  10.9 0.0 copy-done.3
  10.9 0.0 copy-done.21
  10.9 1.3 fusion.3.own
  12.2 1.3 pad_maximum_fusion
  13.5 0.0 copy-done.29
  13.5 77.2 %attention_forward.1 = (bf16[4,256,2048]{2,1,0:T(8,128)(2,1)}, bf16[1024,512]{1,0:T(8,128)(2,1)}, bf16[1024,512]{1,0:T(8,128)(2,1)}, bf16[1024,512]{1,0:T(8,128)...) custom-call(bf16[256,2048]{1,0:T(8,128)(2,1)} %fusion.3.own, ...), custom_call_target="tpu_custom_call" | custom-call | flops 8589934592 | bytes 67108864 | tf_op jit(solution)/shard_map/attention_forward/pallas_call | solution.py:1127
  90.6 0.0 copy-start.16
  90.7 2.0 multiply_reduce_fusion.2
  92.6 0.0 copy-start.19
  92.6 0.0 copy-start.23
  92.7 0.0 copy-done
  92.7 0.0 copy-done.16
  92.7 1.8 fusion.12
  94.5 0.0 copy-done.19
  94.6 0.0 copy-start.14
  94.6 0.0 copy-start.27
  94.7 0.1 copy.36
  94.8 0.4 copy-done.25
  95.1 0.0 copy-done.27
  95.2 0.7 copy.38
  95.9 0.1 copy.37
  96.0 0.2 fusion.13
  96.3 0.6 subtract_convert_fusion
  96.9 2.6 concatenate.11.own_rows
  99.6 0.0 copy-start.28
  99.6 0.0 copy-start.2
  99.6 0.0 copy-start.17
  99.6 0.0 copy-start.24
  99.6 237.1 %expert_pass.1 = (bf16[2048,2048]{1,0:T(8,128)(2,1)}, bf16[2,2048,2048]{2,1,0:T(8,128)(2,1)}, bf16[8,256,2048]{2,1,0:T(8,128)(2,1)}, f32[256,2176]{1,0:T(8,128)}...) custom-call(bf16[256,2176]{1,0:T(8,128)(2,1)} %concatenate.11.own_ro, ...), custom_call_target="tpu_custom_call" | custom-call | flops 154618822656 | bytes 67108864 | tf_op jit(solution)/shard_map/expert_pass/pallas_call | solution.py:737
  336.8 1.1 slice_add_fusion
  337.8 0.1 copy.39
  338.1 2.0 fusion.11
  340.1 0.0 all-reduce.2.cloned.1.call-update
  340.2 0.0 copy-start.10
  340.2 0.0 slice-start
  340.2 4.7 multiply_reduce_fusion
  344.9 0.0 copy-done.10
  344.9 0.0 copy-start.7
  344.9 1.7 fusion.23.branch
  346.6 5.2 fusion.10.sent_output
  351.9 0.0 slice-done.1
  351.9 0.8 copy-done.7
  352.7 2.5 fusion.sent_input
  355.2 216.7 %attention_backward.1 = (f32[256,2048]{1,0:T(8,128)}, bf16[2,2,2048,256]{3,2,1,0:T(8,128)(2,1)}, bf16[2,256,2048]{2,1,0:T(8,128)(2,1)}, bf16[256,2048]{1,0:T(8,1...) custom-call(bf16[256,2048]{1,0:T(8,128)(2,1)} %fusion.23.branch, ...), custom_call_target="tpu_custom_call" | custom-call | flops 17179869184 | bytes 67108864 | tf_op jit(solution)/shard_map/attention_backward/pallas_call | solution.py:1775
  571.9 6.2 %bitcast_add_fusion = f32[2,256,2048]{2,1,0:T(8,128)} fusion(bf16[2,256,2048]{2,1,0:T(8,128)(2,1)} %get-tuple-element.63, bf16[2,2,256,2048]{3,2,1,0:T(8,128)(2,1)} %get-tuple-element.53, bf16[2,2,256,2048]{3,2,1,0:T(8,128)(2,1)} %get-tuple-element.52), kind=kLoop, calls=%fused_computation.4 | loop fusion | flops 5242880 | bytes 10485760 | tf_op jit(solution)/shard_map/add | solution.py:1843
  578.2 6.7 %convert_add_fusion = (f32[2,2048,256]{2,1,0:T(8,128)}, f32[2,2048,256]{2,1,0:T(8,128)}) fusion(bf16[2,2,2048,256]{3,2,1,0:T(8,128)(2,1)S(1)} %copy-done.9, bf16[2,2,2,2048,256]{4,3,2,1,0:T(8,128)(2,1)} %get-tuple-element.51, bf16[2,2,2,2048,256]{4,3,2,1,0:T(8,128)(2,1)} %get-tuple-element.50), kind=kLoop, calls=%fused_computation.2 | loop fusion | flops 10485760 | bytes 20971520 | tf_op jit(solution)/shard_map/add | solution.py:1843
  584.9 0.4 fusion.9
  585.3 1.7 fusion.24
  587.0 0.0 copy-done.6
  587.0 3.2 fusion.7
  590.2 1.3 slice_bitcast_fusion
  591.4 0.6 div.50
  592.1 2.0 copy.40
  594.1 1.9 copy.45
  596.0 0.8 copy.46
  596.8 0.8 copy.47
  597.6 0.7 copy.48
  (56 shorter events, 0.3 us)
Async XLA Ops:
  7.2 85.5 %copy-start = (f32[2048,16]{0,1:T(8,128)S(1)}, f32[2048,16]{0,1:T(8,128)}, u32[]{:S(2)}) copy-start(f32[2048,16]{0,1:T(8,128)} %param.26) | copy-start | bytes 393220
  7.2 3.7 copy-start.3
  7.2 3.7 copy-start.21
  7.2 586.9 %all-reduce.2.cloned.1.call-start = ((), (), s32[]{:S(2)}) async-start(), calls=%async_computation | async-start | bytes 262144 | tf_op jit(solution)/shard_map/psum | solution.py:1946
  8.9 4.6 copy-start.29
  90.6 2.0 copy-start.16
  92.6 3.7 copy-start.1
  92.6 1.9 copy-start.19
  92.6 3.6 copy-start.23
  94.6 1.4 copy-start.14
  94.6 0.6 copy-start.25
  94.6 0.6 copy-start.27
  99.5 238.4 %copy-start.20 = (s32[256,8]{0,1:T(8,128)S(1)}, s32[256,8]{0,1:T(8,128)}, u32[]{:S(2)}) copy-start(s32[256,8]{0,1:T(8,128)} %param.17) | copy-start | bytes 24580
  99.5 238.4 %copy-start.15 = (f32[256,8]{0,1:T(8,128)S(1)}, f32[256,8]{0,1:T(8,128)}, u32[]{:S(2)}) copy-start(f32[256,8]{0,1:T(8,128)} %copy-done.14) | copy-start | bytes 24580
  99.6 238.4 %copy-start.26 = (f32[256]{0:T(256)S(1)}, f32[256]{0:T(256)}, u32[]{:S(2)}) copy-start(f32[256]{0:T(256)} %copy-done.25) | copy-start | bytes 3076
  99.6 238.4 %copy-start.28 = (f32[256]{0:T(256)S(1)}, f32[256]{0:T(256)}, u32[]{:S(2)}) copy-start(f32[256]{0:T(256)} %copy-done.27) | copy-start | bytes 3076
  99.6 238.5 %copy-start.2 = (f32[256,2048]{1,0:T(8,128)S(1)}, f32[256,2048]{1,0:T(8,128)}, u32[]{:S(2)}) copy-start(f32[256,2048]{1,0:T(8,128)} %copy-done.1) | copy-start | bytes 6291460
  99.6 238.5 %copy-start.17 = (f32[2048]{0:T(1024)S(1)}, f32[2048]{0:T(1024)}, u32[]{:S(2)}) copy-start(f32[2048]{0:T(1024)} %param.25) | copy-start | bytes 24580
  99.6 238.5 %copy-start.24 = (f32[256]{0:T(256)S(1)}, f32[256]{0:T(256)}, u32[]{:S(2)}) copy-start(f32[256]{0:T(256)} %copy-done.23) | copy-start | bytes 3076
  340.2 4.7 copy-start.10
  340.2 11.7 %slice-start = ((s8[8388608]{0:T(1024)(128)(4,1)}), s8[4194304]{0:T(1024)(128)(4,1)S(1)}, s32[]{:S(2)}) async-start(s8[8388608]{0:T(1024)(128)(4,1)} %bitcast.31), calls=%async_computation.1 | async-start | bytes 8388608
  344.9 1.8 copy-start.5
  344.9 7.0 %slice-start.1 = ((s8[8388608]{0:T(1024)(128)(4,1)}), s8[4194304]{0:T(1024)(128)(4,1)S(1)}, s32[]{:S(2)}) async-start(s8[8388608]{0:T(1024)(128)(4,1)} %bitcast.31), calls=%async_computation.2 | async-start | bytes 8388608
  344.9 7.8 %copy-start.7 = (bf16[2,2,2,2048,256]{4,3,2,1,0:T(8,128)(2,1)S(1)}, bf16[2,2,2,2048,256]{4,3,2,1,0:T(8,128)(2,1)}, u32[]{:S(2)}) copy-start(bf16[2,2,2,2048,256]{4,3,2,1,0:T(8,128)(2,1)} %get-tuple-element.50) | copy-start | bytes 25165828
  571.9 6.3 %copy-start.9 = (bf16[2,2,2048,256]{3,2,1,0:T(8,128)(2,1)S(1)}, bf16[2,2,2048,256]{3,2,1,0:T(8,128)(2,1)}, u32[]{:S(2)}) copy-start(bf16[2,2,2048,256]{3,2,1,0:T(8,128)(2,1)} %get-tuple-element.62) | copy-start | bytes 12582916
  578.2 6.7 %copy-start.4 = (bf16[256,2048]{1,0:T(8,128)(2,1)S(1)}, bf16[256,2048]{1,0:T(8,128)(2,1)}, u32[]{:S(2)}) copy-start(bf16[256,2048]{1,0:T(8,128)(2,1)} %param.15) | copy-start | bytes 3145732
  578.2 6.7 %copy-start.8 = (f32[256,2048]{1,0:T(8,128)S(1)}, f32[256,2048]{1,0:T(8,128)}, u32[]{:S(2)}) copy-start(f32[256,2048]{1,0:T(8,128)} %get-tuple-element.56) | copy-start | bytes 6291460
  578.2 6.7 %copy-start.22 = (f32[2048]{0:T(1024)S(1)}, f32[2048]{0:T(1024)}, u32[]{:S(2)}) copy-start(f32[2048]{0:T(1024)} %param.18) | copy-start | bytes 24580
  584.9 2.1 copy-start.6
  584.9 2.1 copy-start.11
  584.9 2.1 copy-start.30
  590.2 5.8 copy-start.13
  590.2 6.6 %copy-start.12 = (f32[256,512]{1,0:T(8,128)S(1)}, f32[256,512]{1,0:T(8,128)}, u32[]{:S(2)}) copy-start(f32[256,512]{1,0:T(8,128)} %get-tuple-element.143) | copy-start | bytes 1572868
  594.1 3.5 copy-start.18
Sparse Core Ops, SparseCore 0:
  340.3 134.2 all-reduce.1
